TPU v7x, 32 devices: a whole 2x2x4 slice. The times are simulated.
32 devices in a mesh: img: 2 (over core), pix: 16 (over z, y, x).
Axes of the slice: x: 2, y: 2, z: 4, core: 2. Of those that a mesh axis runs over, the one named last changes fastest.
Arguments:
- latents: bfloat16 [2, 256, 1024], P('img'), may hold values from -6 to 6
- pixels: float32 [2, 3, 6144], P('img', None, 'pix'), may hold values from -5 to 5
- coords: int32 [2, 2, 6144], P('img', None, 'pix'), may hold values from 0 to 223, as said below
- kept_mask: int32 [2, 6144], P('img', 'pix'), may hold values from 0 to 1, as said below
- lat_gain: float32 [1024], replicated, may hold values from 0.1 to 1.9
- lat_shift: float32 [1024], replicated, may hold values from -3 to 3
- query_weight: bfloat16 [1024, 1024], replicated, may hold values from -0.1875 to 0.1875
- query_bias: float32 [1024], replicated, may hold values from -3 to 3
- in_gain: float32 [261], replicated, may hold values from 0.1 to 1.9
- in_shift: float32 [261], replicated, may hold values from -3 to 3
- key_weight: bfloat16 [261, 1024], replicated, may hold values from -0.75 to 0.75
- value_weight: bfloat16 [261, 1024], replicated, may hold values from -2.023352 to 2.023352
- value_bias: float32 [1024], replicated, may hold values from -4 to 4
- mlp_gain: float32 [1024], replicated, may hold values from 0.1 to 1.9
- mlp_shift: float32 [1024], replicated, may hold values from -3 to 3
- up_weight: bfloat16 [1024, 1024], replicated, may hold values from -0.1875 to 0.1875
- up_bias: float32 [1024], replicated, may hold values from -3 to 3
- down_weight: bfloat16 [1024, 1024], replicated, may hold values from -0.1875 to 0.1875
- down_bias: float32 [1024], replicated, may hold values from -3 to 3
- cotangent: bfloat16 [2, 256, 1024], P('img'), may hold values from -6 to 6
Outputs:
- encoded: bfloat16 [2, 256, 1024], P('img')
- latent_grad: float32 [2, 256, 1024], P('img')
- pixel_grad: float32 [2, 3, 6144], P('img', None, 'pix')
- lat_gain_grad: float32 [1024], replicated
- lat_shift_grad: float32 [1024], replicated
- query_weight_grad: float32 [1024, 1024], replicated
- query_bias_grad: float32 [1024], replicated
- in_gain_grad: float32 [261], replicated
- in_shift_grad: float32 [261], replicated
- key_weight_grad: float32 [261, 1024], replicated
- value_weight_grad: float32 [261, 1024], replicated
- value_bias_grad: float32 [1024], replicated
- mlp_gain_grad: float32 [1024], replicated
- mlp_shift_grad: float32 [1024], replicated
- up_weight_grad: float32 [1024, 1024], replicated
- up_bias_grad: float32 [1024], replicated
- down_weight_grad: float32 [1024, 1024], replicated
- down_bias_grad: float32 [1024], replicated
Inputs may be any that keep to these rules, and one draw needn't show every extreme that they name: `coords`: for each image the pixels are distinct cells of a 224 x 224 grid in row-major order, given as (row, column); the first and the last cell of the grid are always among them. `kept_mask`: exactly half of each image's pixels are kept; dropped keys cluster in square patches of 16 x 16 grid cells, with a share that varies by patch row.
All inputs are finite; a program needn't handle non-finite values.
Results may differ from a plain program's by a relative error of at most 0.017.
The roundings to bfloat16 on the way count: a program that leaves them out, or rounds other values in their place, can miss the bound.
Values may be sent and summed in bfloat16 or wider, within the bound.
No kernel may reach another device: no remote copies, remote signals or barrier semaphores. Data moves between devices by JAX's collectives and lax.ppermute only.
A program may use at most 128 MiB of HBM per device.

v0:
```python
from functools import partial
import math

import jax
import jax.numpy as jnp
from jax import lax
from jax.sharding import PartitionSpec as P

BANDS = 64
GRID = 224


EPSILON = 1e-05
HIGHEST = lax.Precision.HIGHEST
FLOOR = -1e30


def norm_axis(values, gain_vec, shift_vec, axis_pos):
    centre = values - jnp.mean(values, axis=axis_pos, keepdims=True)
    spread_sq = jnp.mean(centre * centre, axis=axis_pos, keepdims=True)
    return centre * lax.rsqrt(spread_sq + EPSILON) * gain_vec + shift_vec


def fourier_table(colors, grid_pos):
    position = grid_pos.astype(jnp.float32) * (2.0 / (GRID - 1)) - 1.0
    frequency = 1.0 + jnp.arange(BANDS, dtype=jnp.float32) * ((GRID / 2.0 - 1.0) / (BANDS - 1))
    phases = (position[:, None, :] * (math.pi * frequency)[None, :, None]).reshape(
        2 * BANDS, position.shape[1]
    )
    return jnp.concatenate([colors, position, jnp.sin(phases), jnp.cos(phases)], axis=0)


def contract(left, right, left_dim, right_dim, exact=None):
    return lax.dot_general(
        left,
        right,
        (((left_dim,), (right_dim,)), ((), ())),
        precision=exact,
        preferred_element_type=jnp.float32,
    )


def forward_pass(latents, pixels, coords, kept_mask, weights):
    (
        lat_gain,
        lat_shift,
        query_weight,
        query_bias,
        in_gain,
        in_shift,
        key_weight,
        value_weight,
        value_bias,
        mlp_gain,
        mlp_shift,
        up_weight,
        up_bias,
        down_weight,
        down_bias,
    ) = weights
    latent = latents[0].astype(jnp.float32)
    norm_one = norm_axis(latent, lat_gain, lat_shift, 1).astype(jnp.bfloat16)
    query = (
        jnp.dot(norm_one, query_weight, preferred_element_type=jnp.float32) + query_bias
    ).astype(jnp.bfloat16)
    table = fourier_table(pixels[0], coords[0]).astype(jnp.bfloat16)
    live_row = kept_mask[0].astype(jnp.bfloat16)
    slot_order = jnp.arange(live_row.shape[0], dtype=jnp.int32)
    table_full = table.astype(jnp.float32)
    x_in = norm_axis(table_full, in_gain[:, None], in_shift[:, None], 0).astype(jnp.bfloat16)
    keys = contract(x_in, key_weight, 0, 0).astype(jnp.bfloat16)
    values = (contract(x_in, value_weight, 0, 0) + value_bias).astype(jnp.bfloat16)
    inv_root = 1.0 / math.sqrt(query.shape[1])
    score = contract(query, keys, 1, 1) * inv_root
    live_mask = live_row > 0
    local_top = jnp.max(jnp.where(live_mask, score, FLOOR), axis=1)
    values_full = values.astype(jnp.float32)
    row_top = lax.pmax(local_top, "pix")
    weight = jnp.where(live_mask, jnp.exp(score - row_top[:, None]), 0.0)
    row_total, weighted = lax.psum(
        (jnp.sum(weight, axis=1), jnp.dot(weight, values_full, precision=HIGHEST)), "pix"
    )
    attn = weighted / row_total[:, None]
    mixed = latent + attn
    norm_two = norm_axis(mixed, mlp_gain, mlp_shift, 1).astype(jnp.bfloat16)
    pre_act = jnp.dot(norm_two, up_weight, preferred_element_type=jnp.float32) + up_bias
    hidden = jax.nn.gelu(pre_act, approximate=False).astype(jnp.bfloat16)
    encoded = mixed + jnp.dot(hidden, down_weight, preferred_element_type=jnp.float32) + down_bias
    saved = (
        latent,
        norm_one,
        query,
        table_full,
        x_in,
        keys,
        values,
        score,
        live_mask,
        row_top,
        row_total,
        attn,
        mixed,
        norm_two,
        pre_act,
        hidden,
        slot_order,
        slot_order,
    )
    return (encoded.astype(jnp.bfloat16)[None], saved)


def shards(
    latents,
    pixels,
    coords,
    kept_mask,
    lat_gain,
    lat_shift,
    query_weight,
    query_bias,
    in_gain,
    in_shift,
    key_weight,
    value_weight,
    value_bias,
    mlp_gain,
    mlp_shift,
    up_weight,
    up_bias,
    down_weight,
    down_bias,
    cotangent,
):
    weights = (
        lat_gain,
        lat_shift,
        query_weight,
        query_bias,
        in_gain,
        in_shift,
        key_weight,
        value_weight,
        value_bias,
        mlp_gain,
        mlp_shift,
        up_weight,
        up_bias,
        down_weight,
        down_bias,
    )
    encoded, saved = forward_pass(latents, pixels, coords, kept_mask, weights)
    fresh = lax.optimization_barrier((latents, pixels, coords, kept_mask, weights))
    discarded, saved = forward_pass(fresh[0], fresh[1], fresh[2], fresh[3], fresh[4])
    (
        latent,
        norm_one,
        query,
        table_full,
        x_in,
        keys,
        values,
        score,
        live_mask,
        row_top,
        row_total,
        attn,
        mixed,
        norm_two,
        pre_act,
        hidden,
        slot_order,
        kept_index,
    ) = saved
    inv_root = 1.0 / math.sqrt(query.shape[1])
    out_grad = cotangent[0]
    out_grad_full = out_grad.astype(jnp.float32)
    down_weight_grad = contract(hidden, out_grad, 0, 0)
    down_bias_grad = jnp.sum(out_grad_full, axis=0)
    hidden_grad = contract(out_grad, down_weight, 1, 1)
    ignored, gelu_pull = jax.vjp(partial(jax.nn.gelu, approximate=False), pre_act)
    pre_grad = gelu_pull(hidden_grad)[0].astype(jnp.bfloat16)
    up_weight_grad = contract(norm_two, pre_grad, 0, 0)
    up_bias_grad = jnp.sum(pre_grad.astype(jnp.float32), axis=0)
    norm_two_grad = contract(pre_grad, up_weight, 1, 1)
    ignored, mlp_pull = jax.vjp(partial(norm_axis, axis_pos=1), mixed, mlp_gain, mlp_shift)
    mixed_part, mlp_gain_grad, mlp_shift_grad = mlp_pull(norm_two_grad)
    mixed_grad = out_grad_full + mixed_part
    attn_grad = mixed_grad.astype(jnp.bfloat16)
    attn_grad_full = attn_grad.astype(jnp.float32)
    row_delta = jnp.sum(attn_grad_full * attn, axis=1)
    prob = jnp.where(live_mask, jnp.exp(score - row_top[:, None]), 0.0) / row_total[:, None]
    prob_grad = contract(attn_grad, values, 1, 1)
    score_grad = (prob * (prob_grad - row_delta[:, None])).astype(jnp.bfloat16)
    query_part = jnp.dot(score_grad, keys, preferred_element_type=jnp.float32) * inv_root
    key_grad = (contract(score_grad, query, 0, 0) * inv_root).astype(jnp.bfloat16)
    value_grad = contract(prob, attn_grad_full, 0, 0, HIGHEST).astype(jnp.bfloat16)
    key_weight_grad = contract(x_in, key_grad, 1, 0)
    value_weight_grad = contract(x_in, value_grad, 1, 0)
    value_bias_grad = jnp.sum(value_grad.astype(jnp.float32), axis=0)
    x_in_grad = contract(key_weight, key_grad, 1, 1) + contract(value_weight, value_grad, 1, 1)
    ignored, input_pull = jax.vjp(
        partial(norm_axis, axis_pos=0), table_full, in_gain[:, None], in_shift[:, None]
    )
    table_grad, in_gain_col, in_shift_col = input_pull(x_in_grad)
    color_grad = table_grad[:3]
    query_grad = lax.psum(query_part, "pix").astype(jnp.bfloat16)
    query_weight_grad = contract(norm_one, query_grad, 0, 0)
    query_bias_grad = jnp.sum(query_grad.astype(jnp.float32), axis=0)
    norm_one_grad = contract(query_grad, query_weight, 1, 1)
    ignored, latent_pull = jax.vjp(partial(norm_axis, axis_pos=1), latent, lat_gain, lat_shift)
    latent_part, lat_gain_grad, lat_shift_grad = latent_pull(norm_one_grad)
    latent_grad = mixed_grad + latent_part
    pixel_sums = lax.psum(
        (
            key_weight_grad,
            value_weight_grad,
            value_bias_grad,
            in_gain_col[:, 0],
            in_shift_col[:, 0],
        ),
        ("img", "pix"),
    )
    replica_sums = (
        lax.psum(lat_gain_grad.astype(jnp.bfloat16), "img").astype(jnp.float32),
        lax.psum(lat_shift_grad.astype(jnp.bfloat16), "img").astype(jnp.float32),
        lax.psum(query_weight_grad.astype(jnp.bfloat16), "img").astype(jnp.float32),
        lax.psum(query_bias_grad.astype(jnp.bfloat16), "img").astype(jnp.float32),
        lax.psum(mlp_gain_grad.astype(jnp.bfloat16), "img").astype(jnp.float32),
        lax.psum(mlp_shift_grad.astype(jnp.bfloat16), "img").astype(jnp.float32),
        lax.psum(up_weight_grad.astype(jnp.bfloat16), "img").astype(jnp.float32),
        lax.psum(up_bias_grad.astype(jnp.bfloat16), "img").astype(jnp.float32),
        lax.psum(down_weight_grad.astype(jnp.bfloat16), "img").astype(jnp.float32),
        lax.psum(down_bias_grad.astype(jnp.bfloat16), "img").astype(jnp.float32),
    )
    return (
        encoded,
        latent_grad[None],
        color_grad[None],
        replica_sums[0],
        replica_sums[1],
        replica_sums[2],
        replica_sums[3],
        pixel_sums[3],
        pixel_sums[4],
        pixel_sums[0],
        pixel_sums[1],
        pixel_sums[2],
        replica_sums[4],
        replica_sums[5],
        replica_sums[6],
        replica_sums[7],
        replica_sums[8],
        replica_sums[9],
    )


def solution(mesh):
    return jax.shard_map(
        shards,
        mesh=mesh,
        in_specs=(
            P("img", None, None),
            P("img", None, "pix"),
            P("img", None, "pix"),
            P("img", "pix"),
            P(),
            P(),
            P(),
            P(),
            P(),
            P(),
            P(),
            P(),
            P(),
            P(),
            P(),
            P(),
            P(),
            P(),
            P(),
            P("img", None, None),
        ),
        out_specs=(
            P("img", None, None),
            P("img", None, None),
            P("img", None, "pix"),
            P(),
            P(),
            P(),
            P(),
            P(),
            P(),
            P(),
            P(),
            P(),
            P(),
            P(),
            P(),
            P(),
            P(),
            P(),
        ),
        check_vma=False,
    )
```

profile of v0, /device:TPU:0, one launch (start us, length us, event | category | flops | bytes accessed | tf_op | source)
XLA Modules:
  0.0 493.2 jit_solution(3824822552677520739)
XLA Ops:
  7.3 0.8 fusion.175
  8.1 0.7 copy.47
  8.8 0.7 compare_reduce_fusion.1
  9.5 1.3 convert_reduce_fusion.2
  10.7 0.7 fusion.176
  11.5 0.7 copy.48
  12.2 1.6 fusion.121
  14.1 2.8 add_convert_fusion.1
  17.3 1.6 fusion.10
  19.4 0.5 copy-done.49
  20.1 3.0 select_reduce_fusion.1
  23.1 1.9 convolution_convert_fusion.3
  25.1 0.8 fusion.11
  25.9 0.5 select_reduce_fusion
  26.7 43.5 %all-reduce.4 = (f32[256]{0:T(256)S(1)}, f32[256]{0:T(256)S(1)}) all-reduce(f32[256]{0:T(256)S(1)} %get-tuple-element.120, f32[256]{0:T(256)S(1)} %get-tuple-element.122), channel_id=1, replica_groups=mesh['img'=2,'pix'=16] {'pix'}, use_global_device_ids=true, to_apply=%region_5.6 | all-reduce | flops 512 | bytes 4096 | tf_op jit(solution)/shard_map/pmax | solution.py:78
  70.2 1.9 add_convert_fusion
  72.1 2.0 fusion.115
  74.1 2.0 fusion.118
  76.5 37.6 %psum.143 = f32[256]{0:T(256)S(1)} all-reduce(f32[256]{0:T(256)S(1)} %fusion.117), channel_id=1, replica_groups=mesh['img'=2,'pix'=16] {'pix'}, use_global_device_ids=true, to_apply=%region_19.20 | all-reduce | flops 256 | bytes 2048 | tf_op jit(solution)/shard_map/psum | solution.py:80
  114.0 1.8 fusion.114
  115.8 83.1 %all-reduce.14.cloned.1.call-done = (f32[256,1024]{1,0:T(8,128)}, f32[256,1024]{1,0:T(8,128)}) async-done(((f32[256,1024]{1,0:T(8,128)}, f32[256,1024]{1,0:T(8,128)}), (f32[256,1024]{1,0:T(8,128)}, f32[256,1024]{1,0:T(8,128)})) %all-reduce.14.cloned.1.call-update) | async-done | bytes 2097168 | tf_op jit(solution)/shard_map/psum | solution.py:80
  198.9 1.5 fusion.197
  200.8 0.8 convolution_add_fusion
  201.8 0.7 copy-done.75
  202.5 3.7 fusion.201
  206.3 1.6 multiply_reduce_fusion
  207.9 2.2 convolution_convert_fusion.1
  210.1 4.0 convolution_convert_fusion
  214.6 0.7 copy-done.4
  216.2 1.1 fusion.20
  217.4 1.4 convolution_multiply_fusion
  218.8 89.6 %all-reduce.17 = (f32[256]{0:T(256)}, bf16[256,1024]{1,0:T(8,128)(2,1)}) all-reduce(f32[256]{0:T(256)} %fusion.114, f32[256,1024]{1,0:T(8,128)} %convolution_multiply_fusion), channel_id=1, replica_groups=mesh['img'=2,'pix'=16] {'pix'}, use_global_device_ids=true, to_apply=%region_8.9 | all-reduce | flops 262400 | bytes 1574912 | tf_op jit(solution)/shard_map/psum | solution.py:80
  308.4 3.3 convolution_convert_fusion.2
  312.0 0.7 reduce_sum.382
  312.7 1.7 fusion.193
  314.4 1.0 copy-done.6
  315.8 2.2 fusion.191
  318.1 1.1 fusion.23
  319.2 0.5 add_rsqrt_fusion.1
  319.7 0.5 negate_multiply_fusion.3
  320.7 1.0 convert_reduce_fusion
  321.7 0.5 fusion.202
  322.2 0.6 fusion.107
  323.2 1.5 fusion.186
  324.6 1.5 fusion.184
  326.2 3.0 add_bitcast_fusion
  329.3 0.9 copy-done.27
  330.3 0.6 copy.40
  330.9 3.3 all-reduce.5
  334.3 0.6 convert_element_type.207
  334.8 0.6 convert_element_type.209
  335.4 0.6 convert_element_type.212
  336.2 0.6 convert_element_type.215
  336.8 0.6 convert_element_type.217
  337.4 0.6 convert_element_type.220
  338.0 0.6 convert_element_type.224
  338.6 37.2 %all-reduce = (f32[261]{0:T(512)}, f32[261]{0:T(512)}, f32[1024]{0:T(1024)}) all-reduce(f32[261]{0:T(512)S(1)} %get-tuple-element.77, f32[261]{0:T(512)S(1)} %reduce_sum.377, f32[1024]{0:T(1024)S(1)} %get-tuple-element.129), channel_id=1, replica_groups=mesh['img'=2,'pix'=16] {'img','pix'}, use_global_device_ids=true, to_apply=%region_38.39 | all-reduce | flops 1546 | bytes 12368 | tf_op jit(solution)/shard_map/psum | solution.py:213
  375.8 6.7 %fusion.15 = bf16[1,256,1024]{2,1,0:T(8,128)(2,1)} fusion(f32[256,1024]{1,0:T(8,128)} %copy-done.6, bf16[1024,1024]{1,0:T(8,128)(2,1)} %param.37, bf16[1024,1024]{1,0:T(8,128)(2,1)S(1)} %copy-done, f32[1024]{0:T(1024)S(1)} %copy-done.82, f32[1024]{0:T(1024)S(1)} %copy-done.81, f32[1024]{0:T(1024)S(1)} %copy-done.60, f32[1024]{0:T(1024)S(1)} %copy-done.36, ...), kind=kOutput, calls=%fused_computation.39 | convolution fusion | flops 1093140480 | bytes 5785600 | tf_op jit(solution)/shard_map/dot_general | solution.py:88
  382.5 4.2 convert_element_type.211
  386.7 2.5 convert_element_type.219
  389.2 2.5 convert_element_type.223
  391.7 91.6 %all-reduce.12.cloned.1.call-done = (f32[261,1024]{1,0:T(8,128)}, f32[261,1024]{1,0:T(8,128)}) async-done(((f32[261,1024]{1,0:T(8,128)}, f32[261,1024]{1,0:T(8,128)}), (f32[261,1024]{1,0:T(8,128)}, f32[261,1024]{1,0:T(8,128)})) %all-reduce.12.cloned.1.call-update) | async-done | bytes 2138128 | tf_op jit(solution)/shard_map/psum | solution.py:213
  483.3 2.4 copy.59
  485.7 1.0 copy.60
  (204 shorter events, 5.4 us)
Async XLA Ops:
  7.2 193.5 %copy-start = (bf16[1024,1024]{1,0:T(8,128)(2,1)S(1)}, bf16[1024,1024]{1,0:T(8,128)(2,1)}, u32[]{:S(2)}) copy-start(bf16[1024,1024]{1,0:T(8,128)(2,1)} %param.35) | copy-start | bytes 6291460
  7.2 191.7 %all-reduce.14.cloned.1.call-start = ((), (), s32[]{:S(2)}) async-start(), calls=%async_computation.1 | async-start | bytes 4194304 | tf_op jit(solution)/shard_map/psum | solution.py:80
  9.5 7.5 %copy-start.1 = (bf16[1,256,1024]{2,1,0:T(8,128)(2,1)S(1)}, bf16[1,256,1024]{2,1,0:T(8,128)(2,1)}, u32[]{:S(2)}) copy-start(bf16[1,256,1024]{2,1,0:T(8,128)(2,1)} %param.20) | copy-start | bytes 1572868
  13.8 3.5 copy-start.32
  13.8 3.5 copy-start.72
  13.8 3.5 copy-start.77
  13.8 3.5 copy-start.79
  17.3 2.8 copy-start.28
  17.3 2.8 copy-start.51
  18.9 57.3 %copy-start.56 = (pred[384]{0:T(512)(128)(4,1)}, pred[384]{0:T(512)(128)(4,1)S(1)}, u32[]{:S(2)}) copy-start(pred[384]{0:T(512)(128)(4,1)S(1)} %compare_reduce_fusion) | copy-start | bytes 1156
  19.1 5.9 %copy-start.37 = (f32[256]{0:T(256)}, f32[256]{0:T(256)S(1)}, u32[]{:S(2)}) copy-start(f32[256]{0:T(256)S(1)} %broadcast_multiply_fusion.3) | copy-start | bytes 3076
  19.4 5.6 %copy-start.46 = (f32[256]{0:T(256)}, f32[256]{0:T(256)S(1)}, u32[]{:S(2)}) copy-start(f32[256]{0:T(256)S(1)} %fusion.137) | copy-start | bytes 3076
  20.1 4.9 %copy-start.30 = (f32[384]{0:T(512)}, f32[384]{0:T(512)S(1)}, u32[]{:S(2)}) copy-start(f32[384]{0:T(512)S(1)} %fusion.112) | copy-start | bytes 4612
  23.1 2.0 copy-start.73
  25.0 45.1 %copy-start.78 = (f32[1024]{0:T(1024)S(1)}, f32[1024]{0:T(1024)}, u32[]{:S(2)}) copy-start(f32[1024]{0:T(1024)} %param.32) | copy-start | bytes 12292
  26.7 49.5 %copy-start.11 = (f32[256,384]{1,0:T(8,128)}, f32[256,384]{1,0:T(8,128)S(1)}, u32[]{:S(2)}) copy-start(f32[256,384]{1,0:T(8,128)S(1)} %get-tuple-element.123) | copy-start | bytes 1179652
  70.2 6.0 %copy-start.61 = (f32[256]{0:T(256)}, f32[256]{0:T(256)S(1)}, u32[]{:S(2)}) copy-start(f32[256]{0:T(256)S(1)} %get-tuple-element.89) | copy-start | bytes 3076
  70.2 1.9 copy-start.14
  70.2 1.9 copy-start.18
  72.1 2.0 copy-start.16
  76.1 306.4 %all-reduce.16.cloned.1.call-start = ((), (), s32[]{:S(2)}) async-start(), calls=%async_computation.2 | async-start | bytes 12582912 | tf_op jit(solution)/shard_map/psum | solution.py:226
  76.4 124.3 %copy-start.35 = (f32[1024]{0:T(1024)S(1)}, f32[1024]{0:T(1024)}, u32[]{:S(2)}) copy-start(f32[1024]{0:T(1024)} %param.33) | copy-start | bytes 12292
  76.4 124.3 %copy-start.59 = (f32[1024]{0:T(1024)S(1)}, f32[1024]{0:T(1024)}, u32[]{:S(2)}) copy-start(f32[1024]{0:T(1024)} %param.34) | copy-start | bytes 12292
  76.5 124.3 %copy-start.80 = (f32[1024]{0:T(1024)S(1)}, f32[1024]{0:T(1024)}, u32[]{:S(2)}) copy-start(f32[1024]{0:T(1024)} %param.36) | copy-start | bytes 12292
  114.0 100.6 %copy-start.40 = (f32[256]{0:T(256)}, f32[256]{0:T(256)S(1)}, u32[]{:S(2)}) copy-start(f32[256]{0:T(256)S(1)} %psum.143) | copy-start | bytes 3076
  200.8 1.8 copy-start.75
  214.5 2.9 copy-start.2
  311.8 171.5 %all-reduce.12.cloned.1.call-start = ((), (), s32[]{:S(2)}) async-start(), calls=%async_computation | async-start | bytes 4325376 | tf_op jit(solution)/shard_map/psum | solution.py:213
  312.7 3.0 copy-start.26
  312.7 3.0 copy-start.74
  315.7 2.3 copy-start.50
  315.7 2.3 copy-start.33
  315.8 2.3 copy-start.38
  315.8 2.3 copy-start.47
  315.8 4.5 copy-start.23
  318.0 3.7 copy-start.5
  318.0 2.6 copy-start.13
  318.0 2.7 copy-start.25
  318.0 2.7 copy-start.41
  318.0 2.7 copy-start.58
  318.0 2.7 copy-start.63
  318.1 3.6 copy-start.44
  322.9 1.8 copy-start.9
  323.1 3.1 copy-start.34
  323.1 3.1 copy-start.39
  323.1 3.0 copy-start.43
  323.1 3.0 copy-start.45
  323.1 3.0 copy-start.48
  323.1 3.0 copy-start.64
  329.2 1.8 copy-start.53
  329.2 1.8 copy-start.54
  329.2 1.8 copy-start.67
  329.2 1.8 copy-start.68
  329.2 1.8 copy-start.69
  329.2 6.8 %copy-start.10 = (f32[384,261]{0,1:T(8,128)S(1)}, f32[384,261]{0,1:T(8,128)}, u32[]{:S(2)}) copy-start(f32[384,261]{0,1:T(8,128)} %copy-done.9) | copy-start | bytes 1202692
  329.2 46.6 %copy-start.36 = (f32[1024]{0:T(1024)S(1)}, f32[1024]{0:T(1024)}, u32[]{:S(2)}) copy-start(f32[1024]{0:T(1024)} %param.33) | copy-start | bytes 12292
  329.2 46.6 %copy-start.60 = (f32[1024]{0:T(1024)S(1)}, f32[1024]{0:T(1024)}, u32[]{:S(2)}) copy-start(f32[1024]{0:T(1024)} %param.34) | copy-start | bytes 12292
  329.2 46.5 %copy-start.66 = (f32[256]{0:T(256)S(1)}, f32[256]{0:T(256)}, u32[]{:S(2)}) copy-start(f32[256]{0:T(256)} %copy-done.65) | copy-start | bytes 3076
  329.2 46.5 %copy-start.71 = (f32[256]{0:T(256)S(1)}, f32[256]{0:T(256)}, u32[]{:S(2)}) copy-start(f32[256]{0:T(256)} %add_rsqrt_fusion.1) | copy-start | bytes 3076
  329.3 46.5 %copy-start.81 = (f32[1024]{0:T(1024)S(1)}, f32[1024]{0:T(1024)}, u32[]{:S(2)}) copy-start(f32[1024]{0:T(1024)} %param.36) | copy-start | bytes 12292
  329.3 46.5 %copy-start.82 = (f32[1024]{0:T(1024)S(1)}, f32[1024]{0:T(1024)}, u32[]{:S(2)}) copy-start(f32[1024]{0:T(1024)} %param.38) | copy-start | bytes 12292
  382.5 4.2 copy-start.8
  386.7 2.5 copy-start.7
  483.3 2.4 copy-start.15
  (22 other events, 28.5 us)
Sparse Core Ops, SparseCore 0:
  76.3 122.6 all-reduce.13
  311.9 28.9 all-reduce.15
  347.3 135.9 all-reduce.11
where the time goes:
time: 494 us; the launch traced here: 493 us
  blocking collectives  211 us (43%)
  waiting for transfers between devices  175 us (35%)
  matrix products  49 us (10%)
  other arithmetic  32.3 us (7%)
  between operations  14.9 us (3%)
  local copies, waits for them, and re-layouts  10.8 us (2%)
    psum x2, blocking collectives, forward_pass(): lax.psum((jnp.sum(weight, axis=1), jnp.dot(weight, values_full, precision...  127 us
    psum x1, waiting for transfers between devices, shards(): lax.psum((key_weight_grad, value_weight_grad, value_bias_grad, in_gain_co...  91.6 us
    psum x1, waiting for transfers between devices, forward_pass(): lax.psum((jnp.sum(weight, axis=1), jnp.dot(weight, values_full, precision...  83.1 us
    pmax x1, blocking collectives, forward_pass(): row_top = lax.pmax(local_top, 'pix')  43.5 us
    psum x1, blocking collectives, shards(): lax.psum((key_weight_grad, value_weight_grad, value_bias_grad, in_gain_co...  37.2 us
    dot_general x18, matrix products, contract(): lax.dot_general(left, right, (((left_dim,), (right_dim,)), ((), ())), pre...  33.8 us
    unnamed x170, local copies, waits for them, and re-layouts  10.1 us
  transfers between devices with their start and end apart: 3, of which 2 were waited for; matrix products, arithmetic and copies ran while one was open for 8% of the time, Pallas kernels for 0%

commit v1 on v0

v1 whole, which is shorter than its diff:
```python
import math

import jax
import jax.numpy as jnp
import numpy as np
from jax import lax
from jax.sharding import PartitionSpec as P

BANDS = 64
GRID = 224
EPSILON = 1e-05
FLOOR = -1e30
BLOCK = 16
BF = jnp.bfloat16
F32 = jnp.float32


def fourier_lookup():
    position = np.arange(GRID, dtype=np.float32) * np.float32(2.0 / (GRID - 1)) - np.float32(1.0)
    frequency = np.float32(1.0) + np.arange(BANDS, dtype=np.float32) * np.float32(
        (GRID / 2.0 - 1.0) / (BANDS - 1)
    )
    phases = position[None, :] * (np.float32(math.pi) * frequency)[:, None]
    waves = np.concatenate([np.sin(phases.astype(np.float64)), np.cos(phases.astype(np.float64))])
    return waves.astype(np.float32)


def contract(left, right, left_dim, right_dim):
    return lax.dot_general(
        left, right, (((left_dim,), (right_dim,)), ((), ())), preferred_element_type=F32
    )


def norm_stats(values, axis):
    centre = values - jnp.mean(values, axis=axis, keepdims=True)
    spread = lax.rsqrt(jnp.mean(centre * centre, axis=axis, keepdims=True) + EPSILON)
    return centre * spread, spread


def norm_back(upstream, gain, unit, spread, axis):
    inner = upstream * gain
    return spread * (
        inner
        - jnp.mean(inner, axis=axis, keepdims=True)
        - unit * jnp.mean(inner * unit, axis=axis, keepdims=True)
    )


def shards(
    latents,
    pixels,
    coords,
    kept_mask,
    lat_gain,
    lat_shift,
    query_weight,
    query_bias,
    in_gain,
    in_shift,
    key_weight,
    value_weight,
    value_bias,
    mlp_gain,
    mlp_shift,
    up_weight,
    up_bias,
    down_weight,
    down_bias,
    cotangent,
):
    pix = lax.axis_size("pix")
    mine = lax.axis_index("pix")
    own = pixels.shape[2]
    packed = jnp.concatenate(
        [
            pixels[0].astype(BF),
            coords[0].astype(BF),
            kept_mask.astype(BF),
            jnp.zeros((2, own), BF),
        ],
        axis=0,
    )
    gathered = lax.all_to_all(jnp.broadcast_to(packed[None], (pix,) + packed.shape), "pix", 0, 0)
    every = gathered.transpose(1, 0, 2).reshape(packed.shape[0], pix * own)
    swap = [(0, 1), (1, 0)]

    def other(value):
        return lax.ppermute(value, "img", swap)

    root = math.sqrt(latents.shape[2])
    latent = latents[0].astype(F32)
    lat_unit, lat_spread = norm_stats(latent, 1)
    norm_one = (lat_unit * lat_gain + lat_shift).astype(BF)
    query = (jnp.dot(norm_one, query_weight, preferred_element_type=F32) + query_bias).astype(BF)
    absorbed = (contract(query, key_weight, 1, 1) * (1.0 / root)).astype(BF)

    waves = jnp.asarray(fourier_lookup(), BF)
    places = jnp.arange(GRID, dtype=F32)[:, None]

    def features(part):
        cells = part[3:5].astype(F32)
        position = (cells * (2.0 / (GRID - 1)) - 1.0).astype(BF)
        row_waves = jnp.dot(waves, (cells[0:1] == places).astype(BF), preferred_element_type=F32).astype(BF)
        col_waves = jnp.dot(waves, (cells[1:2] == places).astype(BF), preferred_element_type=F32).astype(BF)
        table = jnp.concatenate(
            [part[0:3], position, row_waves[:BANDS], col_waves[:BANDS], row_waves[BANDS:], col_waves[BANDS:]],
            axis=0,
        ).astype(F32)
        unit, spread = norm_stats(table, 0)
        x_in = (unit * in_gain[:, None] + in_shift[:, None]).astype(BF)
        score = jnp.dot(absorbed, x_in, preferred_element_type=F32)
        return unit, spread, x_in, jnp.where(part[5:6] > 0, score, FLOOR), part[5:6] > 0

    def pool(part, feats):
        unit, spread, x_in, score, live = feats
        top = jnp.max(score, axis=1, keepdims=True)
        weight = jnp.where(live, jnp.exp(score - top), 0.0)
        return top, jnp.sum(weight, axis=1, keepdims=True), contract(weight.astype(BF), x_in, 1, 1)

    blocks = max(1, pix // BLOCK)
    parts = every.reshape(packed.shape[0], blocks, -1).transpose(1, 0, 2)
    if blocks == 1:
        feats = features(parts[0])
        row_top, row_total, pooled = pool(parts[0], feats)
    else:

        def merge(carry, part):
            top, total, sums = pool(part, features(part))
            new_top = jnp.maximum(carry[0], top)
            old_scale, new_scale = jnp.exp(carry[0] - new_top), jnp.exp(top - new_top)
            return (
                new_top,
                carry[1] * old_scale + total * new_scale,
                carry[2] * old_scale + sums * new_scale,
            ), None

        start = (
            jnp.full((latent.shape[0], 1), FLOOR, F32),
            jnp.zeros((latent.shape[0], 1), F32),
            jnp.zeros((latent.shape[0], in_gain.shape[0]), F32),
        )
        row_top, row_total, pooled = lax.scan(merge, start, parts)[0]
    pooled = pooled / row_total
    pooled_low = pooled.astype(BF)
    attn = jnp.dot(pooled_low, value_weight, preferred_element_type=F32) + value_bias
    mixed = latent + attn
    mix_unit, mix_spread = norm_stats(mixed, 1)
    norm_two = (mix_unit * mlp_gain + mlp_shift).astype(BF)
    pre_act = jnp.dot(norm_two, up_weight, preferred_element_type=F32) + up_bias
    half_erf = 0.5 * (1.0 + lax.erf(pre_act * (1.0 / math.sqrt(2.0))))
    hidden = (pre_act * half_erf).astype(BF)
    encoded = (
        mixed + jnp.dot(hidden, down_weight, preferred_element_type=F32) + down_bias
    ).astype(BF)

    out_grad = cotangent[0]
    out_grad_full = out_grad.astype(F32)
    hidden_grad = contract(out_grad, down_weight, 1, 1)
    slope = half_erf + pre_act * jnp.exp(-0.5 * pre_act * pre_act) * (1.0 / math.sqrt(2.0 * math.pi))
    pre_grad = (hidden_grad * slope).astype(BF)
    norm_two_grad = contract(pre_grad, up_weight, 1, 1)
    mixed_grad = out_grad_full + norm_back(norm_two_grad, mlp_gain, mix_unit, mix_spread, 1)
    attn_grad = mixed_grad.astype(BF)

    lifted = contract(attn_grad, value_weight, 1, 1).astype(BF)
    row_delta = jnp.sum(lifted.astype(F32) * pooled, axis=1, keepdims=True)

    def pull(part, feats):
        unit, spread, x_in, score, live = feats
        prob = jnp.where(live, jnp.exp(score - row_top), 0.0) / row_total
        score_grad = (prob * (jnp.dot(lifted, x_in, preferred_element_type=F32) - row_delta)).astype(BF)
        score_pool = contract(score_grad, x_in, 1, 1)
        x_in_grad = contract(absorbed, score_grad, 0, 0) + contract(lifted, prob.astype(BF), 0, 0)
        gain_part = jnp.sum(x_in_grad * unit, axis=1)
        shift_part = jnp.sum(x_in_grad, axis=1)
        colour_part = norm_back(x_in_grad, in_gain[:, None], unit, spread, 0)[:3]
        return score_pool, gain_part, shift_part, colour_part

    if blocks == 1:
        score_pool, in_gain_grad, in_shift_grad, all_colors = pull(parts[0], feats)
    else:

        def gather_up(carry, part):
            found = pull(part, features(part))
            return tuple(kept + new for kept, new in zip(carry, found[:3])), found[3]

        start = (
            jnp.zeros((latent.shape[0], in_gain.shape[0]), F32),
            jnp.zeros_like(in_gain),
            jnp.zeros_like(in_shift),
        )
        (score_pool, in_gain_grad, in_shift_grad), stacked = lax.scan(gather_up, start, parts)
        all_colors = stacked.transpose(1, 0, 2).reshape(3, -1)
    color_grad = lax.dynamic_slice(all_colors, (0, mine * own), (3, own))
    score_pool_low = score_pool.astype(BF)
    query_grad = (
        jnp.dot(score_pool_low, key_weight, preferred_element_type=F32) * (1.0 / root)
    ).astype(BF)
    norm_one_grad = contract(query_grad, query_weight, 1, 1)
    latent_grad = mixed_grad + norm_back(norm_one_grad, lat_gain, lat_unit, lat_spread, 1)

    def both(value):
        return jnp.concatenate([value, other(value)], axis=0)

    out_both = both(out_grad)
    hidden_both = both(hidden)
    two_both = both(norm_two)
    pre_both = both(pre_grad)
    attn_both = both(attn_grad)
    one_both = both(norm_one)
    query_both = both(query)
    query_grad_both = both(query_grad)
    pool_both = both(pooled_low)
    score_both = both(score_pool_low)
    wide = jnp.stack(
        [
            jnp.sum(norm_one_grad * lat_unit, axis=0),
            jnp.sum(norm_one_grad, axis=0),
            jnp.sum(norm_two_grad * mix_unit, axis=0),
            jnp.sum(norm_two_grad, axis=0),
        ]
    )
    narrow = jnp.stack([in_gain_grad, in_shift_grad])
    wide = wide + other(wide)
    narrow = narrow + other(narrow)
    return (
        encoded[None],
        latent_grad[None],
        color_grad[None],
        wide[0],
        wide[1],
        contract(one_both, query_grad_both, 0, 0),
        jnp.sum(query_grad_both.astype(F32), axis=0),
        narrow[0],
        narrow[1],
        contract(score_both, query_both, 0, 0) * (1.0 / root),
        contract(pool_both, attn_both, 0, 0),
        jnp.sum(attn_both.astype(F32), axis=0),
        wide[2],
        wide[3],
        contract(two_both, pre_both, 0, 0),
        jnp.sum(pre_both.astype(F32), axis=0),
        contract(hidden_both, out_both, 0, 0),
        jnp.sum(out_both.astype(F32), axis=0),
    )


def solution(mesh):
    lat = P("img", None, None)
    whole = P()
    return jax.shard_map(
        shards,
        mesh=mesh,
        in_specs=(lat, P("img", None, "pix"), P("img", None, "pix"), P("img", "pix"))
        + (whole,) * 15
        + (lat,),
        out_specs=(lat, lat, P("img", None, "pix")) + (whole,) * 15,
        check_vma=False,
    )
```

time: 494 us -> 121 us (0.24)
  blocking collectives: 211 us -> 0 us
  waiting for transfers between devices: 175 us -> 0.26 us
  local copies, waits for them, and re-layouts: 10.8 us -> 32.7 us
  between operations: 14.9 us -> 1.12 us
  other arithmetic: 32.3 us -> 19.2 us
  starting transfers between devices: 0.34 us -> 11.6 us
  matrix products: 49 us -> 54 us
    psum x3 -> x0, waiting for transfers between devices: 175 us -> none  [the longest x1 91.6 us: shards(): lax.psum((key_weight_grad, value_weight_grad, value_bias_grad, in_gain_co...]
    psum x4 -> x0, blocking collectives: 168 us -> none  [the longest x2 127 us: forward_pass(): lax.psum((jnp.sum(weight, axis=1), jnp.dot(weight, values_full, precision...]
    pmax x1 -> x0, blocking collectives: 43.5 us -> none  [forward_pass(): row_top = lax.pmax(local_top, 'pix')]
    concatenate x0 -> x2, local copies, waits for them, and re-layouts: none -> 24.7 us  [the longest x1 24.6 us: features(): jnp.concatenate([part[0:3], position, row_waves[:BANDS], col_waves[:BANDS...]
    unnamed x170 -> x43, local copies, waits for them, and re-layouts: 10.1 us -> 1.34 us
    all_to_all x0 -> x1, starting transfers between devices: none -> 8.31 us  [shards(): lax.all_to_all(jnp.broadcast_to(packed[None], (pix,) + packed.shape), 'pi...]
    convert_element_type x10 -> x8, other arithmetic: 13.3 us -> 5.73 us  [the longest x1 2.13 us: shards(): norm_one = (lat_unit * lat_gain + lat_shift).astype(BF)]
    dot_general x7 -> x9, matrix products: 15.2 us -> 20.5 us  [the longest x1 4.47 us: features(): score = jnp.dot(absorbed, x_in, preferred_element_type=F32)]
  transfers between devices with their start and end apart: 3 -> 13, of which waited for: 2 -> 1; matrix products, arithmetic and copies ran while one was open for 8% -> 82% of each run, Pallas kernels for 0% -> 0%
where the time goes in v1:
time: 121 us; the launch traced here: 119 us
  matrix products  54 us (45%)
  local copies, waits for them, and re-layouts  32.7 us (27%)
  other arithmetic  19.2 us (16%)
  starting transfers between devices  11.6 us (10%)
    dot_general x14, matrix products, contract(): lax.dot_general(left, right, (((left_dim,), (right_dim,)), ((), ())), pre...  33.5 us
    concatenate x1, local copies, waits for them, and re-layouts, features(): jnp.concatenate([part[0:3], position, row_waves[:BANDS], col_waves[:BANDS...  24.6 us
    all_to_all x1, starting transfers between devices, shards(): lax.all_to_all(jnp.broadcast_to(packed[None], (pix,) + packed.shape), 'pi...  8.31 us
    dot_general x1, matrix products, features(): score = jnp.dot(absorbed, x_in, preferred_element_type=F32)  4.47 us
    reduce_sum x2, other arithmetic, norm_stats(): centre = values - jnp.mean(values, axis=axis, keepdims=True)  3.82 us
    dot_general x1, matrix products, pull(): jnp.dot(lifted, x_in, preferred_element_type=F32) - row_delta  3.81 us
    ppermute x12, starting transfers between devices, other(): return lax.ppermute(value, 'img', swap)  3.26 us
    dot_general x1, matrix products, shards(): jnp.dot(norm_one, query_weight, preferred_element_type=F32) + query_bias  3.18 us
  transfers between devices with their start and end apart: 13, of which 1 were waited for; matrix products, arithmetic and copies ran while one was open for 82% of the time, Pallas kernels for 0%

profile of v1, /device:TPU:0, one launch (start us, length us, event | category | flops | bytes accessed | tf_op | source)
XLA Modules:
  0.0 118.8 jit_solution(11999701880877154859)
XLA Ops:
  0.7 0.8 convert_element_type.120
  1.5 0.7 convert_bitcast_fusion.1
  2.3 0.7 convert_element_type.116
  3.1 0.7 broadcast_in_dim.33
  3.8 8.3 %all-to-all-start = ((bf16[16,8,384]{2,1,0:T(8,128)(2,1)}), bf16[16,8,384]{2,1,0:T(8,128)(2,1)S(1)}, u32[]{:S(2)}, u32[]{:S(2)}) async-start(bf16[16,8,384]{2,1,0:T(8,128)(2,1)} %broadcast_in_dim.33), calls=%async_computation | async-start | bytes 196608 | tf_op jit(solution)/shard_map/all_to_all | solution.py:83
  12.1 1.2 %convert_reduce_fusion.5 = f32[256]{0:T(256)S(1)} fusion(bf16[1,256,1024]{2,1,0:T(8,128)(2,1)} %param.21), kind=kLoop, calls=%fused_computation.45 | loop fusion | flops 524032 | bytes 525312 | tf_op jit(solution)/shard_map/reduce_sum | solution.py:35
  13.3 1.3 %fusion.44 = f32[256]{0:T(256)S(1)} fusion(bf16[1,256,1024]{2,1,0:T(8,128)(2,1)} %param.21, f32[256]{0:T(256)S(1)} %broadcast_multiply_fusion.9), kind=kLoop, calls=%fused_computation.72 | loop fusion | flops 1048320 | bytes 526336 | tf_op jit(solution)/shard_map/reduce_sum | solution.py:36
  14.6 2.1 %fusion.37 = bf16[256,1024]{1,0:T(8,128)(2,1)} fusion(bf16[1,256,1024]{2,1,0:T(8,128)(2,1)} %param.21, f32[1024]{0:T(1024)} %param.26, f32[1024]{0:T(1024)} %param.25, f32[256]{0:T(256)S(1)} %add_rsqrt_fusion.2, f32[256]{0:T(256)S(1)} %broadcast_multiply_fusion.9), kind=kLoop, calls=%fused_computation.65 | loop fusion | flops 1572864 | bytes 1058816 | tf_op jit(solution)/shard_map/convert_element_type | solution.py:93
  16.8 3.2 %fusion.22 = bf16[256,1024]{1,0:T(8,128)(2,1)} fusion(bf16[256,1024]{1,0:T(8,128)(2,1)} %fusion.37, bf16[1024,1024]{1,0:T(8,128)(2,1)} %param.27, f32[1024]{0:T(1024)} %param.28), kind=kOutput, calls=%fused_computation.49 | convolution fusion | flops 537395200 | bytes 3149824 | tf_op jit(solution)/shard_map/dot_general | solution.py:94
  20.0 0.5 collective-permute-start.5
  20.5 1.4 %fusion.32 = bf16[256,261]{0,1:T(8,128)(2,1)S(1)} fusion(bf16[256,1024]{1,0:T(8,128)(2,1)} %fusion.22, bf16[261,1024]{1,0:T(8,128)(2,1)S(1)} %copy-done.7), kind=kOutput, calls=%fused_computation.61 | convolution fusion | flops 136972800 | bytes 1192448 | tf_op jit(solution)/shard_map/dot_general | solution.py:29
  21.9 0.6 slice.74
  22.5 0.6 add_convert_fusion.2
  23.3 2.0 %fusion.5 = bf16[128,6144]{1,0:T(8,128)(2,1)S(1)} fusion(bf16[128,224]{1,0:T(8,128)(2,1)} %constant.59.clone, f32[6144]{0:T(1024)S(1)} %bitcast.104), kind=kOutput, calls=%fused_computation.12 | convolution fusion | flops 354484224 | bytes 1654784 | tf_op jit(solution)/shard_map/dot_general | solution.py:104
  25.4 2.0 %fusion.4 = bf16[128,6144]{1,0:T(8,128)(2,1)S(1)} fusion(bf16[128,224]{1,0:T(8,128)(2,1)} %constant.59.clone, f32[6144]{0:T(1024)S(1)} %bitcast.103), kind=kOutput, calls=%fused_computation.11 | convolution fusion | flops 354484224 | bytes 1654784 | tf_op jit(solution)/shard_map/dot_general | solution.py:103
  27.4 1.5 %fusion.85 = (bf16[64,6144]{1,0:T(8,128)(2,1)S(1)}, bf16[64,6144]{1,0:T(8,128)(2,1)}, bf16[64,6144]{1,0:T(8,128)(2,1)}, bf16[64,6144]{1,0:T(8,128)(2,1)}) fusion(bf16[128,6144]{1,0:T(8,128)(2,1)S(1)} %fusion.5, bf16[128,6144]{1,0:T(8,128)(2,1)S(1)} %fusion.4), kind=kLoop, calls=%fused_computation.151 | loop fusion | bytes 6291456 | tf_op jit(solution)/shard_map/slice | solution.py:106
  28.9 24.6 %concatenate.37 = bf16[261,6144]{1,0:T(8,128)(2,1)} concatenate(bf16[3,6144]{1,0:T(4,128)(2,1)} %bitcast.101, bf16[2,6144]{1,0:T(2,128)(2,1)} %bitcast.102, bf16[64,6144]{1,0:T(8,128)(2,1)} %get-tuple-element.60, bf16[64,6144]{1,0:T(8,128)(2,1)} %get-tuple-element.39, bf16[64,6144]{1,0:T(8,128)(2,1)} %get-tuple-element.61, bf16[64,6144]{1,0:T(8,128)(2,1)S(1)} %get-tuple-element.38), dimensions={0} | concatenate | bytes 6414336 | tf_op jit(solution)/shard_map/concatenate | solution.py:105
  53.5 2.6 %convert_reduce_fusion = f32[6144]{0:T(1024)S(1)} fusion(bf16[261,6144]{1,0:T(8,128)(2,1)} %concatenate.37), kind=kLoop, calls=%fused_computation.5 | loop fusion | flops 3201024 | bytes 3231744 | tf_op jit(solution)/shard_map/reduce_sum | solution.py:35
  56.1 0.2 copy-done.2
  56.4 0.9 fusion.6
  57.3 4.5 %fusion.89 = (f32[256]{0:T(256)S(1)}, f32[256,6144]{1,0:T(8,128)S(1)}) fusion(bf16[256,261]{0,1:T(8,128)(2,1)S(1)} %fusion.32, f32[261]{0:T(512)S(1)} %copy-done.19, f32[261]{0:T(512)S(1)} %copy-done.20, f32[6144]{0:T(1024)S(1)} %add_rsqrt_fusion, f32[6144]{0:T(1024)S(1)} %broadcast_multiply_fusion.3, bf16[261,6144]{1,0:T(8,128)(2,1)} %concatenate.37, ...), kind=kOutput, calls=%fused_computation.155 | convolution fusion | flops 833801984 | bytes 9690664 | tf_op jit(solution)/shard_map/dot_general | solution.py:111
  61.8 1.3 %fusion.8 = f32[256]{0:T(256)S(1)} fusion(f32[256,6144]{1,0:T(8,128)S(1)} %get-tuple-element.49, f32[256]{0:T(256)S(1)} %get-tuple-element.48, pred[6144]{0:T(1024)(128)(4,1)S(1)} %gt.13), kind=kLoop, calls=%fused_computation.21 | loop fusion | flops 4718336 | bytes 6299648 | tf_op jit(solution)/shard_map/reduce_sum | solution.py:118
  63.2 0.6 copy-done.3
  63.7 2.2 %fusion.90 = (bf16[256,261]{0,1:T(8,128)(2,1)S(1)}, f32[256,261]{0,1:T(8,128)S(1)}) fusion(f32[256]{0:T(256)S(1)} %fusion.8, f32[261]{0:T(512)S(1)} %copy-done.19, f32[261]{0:T(512)S(1)} %copy-done.20, f32[6144]{0:T(1024)S(1)} %add_rsqrt_fusion, f32[6144]{0:T(1024)S(1)} %broadcast_multiply_fusion.3, bf16[261,6144]{1,0:T(8,128)(2,1)S(1)} %copy-done.3, ...), kind=kOutput, calls=%fused_computation.156 | convolution fusion | flops 835508736 | bytes 9958952 | tf_op jit(solution)/shard_map/dot_general | solution.py:29
  66.0 0.5 fusion.91
  66.6 0.3 multiply_reduce_fusion.4
  66.9 0.3 add_convert_fusion.1
  67.2 0.8 multiply_convert_fusion
  68.0 0.4 copy-done.16
  68.4 1.0 fusion.23
  69.5 1.1 multiply_reduce_fusion.2
  70.6 0.4 fusion.84
  71.0 0.4 multiply_reduce_fusion.7
  71.4 3.8 %fusion.1 = bf16[256,6144]{1,0:T(8,128)(2,1)S(1)} fusion(bf16[256,261]{0,1:T(8,128)(2,1)S(1)} %get-tuple-element.58, f32[256]{0:T(256)S(1)} %get-tuple-element.57, f32[256]{0:T(256)S(1)} %fusion.8, f32[256,6144]{1,0:T(8,128)S(1)} %get-tuple-element.49, f32[256]{0:T(256)S(1)} %get-tuple-element.48, pred[6144]{0:T(1024)(128)(4,1)S(1)} %gt.13, ...), kind=kOutput, calls=%fused_computation.6 | convolution fusion | flops 840093696 | bytes 12838440 | tf_op jit(solution)/shard_map/dot_general | solution.py:171
  75.2 1.8 %convolution_convert_fusion.3 = bf16[256,261]{0,1:T(8,128)(2,1)S(1)} fusion(bf16[256,6144]{1,0:T(8,128)(2,1)S(1)} %fusion.1, f32[261]{0:T(512)S(1)} %copy-done.19, f32[261]{0:T(512)S(1)} %copy-done.20, f32[6144]{0:T(1024)S(1)} %add_rsqrt_fusion, f32[6144]{0:T(1024)S(1)} %broadcast_multiply_fusion.3, bf16[261,6144]{1,0:T(8,128)(2,1)S(1)} %copy-done.3), kind=kOutput, calls=%fused_computation.62 | convolution fusion | flops 830723328 | bytes 6537768 | tf_op jit(solution)/shard_map/dot_general | solution.py:29
  77.0 1.0 fusion.92
  78.1 0.5 fusion.24
  78.6 0.6 collective-permute-start.4
  79.1 1.1 fusion.43
  80.3 7.2 %fusion.83 = (f32[6144]{0:T(1024)S(1)}, f32[6144]{0:T(1024)S(1)}, f32[261]{0:T(512)S(1)}, f32[261]{0:T(512)S(1)}, f32[261,6144]{1,0:T(8,128)}, /*index=5*/f32[261,6144]{1,0:T(8,128)}) fusion(f32[6144]{0:T(1024)S(1)} %add_rsqrt_fusion, f32[6144]{0:T(1024)S(1)} %broadcast_multiply_fusion.3, bf16[261,6144]{1,0:T(8,128)(2,1)S(1)} %copy-done.3, ...), kind=kOutput, calls=%fused_computation.149 | convolution fusion | flops 844953088 | bytes 28984892 | tf_op jit(solution)/shard_map/dot_general | solution.py:29
  87.5 0.9 slice.83
  88.4 0.9 slice.82
  89.6 0.2 collective-permute-start.3
  89.9 3.1 %fusion.31 = bf16[1,256,1024]{2,1,0:T(8,128)(2,1)} fusion(f32[256,1024]{1,0:T(8,128)S(1)} %get-tuple-element.53, bf16[256,1024]{1,0:T(8,128)(2,1)S(1)} %get-tuple-element.54, bf16[1024,1024]{1,0:T(8,128)(2,1)} %param.38, f32[1024]{0:T(1024)S(1)} %copy-done.18), kind=kOutput, calls=%fused_computation.58 | convolution fusion | flops 537657344 | bytes 4198400 | tf_op jit(solution)/shard_map/dot_general | solution.py:153
  93.0 1.4 %fusion.42 = f32[1,256,1024]{2,1,0:T(8,128)} fusion(f32[256,1024]{1,0:T(8,128)S(1)} %get-tuple-element.36, bf16[1,256,1024]{2,1,0:T(8,128)(2,1)S(1)} %copy-done.4, f32[256,1024]{1,0:T(8,128)S(1)} %get-tuple-element.59, f32[256]{0:T(256)S(1)} %broadcast_multiply_fusion.4, f32[256]{0:T(256)S(1)} %broadcast_multiply_fusion.5, f32[1024]{0:T(1024)S(1)} %copy-done.9, ...), kind=kLoop, calls=%fused_computation.70 | loop fusion | flops 2359296 | bytes 3678208 | tf_op jit(solution)/shard_map/broadcast_in_dim | solution.py:228
  94.4 0.6 broadcast_in_dim.39
  95.0 0.3 collective-permute-start
  95.3 0.6 slice_reduce_fusion
  95.9 0.2 collective-permute-done
  96.2 0.3 collective-permute-start.7
  96.5 0.2 collective-permute-start.2
  96.8 0.3 collective-permute-start.9
  97.1 0.6 fusion.88
  97.9 2.6 %convolution_multiply_fusion = f32[261,1024]{1,0:T(8,128)} fusion(bf16[256,1024]{1,0:T(8,128)(2,1)} %collective-permute-done.5, bf16[256,1024]{1,0:T(8,128)(2,1)} %fusion.22, bf16[256,261]{0,1:T(8,128)(2,1)S(1)} %collective-permute-done.4, bf16[256,261]{0,1:T(8,128)(2,1)S(1)} %convolution_convert_fusion.3), kind=kOutput, calls=%fused_computation.36 | convolution fusion | flops 276577280 | bytes 2384896 | tf_op jit(solution)/shard_map/dot_general | solution.py:29
  100.6 0.3 collective-permute-start.8
  100.9 1.8 %convert_reduce_fusion.1 = f32[1024]{0:T(1024)} fusion(bf16[256,1024]{1,0:T(8,128)(2,1)} %collective-permute-done.11, bf16[256,1024]{1,0:T(8,128)(2,1)S(1)} %bitcast.95), kind=kLoop, calls=%fused_computation.31 | loop fusion | flops 2620416 | bytes 1052672 | tf_op jit(solution)/shard_map/reduce_sum | solution.py:244
  102.7 0.8 convert_reduce_fusion.3
  103.5 0.2 collective-permute-start.10
  103.7 1.4 %fusion.64 = f32[261,1024]{1,0:T(8,128)} fusion(bf16[256,1024]{1,0:T(8,128)(2,1)S(1)} %collective-permute-done.7, bf16[256,1024]{1,0:T(8,128)(2,1)S(1)} %get-tuple-element.35, bf16[256,261]{0,1:T(8,128)(2,1)S(1)} %collective-permute-done.6, bf16[256,261]{0,1:T(8,128)(2,1)S(1)} %get-tuple-element.50), kind=kOutput, calls=%fused_computation.106 | convolution fusion | flops 276310016 | bytes 2384896 | tf_op jit(solution)/shard_map/dot_general | solution.py:29
  105.1 0.8 convert_reduce_fusion.4
  105.9 0.8 convert_reduce_fusion.2
  106.7 4.5 %fusion.49 = f32[1024,1024]{1,0:T(8,128)} fusion(bf16[256,1024]{1,0:T(8,128)(2,1)} %collective-permute-done.1, bf16[256,1024]{1,0:T(8,128)(2,1)} %fusion.37, bf16[256,1024]{1,0:T(8,128)(2,1)S(1)} %collective-permute-done.2, bf16[256,1024]{1,0:T(8,128)(2,1)S(1)} %fusion.24), kind=kOutput, calls=%fused_computation.77 | convolution fusion | flops 1077936128 | bytes 6291456 | tf_op jit(solution)/shard_map/dot_general | solution.py:29
  111.2 3.3 %fusion.56 = f32[1024,1024]{1,0:T(8,128)} fusion(bf16[256,1024]{1,0:T(8,128)(2,1)S(1)} %collective-permute-done.8, bf16[256,1024]{1,0:T(8,128)(2,1)S(1)} %add_convert_fusion.1, bf16[256,1024]{1,0:T(8,128)(2,1)S(1)} %collective-permute-done.9, bf16[256,1024]{1,0:T(8,128)(2,1)S(1)} %fusion.23), kind=kOutput, calls=%fused_computation.86 | convolution fusion | flops 1077936128 | bytes 6291456 | tf_op jit(solution)/shard_map/dot_general | solution.py:29
  114.5 4.4 %fusion.60 = f32[1024,1024]{1,0:T(8,128)} fusion(bf16[256,1024]{1,0:T(8,128)(2,1)S(1)} %collective-permute-done.10, bf16[256,1024]{1,0:T(8,128)(2,1)S(1)} %get-tuple-element.54, bf16[256,1024]{1,0:T(8,128)(2,1)} %collective-permute-done.11, bf16[256,1024]{1,0:T(8,128)(2,1)S(1)} %bitcast.96), kind=kOutput, calls=%fused_computation.91 | convolution fusion | flops 1077936128 | bytes 6291456 | tf_op jit(solution)/shard_map/dot_general | solution.py:29
  (84 shorter events, 1.0 us)
Async XLA Ops:
  0.7 66.5 %copy-start = (bf16[1024,1024]{1,0:T(8,128)(2,1)S(1)}, bf16[1024,1024]{1,0:T(8,128)(2,1)}, u32[]{:S(2)}) copy-start(bf16[1024,1024]{1,0:T(8,128)(2,1)} %param.36) | copy-start | bytes 6291460
  0.7 19.8 %copy-start.6 = (bf16[1,256,1024]{2,1,0:T(8,128)(2,1)S(1)}, bf16[1,256,1024]{2,1,0:T(8,128)(2,1)}, u32[]{:S(2)}) copy-start(bf16[1,256,1024]{2,1,0:T(8,128)(2,1)} %param.40) | copy-start | bytes 1572868
  0.7 19.8 %copy-start.7 = (bf16[261,1024]{1,0:T(8,128)(2,1)S(1)}, bf16[261,1024]{1,0:T(8,128)(2,1)}, u32[]{:S(2)}) copy-start(bf16[261,1024]{1,0:T(8,128)(2,1)} %param.31) | copy-start | bytes 1603588
  3.8 18.1 %all-to-all-start = ((bf16[16,8,384]{2,1,0:T(8,128)(2,1)}), bf16[16,8,384]{2,1,0:T(8,128)(2,1)S(1)}, u32[]{:S(2)}, u32[]{:S(2)}) async-start(bf16[16,8,384]{2,1,0:T(8,128)(2,1)} %broadcast_in_dim.33), calls=%async_computation | async-start | bytes 196608 | tf_op jit(solution)/shard_map/all_to_all | solution.py:83
  14.6 5.8 %copy-start.11 = (f32[256]{0:T(256)}, f32[256]{0:T(256)S(1)}, u32[]{:S(2)}) copy-start(f32[256]{0:T(256)S(1)} %add_rsqrt_fusion.2) | copy-start | bytes 3076
  16.8 89.9 %collective-permute-start.1 = (bf16[256,1024]{1,0:T(8,128)(2,1)}, bf16[256,1024]{1,0:T(8,128)(2,1)}, u32[]{:S(2)}, u32[]{:S(2)}) collective-permute-start(bf16[256,1024]{1,0:T(8,128)(2,1)} %fusion.37), channel_id=1, source_target_pairs={{0,16},{16,0},{1,17},{17,1},{2,18},{18,2},{3,19},{19,3},{4,20},{20... | collective-permute-start | bytes 1572872 | tf_op jit(solution)/shard_map/ppermute | solution.py:88
  20.0 76.8 %collective-permute-start.5 = (bf16[256,1024]{1,0:T(8,128)(2,1)}, bf16[256,1024]{1,0:T(8,128)(2,1)}, u32[]{:S(2)}, u32[]{:S(2)}) collective-permute-start(bf16[256,1024]{1,0:T(8,128)(2,1)} %fusion.22), channel_id=1, source_target_pairs={{0,16},{16,0},{1,17},{17,1},{2,18},{18,2},{3,19},{19,3},{4,20},{20... | collective-permute-start | bytes 1572872 | tf_op jit(solution)/shard_map/ppermute | solution.py:88
  20.5 77.3 %collective-permute-start.11 = (bf16[256,1024]{1,0:T(8,128)(2,1)S(1)}, bf16[256,1024]{1,0:T(8,128)(2,1)}, u32[]{:S(2)}, u32[]{:S(2)}) collective-permute-start(bf16[256,1024]{1,0:T(8,128)(2,1)S(1)} %bitcast.94), channel_id=1, source_target_pairs={{0,16},{16,0},{1,17},{17,1},{2,18},{18,2},{3,19},{19,3},{4,20},{20... | collective-permute-start | bytes 1572872 | tf_op jit(solution)/shard_map/ppermute | solution.py:88
  53.5 2.9 %copy-start.2 = (bf16[261,6144]{1,0:T(8,128)(2,1)S(1)}, bf16[261,6144]{1,0:T(8,128)(2,1)}, u32[]{:S(2)}) copy-start(bf16[261,6144]{1,0:T(8,128)(2,1)} %concatenate.37) | copy-start | bytes 9621508
  53.5 3.8 %copy-start.19 = (f32[261]{0:T(512)S(1)}, f32[261]{0:T(512)}, u32[]{:S(2)}) copy-start(f32[261]{0:T(512)} %param.30) | copy-start | bytes 3136
  53.5 3.8 %copy-start.20 = (f32[261]{0:T(512)S(1)}, f32[261]{0:T(512)}, u32[]{:S(2)}) copy-start(f32[261]{0:T(512)} %param.29) | copy-start | bytes 3136
  61.8 1.9 %copy-start.3 = (bf16[261,6144]{1,0:T(8,128)(2,1)S(1)}, bf16[261,6144]{1,0:T(8,128)(2,1)}, u32[]{:S(2)}) copy-start(bf16[261,6144]{1,0:T(8,128)(2,1)} %concatenate.37) | copy-start | bytes 9621508
  63.7 2.3 %copy-start.4 = (bf16[1,256,1024]{2,1,0:T(8,128)(2,1)S(1)}, bf16[1,256,1024]{2,1,0:T(8,128)(2,1)}, u32[]{:S(2)}) copy-start(bf16[1,256,1024]{2,1,0:T(8,128)(2,1)} %param.21) | copy-start | bytes 1572868
  63.7 2.3 %copy-start.5 = (bf16[261,1024]{1,0:T(8,128)(2,1)S(1)}, bf16[261,1024]{1,0:T(8,128)(2,1)}, u32[]{:S(2)}) copy-start(bf16[261,1024]{1,0:T(8,128)(2,1)} %param.32) | copy-start | bytes 1603588
  63.7 2.3 %copy-start.13 = (f32[1024]{0:T(1024)S(1)}, f32[1024]{0:T(1024)}, u32[]{:S(2)}) copy-start(f32[1024]{0:T(1024)} %param.33) | copy-start | bytes 12292
  66.0 0.9 copy-start.10
  66.0 0.9 copy-start.14
  66.0 1.2 copy-start.17
  66.8 1.6 %copy-start.16 = (bf16[1024,1024]{1,0:T(8,128)(2,1)S(1)}, bf16[1024,1024]{1,0:T(8,128)(2,1)}, u32[]{:S(2)}) copy-start(bf16[1024,1024]{1,0:T(8,128)(2,1)} %param.38) | copy-start | bytes 6291460
  77.0 1.1 copy-start.8
  77.0 2.1 %copy-start.9 = (f32[1024]{0:T(1024)S(1)}, f32[1024]{0:T(1024)}, u32[]{:S(2)}) copy-start(f32[1024]{0:T(1024)} %param.25) | copy-start | bytes 12292
  77.0 2.1 %copy-start.12 = (f32[256]{0:T(256)S(1)}, f32[256]{0:T(256)}, u32[]{:S(2)}) copy-start(f32[256]{0:T(256)} %copy-done.11) | copy-start | bytes 3076
  77.0 2.1 %copy-start.15 = (bf16[1024,1024]{1,0:T(8,128)(2,1)S(1)}, bf16[1024,1024]{1,0:T(8,128)(2,1)}, u32[]{:S(2)}) copy-start(bf16[1024,1024]{1,0:T(8,128)(2,1)} %param.27) | copy-start | bytes 6291460
  78.6 18.0 %collective-permute-start.4 = (bf16[256,261]{0,1:T(8,128)(2,1)S(1)}, bf16[256,261]{0,1:T(8,128)(2,1)S(1)}, u32[]{:S(2)}, u32[]{:S(2)}) collective-permute-start(bf16[256,261]{0,1:T(8,128)(2,1)S(1)} %convolution_convert_fusion.3), channel_id=1, source_target_pairs={{0,16},{16,0},{1,17},{17,1},{2,18},{18,2},{3,19},{19,3},{4,20},{20... | collective-permute-start | bytes 400904 | tf_op jit(solution)/shard_map/ppermute | solution.py:88
  80.2 9.6 %copy-start.18 = (f32[1024]{0:T(1024)S(1)}, f32[1024]{0:T(1024)}, u32[]{:S(2)}) copy-start(f32[1024]{0:T(1024)} %param.39) | copy-start | bytes 12292
  89.6 5.4 %collective-permute-start.3 = (f32[2,261]{1,0:T(2,128)S(1)}, f32[2,261]{1,0:T(2,128)S(1)}, u32[]{:S(2)}, u32[]{:S(2)}) collective-permute-start(f32[2,261]{1,0:T(2,128)S(1)} %pad_maximum_fusion.9), channel_id=1, source_target_pairs={{0,16},{16,0},{1,17},{17,1},{2,18},{18,2},{3,19},{19,3},{4,20},{20... | collective-permute-start | bytes 6272 | tf_op jit(solution)/shard_map/ppermute | solution.py:88
  95.0 1.2 collective-permute-start
  96.2 4.4 %collective-permute-start.7 = (bf16[256,1024]{1,0:T(8,128)(2,1)S(1)}, bf16[256,1024]{1,0:T(8,128)(2,1)S(1)}, u32[]{:S(2)}, u32[]{:S(2)}) collective-permute-start(bf16[256,1024]{1,0:T(8,128)(2,1)S(1)} %get-tuple-element.35), channel_id=1, source_target_pairs={{0,16},{16,0},{1,17},{17,1},{2,18},{18,2},{3,19},{19,3},{4,20},{20... | collective-permute-start | bytes 1572872 | tf_op jit(solution)/shard_map/ppermute | solution.py:88
  96.5 8.6 %collective-permute-start.2 = (bf16[256,1024]{1,0:T(8,128)(2,1)S(1)}, bf16[256,1024]{1,0:T(8,128)(2,1)S(1)}, u32[]{:S(2)}, u32[]{:S(2)}) collective-permute-start(bf16[256,1024]{1,0:T(8,128)(2,1)S(1)} %fusion.24), channel_id=1, source_target_pairs={{0,16},{16,0},{1,17},{17,1},{2,18},{18,2},{3,19},{19,3},{4,20},{20... | collective-permute-start | bytes 1572872 | tf_op jit(solution)/shard_map/ppermute | solution.py:88
  96.8 9.1 %collective-permute-start.9 = (bf16[256,1024]{1,0:T(8,128)(2,1)S(1)}, bf16[256,1024]{1,0:T(8,128)(2,1)S(1)}, u32[]{:S(2)}, u32[]{:S(2)}) collective-permute-start(bf16[256,1024]{1,0:T(8,128)(2,1)S(1)} %fusion.23), channel_id=1, source_target_pairs={{0,16},{16,0},{1,17},{17,1},{2,18},{18,2},{3,19},{19,3},{4,20},{20... | collective-permute-start | bytes 1572872 | tf_op jit(solution)/shard_map/ppermute | solution.py:88
  97.7 5.7 %collective-permute-start.6 = (bf16[256,261]{0,1:T(8,128)(2,1)S(1)}, bf16[256,261]{0,1:T(8,128)(2,1)S(1)}, u32[]{:S(2)}, u32[]{:S(2)}) collective-permute-start(bf16[256,261]{0,1:T(8,128)(2,1)S(1)} %get-tuple-element.50), channel_id=1, source_target_pairs={{0,16},{16,0},{1,17},{17,1},{2,18},{18,2},{3,19},{19,3},{4,20},{20... | collective-permute-start | bytes 400904 | tf_op jit(solution)/shard_map/ppermute | solution.py:88
  100.6 10.6 %collective-permute-start.8 = (bf16[256,1024]{1,0:T(8,128)(2,1)S(1)}, bf16[256,1024]{1,0:T(8,128)(2,1)S(1)}, u32[]{:S(2)}, u32[]{:S(2)}) collective-permute-start(bf16[256,1024]{1,0:T(8,128)(2,1)S(1)} %add_convert_fusion.1), channel_id=1, source_target_pairs={{0,16},{16,0},{1,17},{17,1},{2,18},{18,2},{3,19},{19,3},{4,20},{20... | collective-permute-start | bytes 1572872 | tf_op jit(solution)/shard_map/ppermute | solution.py:88
  103.5 11.0 %collective-permute-start.10 = (bf16[256,1024]{1,0:T(8,128)(2,1)S(1)}, bf16[256,1024]{1,0:T(8,128)(2,1)S(1)}, u32[]{:S(2)}, u32[]{:S(2)}) collective-permute-start(bf16[256,1024]{1,0:T(8,128)(2,1)S(1)} %get-tuple-element.54), channel_id=1, source_target_pairs={{0,16},{16,0},{1,17},{17,1},{2,18},{18,2},{3,19},{19,3},{4,20},{20... | collective-permute-start | bytes 1572872 | tf_op jit(solution)/shard_map/ppermute | solution.py:88
  111.2 7.7 %copy-start.1 = (bf16[1024,1024]{1,0:T(8,128)(2,1)S(1)}, bf16[1024,1024]{1,0:T(8,128)(2,1)}, u32[]{:S(2)}) copy-start(bf16[1024,1024]{1,0:T(8,128)(2,1)} %param.36) | copy-start | bytes 6291460

commit v2 on v1

--- a/solution.py
+++ b/solution.py
@@ -4,6 +4,8 @@
 import jax.numpy as jnp
 import numpy as np
 from jax import lax
+from jax.experimental import pallas as pl
+from jax.experimental.pallas import tpu as pltpu
 from jax.sharding import PartitionSpec as P
 
 BANDS = 64
@@ -11,8 +13,12 @@
 EPSILON = 1e-05
 FLOOR = -1e30
 BLOCK = 16
+LANES = 128
 BF = jnp.bfloat16
 F32 = jnp.float32
+VM = pl.BlockSpec(memory_space=pltpu.VMEM)
+ANY = pl.BlockSpec(memory_space=pl.ANY)
+MIB = 1 << 20
 
 
 def fourier_lookup():
@@ -46,7 +52,574 @@
     )
 
 
-def shards(
+def out(shape, dtype):
+    return jax.ShapeDtypeStruct(shape, dtype)
+
+
+def padded(rows, step):
+    return -(-rows // step) * step
+
+
+def lane_ids(shape):
+    return lax.broadcasted_iota(jnp.int32, shape, len(shape) - 1)
+
+
+def waves_first(values, features):
+    width = values.shape[1]
+    lead = features - 4 * BANDS
+    at = lane_ids(values.shape)
+    waves = pltpu.roll(values, width - lead, 1)
+    rest = pltpu.roll(values, 4 * BANDS, 1)
+    return jnp.where(at < 4 * BANDS, waves, jnp.where(at < features, rest, 0.0))
+
+
+def waves_last(values, features):
+    width = values.shape[1]
+    lead = features - 4 * BANDS
+    at = lane_ids(values.shape)
+    rest = pltpu.roll(values, width - 4 * BANDS, 1)
+    waves = pltpu.roll(values, lead, 1)
+    return jnp.where(at < lead, rest, jnp.where(at < features, waves, 0.0))
+
+
+def fold(values):
+    total = values[:, :LANES]
+    for start in range(LANES, values.shape[1], LANES):
+        total = total + values[:, start : start + LANES]
+    return total
+
+
+def fold_max(values):
+    total = values[:, :LANES]
+    for start in range(LANES, values.shape[1], LANES):
+        total = jnp.maximum(total, values[:, start : start + LANES])
+    return total
+
+
+def fold_rows(values):
+    total = values[:8]
+    for start in range(8, values.shape[0], 8):
+        total = total + values[start : start + 8]
+    return total
+
+
+def slot_of(kept_row):
+    own = kept_row.shape[1]
+    shape = (own, own)
+    upper = lax.broadcasted_iota(jnp.int32, shape, 0) <= lax.broadcasted_iota(jnp.int32, shape, 1)
+    tall = jnp.broadcast_to(kept_row, (8, own)).astype(BF)
+    rank = jnp.dot(tall, jnp.where(upper, 1.0, 0.0).astype(BF), preferred_element_type=F32)[:1]
+    slot = jnp.where(kept_row > 0, rank - 1.0, -1.0)
+    return slot == lax.broadcasted_iota(jnp.int32, shape, 0).astype(F32)
+
+
+def pack_kernel(pixels, coords, kept, packed, rows):
+    rows[...] = jnp.zeros_like(rows)
+    rows[0:3, :] = pixels[...]
+    rows[3:5, :] = coords[...].astype(F32)
+    kept_row = kept[...].astype(F32)
+    rows[5:6, :] = kept_row
+    slots = jnp.where(slot_of(kept_row), 1.0, 0.0).astype(BF)
+    squeezed = contract(rows[...].astype(BF), slots, 1, 1).astype(BF)
+    packed[...] = jnp.broadcast_to(squeezed[None], packed.shape)
+
+
+def pad_rows(target, source):
+    rows = source.shape[0]
+    whole = rows // LANES * LANES
+    target[:whole, :] = source[:whole, :]
+    target[whole:, :] = jnp.zeros_like(target[whole:, :])
+    target[whole:rows, :] = source[whole:, :]
+
+
+def query_kernel(
+    features, latent, gain, shift, bias, weight_hbm, key_hbm, grad, down_hbm,
+    one, query, absorbed, hidden_grad, weight, key_raw, key, down, sems,
+):
+    copies = [
+        pltpu.make_async_copy(weight_hbm, weight, sems.at[0]),
+        pltpu.make_async_copy(key_hbm, key_raw, sems.at[1]),
+        pltpu.make_async_copy(down_hbm, down, sems.at[2]),
+    ]
+    for copy in copies:
+        copy.start()
+    count, dim = latent.shape
+    step = 32
+    for start in range(0, count, step):
+        unit, _ = norm_stats(latent[start : start + step, :].astype(F32), 1)
+        one[start : start + step, :] = (unit * gain[...] + shift[...]).astype(BF)
+    copies[0].wait()
+    step = 256
+    for start in range(0, dim, step):
+        part = jnp.dot(one[...], weight[:, start : start + step], preferred_element_type=F32)
+        query[:, start : start + step] = (part + bias[:, start : start + step]).astype(BF)
+    copies[1].wait()
+    pad_rows(key, key_raw)
+    lifted = contract(query[...], key[...], 1, 1) * (1.0 / math.sqrt(dim))
+    absorbed[...] = waves_first(lifted, features).astype(BF)
+    copies[2].wait()
+    for start in range(0, dim, step):
+        hidden_grad[:, start : start + step] = contract(grad[...], down[start : start + step, :], 1, 1)
+
+
+def as_column(row, width, features):
+    wide = jnp.concatenate([row, jnp.zeros((1, width - row.shape[1]), F32)], axis=1)
+    tall = jnp.broadcast_to(wide, (LANES, width))
+    return jnp.transpose(waves_first(tall, features))
+
+
+def forward_kernel(
+    features, step,
+    segments, absorbed, hidden_grad, latent, grad, table, in_gain, in_shift,
+    value_hbm, value_bias, gain, shift, up_hbm, up_bias, down_hbm, down_bias,
+    encoded, packs, mixed_grad, pool_out, lift_out, x_out, unit_out, spread_out, weight_out, stats, sums,
+    placed, gains, shifts, top, total, pooled, mixed, mix_unit, mix_spread,
+    value_raw, value, up, down, sems,
+):
+    copies = [
+        pltpu.make_async_copy(value_hbm, value_raw, sems.at[0]),
+        pltpu.make_async_copy(up_hbm, up, sems.at[1]),
+        pltpu.make_async_copy(down_hbm, down, sems.at[2]),
+    ]
+    for copy in copies:
+        copy.start()
+    count, dim = latent.shape
+    pix, _, own = segments.shape
+    kept = x_out.shape[1]
+    tall = x_out.shape[0]
+    rows = unit_out.shape[0]
+    waves = 4 * BANDS
+
+    placed[...] = jnp.zeros_like(placed)
+
+    def place(index, offset):
+        segment = segments[index].astype(F32)
+        wide = jnp.concatenate([segment, jnp.zeros((8, LANES), F32)], axis=1)
+        inside = lax.rem(offset, LANES)
+        base = pl.multiple_of(jnp.minimum(offset - inside, kept), LANES)
+        placed[:, pl.ds(base, own + LANES)] += pltpu.roll(wide, inside, 1)
+        return offset + jnp.sum(segment[5:6, :]).astype(jnp.int32)
+
+    lax.fori_loop(0, pix, place, jnp.int32(0))
+    gains[...] = as_column(in_gain[...], tall, features)
+    shifts[...] = as_column(in_shift[...], tall, features)
+    top[...] = jnp.full_like(top, FLOOR)
+
+    def make(index, carry):
+        lanes = pl.ds(pl.multiple_of(index * step, LANES), step)
+        raw = placed[:, lanes]
+        places = lax.broadcasted_iota(jnp.int32, (table.shape[1], step), 0).astype(F32)
+        row_hot = jnp.where(places == raw[3:4], 1.0, 0.0).astype(BF)
+        col_hot = jnp.where(places == raw[4:5], 1.0, 0.0).astype(BF)
+        row_waves = jnp.dot(table[...], row_hot, preferred_element_type=F32)
+        col_waves = jnp.dot(table[...], col_hot, preferred_element_type=F32)
+        at = lax.broadcasted_iota(jnp.int32, raw.shape, 0)
+        position = (raw * (2.0 / (GRID - 1)) - 1.0).astype(BF).astype(F32)
+        extra = jnp.where(at < 3, raw, jnp.where(at < 5, position, 0.0))
+        mean = (
+            jnp.sum(row_waves, axis=0, keepdims=True)
+            + jnp.sum(col_waves, axis=0, keepdims=True)
+            + jnp.sum(extra, axis=0, keepdims=True)
+        ) * (1.0 / features)
+        row_waves = row_waves - mean
+        col_waves = col_waves - mean
+        extra = jnp.where(at < features - waves, extra - mean, 0.0)
+        square = (
+            jnp.sum(row_waves * row_waves, axis=0, keepdims=True)
+            + jnp.sum(col_waves * col_waves, axis=0, keepdims=True)
+            + jnp.sum(extra * extra, axis=0, keepdims=True)
+        ) * (1.0 / features)
+        spread = lax.rsqrt(square + EPSILON)
+        spread_out[:, lanes] = jnp.broadcast_to(spread, (8, step))
+        for piece, start in (
+            (row_waves[:BANDS], 0),
+            (col_waves[:BANDS], BANDS),
+            (row_waves[BANDS:], 2 * BANDS),
+            (col_waves[BANDS:], 3 * BANDS),
+            (extra, waves),
+        ):
+            unit = piece * spread
+            span = slice(start, start + piece.shape[0])
+            unit_out[span, lanes] = unit
+            wide = unit * gains[span, :1] + shifts[span, :1]
+            if start == waves:
+                wide = jnp.concatenate([wide, jnp.zeros((tall - waves - 8, step), F32)], axis=0)
+                span = slice(waves, tall)
+            x_out[span, lanes] = wide.astype(BF)
+        score = jnp.dot(absorbed[...], x_out[:, lanes], preferred_element_type=F32)
+        weight_out[:, lanes] = score
+        top[...] = jnp.maximum(top[...], fold_max(score))
+        return carry
+
+    lax.fori_loop(0, kept // step, make, 0)
+    peak = jnp.max(top[...], axis=1, keepdims=True)
+    top[...] = jnp.broadcast_to(peak, top.shape)
+    total[...] = jnp.zeros_like(total)
+    pooled[...] = jnp.zeros_like(pooled)
+
+    def pool(index, carry):
+        lanes = pl.ds(pl.multiple_of(index * step, LANES), step)
+        weight = jnp.exp(weight_out[:, lanes] - top[:, :1])
+        weight_out[:, lanes] = weight
+        total[...] += fold(weight)
+        pooled[...] += contract(weight.astype(BF), x_out[:, lanes], 1, 1)
+        return carry
+
+    lax.fori_loop(0, kept // step, pool, 0)
+    share = 1.0 / jnp.sum(total[...], axis=1, keepdims=True)
+    pooled[...] = pooled[...] * share
+    pool_out[...] = waves_last(pooled[...], features).astype(BF)
+
+    copies[0].wait()
+    pad_rows(value, value_raw)
+    wide = 256
+    for start in range(0, dim, wide):
+        span = slice(start, start + wide)
+        attn = jnp.dot(pool_out[...], value[:, span], preferred_element_type=F32) + value_bias[:, span]
+        mixed[:, span] = latent[:, span].astype(F32) + attn
+    low = 32
+    hidden, two, pre_grad, attn_grad = packs.at[0], packs.at[1], packs.at[2], packs.at[3]
+    for start in range(0, count, low):
+        span = slice(start, start + low)
+        unit, spread = norm_stats(mixed[span, :], 1)
+        mix_unit[span, :] = unit
+        mix_spread[span, :] = jnp.broadcast_to(spread, (low, LANES))
+        two[span, :] = (unit * gain[...] + shift[...]).astype(BF)
+    copies[1].wait()
+    for start in range(0, dim, wide):
+        span = slice(start, start + wide)
+        act = jnp.dot(two[...], up[:, span], preferred_element_type=F32) + up_bias[:, span]
+        half = 0.5 * (1.0 + lax.erf(act * (1.0 / math.sqrt(2.0))))
+        hidden[:, span] = (act * half).astype(BF)
+        slope = half + act * jnp.exp(-0.5 * act * act) * (1.0 / math.sqrt(2.0 * math.pi))
+        pre_grad[:, span] = (hidden_grad[:, span] * slope).astype(BF)
+    copies[2].wait()
+    for start in range(0, dim, wide):
+        span = slice(start, start + wide)
+        part = jnp.dot(hidden[...], down[:, span], preferred_element_type=F32)
+        encoded[:, span] = (mixed[:, span] + part + down_bias[:, span]).astype(BF)
+    for start in range(0, dim, wide):
+        span = slice(start, start + wide)
+        mixed[:, span] = contract(pre_grad[...], up[span, :], 1, 1)
+    gain_sum = jnp.zeros((8, dim), F32)
+    shift_sum = jnp.zeros((8, dim), F32)
+    for start in range(0, count, low):
+        span = slice(start, start + low)
+        upstream = mixed[span, :]
+        unit = mix_unit[span, :]
+        full = grad[span, :].astype(F32) + norm_back(upstream, gain[...], unit, mix_spread[span, :1], 1)
+        mixed_grad[span, :] = full
+        attn_grad[span, :] = full.astype(BF)
+        gain_sum = gain_sum + fold_rows(upstream * unit)
+        shift_sum = shift_sum + fold_rows(upstream)
+    sums[0:1, :] = jnp.sum(gain_sum, axis=0, keepdims=True)
+    sums[1:2, :] = jnp.sum(shift_sum, axis=0, keepdims=True)
+    lifted = waves_first(contract(attn_grad[...], value[...], 1, 1), features).astype(BF)
+    lift_out[...] = lifted
+    delta = jnp.sum(lifted.astype(F32) * pooled[...], axis=1, keepdims=True)
+    at = lane_ids(stats.shape)
+    stats[...] = jnp.where(at == 0, share, delta)
+
+
+def pull_kernel(
+    features, step,
+    segments, kept_row, absorbed, lifted, x_in, unit_in, spread_in, weight, stats, in_gain,
+    key_hbm, weight_hbm, latent, gain, mixed_grad, sums,
+    query_grad, pool_out, latent_grad, color_grad, vectors,
+    gains, factors, pooled, gain_sum, shift_sum, colors, back, key_raw, key, query_weight, sems,
+):
+    copies = [
+        pltpu.make_async_copy(key_hbm, key_raw, sems.at[0]),
+        pltpu.make_async_copy(weight_hbm, query_weight, sems.at[1]),
+    ]
+    for copy in copies:
+        copy.start()
+    count, dim = latent.shape
+    own = kept_row.shape[1]
+    tall, kept = x_in.shape
+    rows = unit_in.shape[0]
+    waves = 4 * BANDS
+    gains[...] = as_column(in_gain[...], tall, features)
+    factors[:, :count] = jnp.transpose(absorbed[...].astype(F32))[:rows].astype(BF)
+    factors[:, count:] = jnp.transpose(lifted[...].astype(F32))[:rows].astype(BF)
+    pooled[...] = jnp.zeros_like(pooled)
+    gain_sum[...] = jnp.zeros_like(gain_sum)
+    shift_sum[...] = jnp.zeros_like(shift_sum)
+
+    def pull(index, carry):
+        lanes = pl.ds(pl.multiple_of(index * step, LANES), step)
+        x_part = x_in[:, lanes]
+        prob = weight[:, lanes] * stats[:, :1]
+        inner = jnp.dot(lifted[...], x_part, preferred_element_type=F32) - stats[:, 1:2]
+        score_grad = (prob * inner).astype(BF)
+        pooled[...] += contract(score_grad, x_part, 1, 1)
+        both = jnp.concatenate([score_grad, prob.astype(BF)], axis=0)
+        upstream = jnp.dot(factors[...], both, preferred_element_type=F32)
+        unit = unit_in[:, lanes]
+        gain_sum[...] += fold(upstream * unit)
+        shift_sum[...] += fold(upstream)
+        inner = upstream * gains[:rows, :1]
+        mean = jnp.sum(inner, axis=0, keepdims=True) * (1.0 / features)
+        tilt = jnp.sum(inner * unit, axis=0, keepdims=True) * (1.0 / features)
+        colors[:, lanes] = spread_in[:, lanes] * (inner[waves:] - mean - unit[waves:] * tilt)
+        return carry
+
+    lax.fori_loop(0, kept // step, pull, 0)
+    colors[:, kept:] = jnp.zeros((8, own + LANES), F32)
+
+    def skip(index, offset):
+        return offset + jnp.sum(segments[index][5:6, :].astype(F32)).astype(jnp.int32)
+
+    offset = lax.fori_loop(0, lax.axis_index("pix"), skip, jnp.int32(0))
+    inside = lax.rem(offset, LANES)
+    base = pl.multiple_of(jnp.minimum(offset - inside, kept), LANES)
+    window = pltpu.roll(colors[:, pl.ds(base, own + LANES)], own + LANES - inside, 1)[:, :own]
+    slots = jnp.where(slot_of(kept_row[...].astype(F32)), 1.0, 0.0)
+    spread_back = jnp.dot(window, slots, precision=lax.Precision.HIGHEST, preferred_element_type=F32)
+    color_grad[...] = spread_back[:3]
+
+    pool_out[...] = waves_last(pooled[...], features).astype(BF)
+    copies[0].wait()
+    pad_rows(key, key_raw)
+    wide = 256
+    for start in range(0, dim, wide):
+        span = slice(start, start + wide)
+        part = jnp.dot(pool_out[...], key[:, span], preferred_element_type=F32) * (1.0 / math.sqrt(dim))
+        query_grad[:, span] = part.astype(BF)
+    copies[1].wait()
+    for start in range(0, dim, wide):
+        span = slice(start, start + wide)
+        back[:, span] = contract(query_grad[...], query_weight[span, :], 1, 1)
+    low = 32
+    lat_gain_sum = jnp.zeros((8, dim), F32)
+    lat_shift_sum = jnp.zeros((8, dim), F32)
+    for start in range(0, count, low):
+        span = slice(start, start + low)
+        unit, spread = norm_stats(latent[span, :].astype(F32), 1)
+        upstream = back[span, :]
+        latent_grad[span, :] = mixed_grad[span, :] + norm_back(upstream, gain[...], unit, spread, 1)
+        lat_gain_sum = lat_gain_sum + fold_rows(upstream * unit)
+        lat_shift_sum = lat_shift_sum + fold_rows(upstream)
+    vectors[...] = jnp.zeros_like(vectors)
+    vectors[0:1, :] = jnp.sum(lat_gain_sum, axis=0, keepdims=True)
+    vectors[1:2, :] = jnp.sum(lat_shift_sum, axis=0, keepdims=True)
+    vectors[2:4, :] = sums[0:2, :]
+    for at, held in ((4, gain_sum), (5, shift_sum)):
+        flat = jnp.sum(held[...], axis=1, keepdims=True)
+        flat = jnp.concatenate([flat, jnp.zeros((tall - rows, 1), F32)], axis=0)
+        turned = jnp.transpose(jnp.broadcast_to(flat, (tall, LANES)))[:8]
+        vectors[at : at + 1, :tall] = waves_last(turned, features)[:1]
+
+
+def outer(left, right, left_other, right_other):
+    return contract(left[...], right[...], 0, 0) + contract(left_other[...], right_other[...], 0, 0)
+
+
+def column_sum(own, far):
+    rows = fold_rows(own[...].astype(F32)) + fold_rows(far[...].astype(F32))
+    return jnp.sum(rows, axis=0, keepdims=True)
+
+
+def late_kernel(
+    features,
+    hidden, hidden_far, grad, grad_far, grad_cols, grad_cols_far, two, two_far, pre, pre_far, pre_cols, pre_cols_far,
+    pool, pool_far, attn, attn_far,
+    down_grad, down_bias, up_grad, up_bias, value_grad, value_bias,
+):
+    down_grad[...] = outer(hidden, grad, hidden_far, grad_far)
+    up_grad[...] = outer(two, pre, two_far, pre_far)
+    value_grad[...] = outer(pool, attn, pool_far, attn_far)[:features]
+    down_bias[...] = column_sum(grad_cols, grad_cols_far)
+    up_bias[...] = column_sum(pre_cols, pre_cols_far)
+    value_bias[...] = column_sum(attn, attn_far)
+
+
+def last_kernel(
+    features,
+    one, one_far, back, back_far, back_cols, back_cols_far, pool, pool_far, query, query_far, vectors, vectors_far,
+    query_grad, query_bias, key_grad, lat_gain, lat_shift, mlp_gain, mlp_shift, in_gain, in_shift,
+):
+    query_grad[...] = outer(one, back, one_far, back_far)
+    root = 1.0 / math.sqrt(back.shape[1])
+    key_grad[...] = outer(pool, query, pool_far, query_far)[:features] * root
+    query_bias[...] = column_sum(back_cols, back_cols_far)
+    sums = vectors[...] + vectors_far[...]
+    lat_gain[...] = sums[0:1]
+    lat_shift[...] = sums[1:2]
+    mlp_gain[...] = sums[2:3]
+    mlp_shift[...] = sums[3:4]
+    in_gain[...] = sums[4:5, :features]
+    in_shift[...] = sums[5:6, :features]
+
+
+def call(body, outs, args, specs, scratch, vmem, flops, moved):
+    return pl.pallas_call(
+        body,
+        out_shape=outs,
+        in_specs=specs,
+        out_specs=jax.tree.map(lambda _: VM, outs),
+        scratch_shapes=scratch,
+        compiler_params=pltpu.CompilerParams(vmem_limit_bytes=vmem * MIB),
+        cost_estimate=pl.CostEstimate(flops=flops, bytes_accessed=moved, transcendentals=0),
+    )(*args)
+
+
+def on_chip(
+    latents, pixels, coords, kept_mask, lat_gain, lat_shift, query_weight, query_bias, in_gain, in_shift,
+    key_weight, value_weight, value_bias, mlp_gain, mlp_shift, up_weight, up_bias, down_weight, down_bias,
+    cotangent,
+):
+    pix = lax.axis_size("pix")
+    own = pixels.shape[2]
+    kept = pix * own // 2
+    _, count, dim = latents.shape
+    features = in_gain.shape[0]
+    tall = padded(features, LANES)
+    rows = padded(features, 8)
+    step = 512 if kept % 512 == 0 else LANES
+    latent, out_grad = latents[0], cotangent[0]
+
+    def flat(vector):
+        return vector.reshape(1, -1)
+
+    swap = [(0, 1), (1, 0)]
+
+    def other(value):
+        return lax.ppermute(value, "img", swap)
+
+    packed = call(
+        pack_kernel, out((pix, 8, own), BF), (pixels[0], coords[0], kept_mask), (VM,) * 3,
+        [pltpu.VMEM((8, own), F32)], 16, 4 * 8 * own * own, 16 * 8 * own,
+    )
+    segments = lax.all_to_all(packed, "pix", 0, 0)
+
+    grid_matrix = pltpu.VMEM((dim, dim), BF)
+    raw = pltpu.VMEM((features, dim), BF)
+    wide = pltpu.VMEM((tall, dim), BF)
+    one, query, absorbed, hidden_grad = call(
+        lambda *refs: query_kernel(features, *refs),
+        (out((count, dim), BF), out((count, dim), BF), out((count, tall), BF), out((count, dim), F32)),
+        (latent, flat(lat_gain), flat(lat_shift), flat(query_bias), query_weight, key_weight, out_grad, down_weight),
+        (VM, VM, VM, VM, ANY, ANY, VM, ANY),
+        [grid_matrix, raw, wide, grid_matrix, pltpu.SemaphoreType.DMA((3,))],
+        32, 4 * count * dim * dim + 2 * count * dim * tall, 8 * MIB,
+    )
+
+    table = np.zeros((2 * BANDS, padded(GRID, LANES)), np.float32)
+    table[:, :GRID] = fourier_lookup()
+    column = pltpu.VMEM((tall, LANES), F32)
+    narrow = pltpu.VMEM((count, LANES), F32)
+    area = pltpu.VMEM((count, dim), F32)
+    (
+        encoded, packs, mixed_grad, pooled, lifted, x_in, unit_in, spread_in, weight, stats, sums,
+    ) = call(
+        lambda *refs: forward_kernel(features, step, *refs),
+        (
+            out((count, dim), BF), out((4, count, dim), BF), out((count, dim), F32), out((count, tall), BF),
+            out((count, tall), BF), out((tall, kept), BF), out((rows, kept), F32), out((8, kept), F32),
+            out((count, kept), F32), out((count, LANES), F32), out((8, dim), F32),
+        ),
+        (
+            segments, absorbed, hidden_grad, latent, out_grad, jnp.asarray(table, BF), flat(in_gain), flat(in_shift),
+            value_weight, flat(value_bias), flat(mlp_gain), flat(mlp_shift), up_weight, flat(up_bias), down_weight,
+            flat(down_bias),
+        ),
+        (VM,) * 8 + (ANY, VM, VM, VM, ANY, VM, ANY, VM),
+        [
+            pltpu.VMEM((8, kept + own + LANES), F32), column, column, narrow, narrow, pltpu.VMEM((count, tall), F32),
+            area, area, narrow, raw, wide, grid_matrix, grid_matrix, pltpu.SemaphoreType.DMA((3,)),
+        ],
+        52, 6 * count * dim * dim + 4 * count * dim * tall + 6 * kept * count * tall, 8 * MIB,
+    )
+
+    query_grad, score_pool, latent_grad, color_grad, vectors = call(
+        lambda *refs: pull_kernel(features, step, *refs),
+        (
+            out((count, dim), BF), out((count, tall), BF), out((count, dim), F32), out((3, own), F32),
+            out((8, dim), F32),
+        ),
+        (
+            segments, kept_mask, absorbed, lifted, x_in, unit_in, spread_in, weight, stats, flat(in_gain),
+            key_weight, query_weight, latent, flat(lat_gain), mixed_grad, sums,
+        ),
+        (VM,) * 10 + (ANY, ANY) + (VM,) * 4,
+        [
+            column, pltpu.VMEM((rows, 2 * count), BF), pltpu.VMEM((count, tall), F32),
+            pltpu.VMEM((rows, LANES), F32), pltpu.VMEM((rows, LANES), F32),
+            pltpu.VMEM((8, kept + own + LANES), F32), area, raw, wide, grid_matrix, pltpu.SemaphoreType.DMA((2,)),
+        ],
+        52, 2 * count * dim * dim + 2 * count * dim * tall + 8 * kept * count * tall, 8 * MIB,
+    )
+
+    block = 256
+    cols = pl.BlockSpec((count, block), lambda i: (0, i))
+    full = pl.BlockSpec((count, dim), lambda i: (0, 0))
+    pool_spec = pl.BlockSpec((count, tall), lambda i: (0, 0))
+    strip = pl.BlockSpec((block, dim), lambda i: (i, 0))
+    slab = pl.BlockSpec((features, block), lambda i: (0, i))
+    line = pl.BlockSpec((1, block), lambda i: (0, i))
+    square = out((dim, dim), F32)
+    slab_out = out((features, dim), F32)
+    line_out = out((1, dim), F32)
+    hidden, two, pre_grad, attn_grad = packs[0], packs[1], packs[2], packs[3]
+    packs_far = other(packs)
+    hidden_far, two_far, pre_far, attn_far = packs_far[0], packs_far[1], packs_far[2], packs_far[3]
+    grad_far = other(out_grad)
+    pooled_far = other(pooled)
+    down_weight_grad, down_bias_grad, up_weight_grad, up_bias_grad, value_weight_grad, value_bias_grad = pl.pallas_call(
+        lambda *refs: late_kernel(features, *refs),
+        grid=(dim // block,),
+        out_shape=(square, line_out, square, line_out, slab_out, line_out),
+        in_specs=(
+            cols, cols, full, full, cols, cols, cols, cols, full, full, cols, cols, pool_spec, pool_spec, cols, cols,
+        ),
+        out_specs=(strip, line, strip, line, slab, line),
+        compiler_params=pltpu.CompilerParams(vmem_limit_bytes=40 * MIB),
+        cost_estimate=pl.CostEstimate(
+            flops=8 * count * dim * dim + 4 * count * dim * tall, bytes_accessed=16 * MIB, transcendentals=0
+        ),
+    )(
+        hidden, hidden_far, out_grad, grad_far, out_grad, grad_far, two, two_far, pre_grad, pre_far, pre_grad, pre_far,
+        pooled, pooled_far, attn_grad, attn_far,
+    )
+
+    query_grad_far = other(query_grad)
+    score_pool_far = other(score_pool)
+    vectors_far = other(vectors)
+    one_far = other(one)
+    query_far = other(query)
+    vector_spec = pl.BlockSpec((8, dim), lambda i: (0, 0))
+    full_line = pl.BlockSpec((1, dim), lambda i: (0, 0))
+    short_line = pl.BlockSpec((1, features), lambda i: (0, 0))
+    short_out = out((1, features), F32)
+    (
+        query_weight_grad, query_bias_grad, key_weight_grad, lat_gain_grad, lat_shift_grad, mlp_gain_grad,
+        mlp_shift_grad, in_gain_grad, in_shift_grad,
+    ) = pl.pallas_call(
+        lambda *refs: last_kernel(features, *refs),
+        grid=(dim // block,),
+        out_shape=(square, line_out, slab_out) + (line_out,) * 4 + (short_out,) * 2,
+        in_specs=(
+            cols, cols, full, full, cols, cols, pool_spec, pool_spec, cols, cols, vector_spec, vector_spec,
+        ),
+        out_specs=(strip, line, slab) + (full_line,) * 4 + (short_line,) * 2,
+        compiler_params=pltpu.CompilerParams(vmem_limit_bytes=32 * MIB),
+        cost_estimate=pl.CostEstimate(
+            flops=4 * count * dim * dim + 4 * count * dim * tall, bytes_accessed=8 * MIB, transcendentals=0
+        ),
+    )(
+        one, one_far, query_grad, query_grad_far, query_grad, query_grad_far, score_pool, score_pool_far, query,
+        query_far, vectors, vectors_far,
+    )
+
+    return (
+        encoded[None], latent_grad[None], color_grad[None], lat_gain_grad[0], lat_shift_grad[0], query_weight_grad,
+        query_bias_grad[0], in_gain_grad[0], in_shift_grad[0], key_weight_grad, value_weight_grad, value_bias_grad[0],
+        mlp_gain_grad[0], mlp_shift_grad[0], up_weight_grad, up_bias_grad[0], down_weight_grad, down_bias_grad[0],
+    )
+
+
+def in_blocks(
     latents,
     pixels,
     coords,
@@ -245,6 +818,13 @@
     )
 
 
+def shards(*args):
+    pixels = args[1]
+    kept = lax.axis_size("pix") * pixels.shape[2] // 2
+    fits = kept <= 4096 and pixels.shape[2] % LANES == 0
+    return (on_chip if fits else in_blocks)(*args)
+
+
 def solution(mesh):
     lat = P("img", None, None)
     whole = P()

time: 121 us -> 79 us (0.65)
  the two profiles are of different devices: /device:TPU:0 before, /device:TPU:31 now
where the time goes in v2:
time: 79 us; the launch traced here: 78.2 us
  Pallas kernels  48.6 us (62%)
  local copies, waits for them, and re-layouts  15.3 us (19%)
  starting transfers between devices  9.38 us (12%)
  waiting for transfers between devices  2.77 us (4%)
  other arithmetic  1.19 us (2%)
  between operations  0.93 us (1%)
    pallas_call x4, Pallas kernels, call(): pl.pallas_call(body, out_shape=outs, in_specs=specs, out_specs=jax.tree.m...  36.9 us
    unnamed x46, local copies, waits for them, and re-layouts  12 us
    pallas_call x1, Pallas kernels, on_chip(): pl.pallas_call(lambda *refs: late_kernel(features, *refs), grid=(dim // b...  6.69 us
    all_to_all x1, starting transfers between devices, on_chip(): segments = lax.all_to_all(packed, 'pix', 0, 0)  6.36 us
    pallas_call x1, Pallas kernels, on_chip(): pl.pallas_call(lambda *refs: last_kernel(features, *refs), grid=(dim // b...  5.07 us
    ppermute x8, starting transfers between devices, other(): return lax.ppermute(value, 'img', swap)  3.03 us
    ppermute x8, waiting for transfers between devices, other(): return lax.ppermute(value, 'img', swap)  2.77 us
    squeeze x1, local copies, waits for them, and re-layouts, on_chip(): packs_far[3]  1.69 us
  transfers between devices with their start and end apart: 9, of which 2 were waited for; matrix products, arithmetic and copies ran while one was open for 6% of the time, Pallas kernels for 29%

profile of v2, /device:TPU:31, one launch (start us, length us, event | category | flops | bytes accessed | tf_op | source)
XLA Modules:
  0.0 78.2 jit_solution(3036199757375937561)
XLA Ops:
  0.7 0.7 copy.42
  1.3 0.7 copy-done.9
  2.0 0.0 copy-start.13
  2.0 0.7 copy-done.13
  2.7 1.0 %shard_map.340 = bf16[16,8,384]{2,1,0:T(8,128)(2,1)} custom-call(f32[3,384]{1,0:T(4,128)S(1)} %bitcast.49, s32[2,384]{1,0:T(2,128)S(1)} %bitcast.55, s32[1,384]{1,0:T(1,128)S(1)} %copy-done.9), custom_call_target="tpu_custom_call" | custom-call | flops 4718592 | bytes 49152 | tf_op jit(solution)/shard_map/pallas_call | solution.py:456
  3.7 6.4 %all-to-all-start = ((bf16[16,8,384]{2,1,0:T(8,128)(2,1)}), bf16[16,8,384]{2,1,0:T(8,128)(2,1)S(1)}, u32[]{:S(2)}, u32[]{:S(2)}) async-start(bf16[16,8,384]{2,1,0:T(8,128)(2,1)} %shard_map.340), calls=%async_computation | async-start | bytes 196608 | tf_op jit(solution)/shard_map/all_to_all | solution.py:494
  10.1 0.7 reshape.71.refs_6_.refs_9_
  10.8 0.7 reshape.72.refs_7_
  11.5 0.0 copy-start
  11.5 1.6 %copy-done = bf16[1024,1024]{1,0:T(8,128)(2,1)S(1)} copy-done((bf16[1024,1024]{1,0:T(8,128)(2,1)S(1)}, bf16[1024,1024]{1,0:T(8,128)(2,1)}, u32[]{:S(2)}) %copy-start) | copy-done | bytes 2097176
  13.0 0.0 copy-start.1
  13.1 1.0 %copy-done.1 = bf16[261,1024]{1,0:T(8,128)(2,1)S(1)} copy-done((bf16[261,1024]{1,0:T(8,128)(2,1)S(1)}, bf16[261,1024]{1,0:T(8,128)(2,1)}, u32[]{:S(2)}) %copy-start.1) | copy-done | bytes 534552
  14.1 0.0 copy-start.2
  14.1 1.6 %copy-done.2 = bf16[1024,1024]{1,0:T(8,128)(2,1)S(1)} copy-done((bf16[1024,1024]{1,0:T(8,128)(2,1)S(1)}, bf16[1024,1024]{1,0:T(8,128)(2,1)}, u32[]{:S(2)}) %copy-start.2) | copy-done | bytes 2097176
  15.7 1.0 %copy-done.3 = bf16[1,256,1024]{2,1,0:T(8,128)(2,1)S(1)} copy-done((bf16[1,256,1024]{2,1,0:T(8,128)(2,1)S(1)}, bf16[1,256,1024]{2,1,0:T(8,128)(2,1)}, u32[]{:S(2)}) %copy-start.3) | copy-done | bytes 524312
  16.7 1.0 %copy-done.5 = bf16[1,256,1024]{2,1,0:T(8,128)(2,1)S(1)} copy-done((bf16[1,256,1024]{2,1,0:T(8,128)(2,1)S(1)}, bf16[1,256,1024]{2,1,0:T(8,128)(2,1)}, u32[]{:S(2)}) %copy-start.5) | copy-done | bytes 524312
  17.8 0.7 copy-done.7
  18.5 0.7 copy-done.11
  19.1 0.7 copy-done.12
  19.8 0.0 copy-start.18
  19.9 0.0 copy-start.19
  19.9 0.0 copy-start.20
  19.9 2.8 %shard_map.341 = (bf16[256,1024]{1,0:T(8,128)(2,1)S(1)}, bf16[256,1024]{1,0:T(8,128)(2,1)}, bf16[256,384]{1,0:T(8,128)(2,1)S(1)}, f32[256,1024]{1,0:T(8,128)S(1)}) custom-call(bf16[256,1024]{1,0:T(8,128)(2,1)S(1)} %bitcast.42, f32[1,1024]{1,0:T(1,128)S(1)} %bitcast.50, f32[1,1024]{1,0:T(1,128)S(1)} %bitcast.53, f32[1,1024]{1,0:T(1,128)S(1)} %bitcast.54, ...), custom_call_target="tpu_custom_call" | custom-call | flops 1275068416 | bytes 8388608 | tf_op jit(solution)/shard_map/pallas_call | solution.py:456
  22.7 0.0 copy-start.14
  22.7 1.0 %copy-done.14 = f32[256,1024]{1,0:T(8,128)} copy-done((f32[256,1024]{1,0:T(8,128)}, f32[256,1024]{1,0:T(8,128)S(1)}, u32[]{:S(2)}) %copy-start.14) | copy-done | bytes 1048600
  23.7 0.0 all-to-all-done.refs_0_
  23.7 0.0 copy-done.4
  23.7 0.0 copy-done.15
  23.7 0.0 copy-done.16
  23.7 0.0 copy-done.17
  23.7 0.0 copy-done.18
  23.7 0.0 copy-done.19
  23.7 0.0 copy-done.20
  23.7 0.0 copy-start.8
  23.8 0.0 copy-start.10
  23.8 18.6 %shard_map.342 = (bf16[256,1024]{1,0:T(8,128)(2,1)}, bf16[4,256,1024]{2,1,0:T(8,128)(2,1)}, f32[256,1024]{1,0:T(8,128)}, bf16[256,384]{1,0:T(8,128)(2,1)S(1)}, b...) custom-call(bf16[16,8,384]{2,1,0:T(8,128)(2,1)S(1)} %all-to-all-done, ...), custom_call_target="tpu_custom_call" | custom-call | flops 3825205248 | bytes 8388608 | tf_op jit(solution)/shard_map/pallas_call | solution.py:456
  42.4 1.3 %collective-permute-start.5 = (bf16[4,256,1024]{2,1,0:T(8,128)(2,1)}, bf16[4,256,1024]{2,1,0:T(8,128)(2,1)}, u32[]{:S(2)}, u32[]{:S(2)}) collective-permute-start(bf16[4,256,1024]{2,1,0:T(8,128)(2,1)} %get-tuple-element.78), channel_id=1, source_target_pairs={{0,16},{16,0},{1,17},{17,1},{2,18},{18,2},{3,19},{19,3},{4,20},{20... | collective-permute-start | bytes 6291464 | tf_op jit(solution)/shard_map/ppermute | solution.py:488
  43.7 0.1 collective-permute-start
  43.8 0.4 collective-permute-start.3
  44.2 0.0 copy-done.8
  44.2 0.0 copy-done.10
  44.2 14.4 %shard_map.343 = (bf16[256,1024]{1,0:T(8,128)(2,1)S(1)}, bf16[256,384]{1,0:T(8,128)(2,1)S(1)}, f32[256,1024]{1,0:T(8,128)}, f32[3,384]{1,0:T(4,128)S(1)}, f32[8,1024]{1,0:T(8,128)S(1)}) custom-call(bf16[16,8,384]{2,1,0:T(8,128)(2,1)S(1)} %all-to-all-done.refs_0_, s32[1,384]{1,0:T(1,128)S(1)} %copy-done.10, ...), custom_call_target="tpu_custom_call" | custom-call | flops 3154116608 | bytes 8388608 | tf_op jit(solution)/shard_map/pallas_call | solution.py:456
  58.6 0.1 collective-permute-start.1
  58.8 0.4 collective-permute-start.4
  59.2 1.4 %collective-permute-done.4.refs_11_ = f32[8,1024]{1,0:T(8,128)S(1)} collective-permute-done((f32[8,1024]{1,0:T(8,128)S(1)}, f32[8,1024]{1,0:T(8,128)S(1)}, u32[]{:S(2)}, u32[]{:S(2)}) %collective-permute-start.4) | collective-permute-done | bytes 32800 | tf_op jit(solution)/shard_map/ppermute | solution.py:488
  60.7 0.1 collective-permute-start.2
  60.8 1.3 %collective-permute-done.2.refs_7_ = bf16[256,384]{1,0:T(8,128)(2,1)S(1)} collective-permute-done((bf16[256,384]{1,0:T(8,128)(2,1)S(1)}, bf16[256,384]{1,0:T(8,128)(2,1)S(1)}, u32[]{:S(2)}, u32[]{:S(2)}) %collective-permute-start.2) | collective-permute-done | bytes 196640 | tf_op jit(solution)/shard_map/ppermute | solution.py:488
  62.1 0.0 copy-done.6
  62.1 0.1 collective-permute-start.6
  62.2 0.0 copy-done.21
  62.3 0.2 slice_bitcast_fusion.4
  62.4 0.6 copy.39
  63.0 0.0 collective-permute-done.refs_1_
  63.0 0.4 collective-permute-start.7
  63.4 0.0 collective-permute-done.3.refs_9_
  63.4 0.0 collective-permute-done.1.refs_3_.refs_5_
  63.4 5.1 %shard_map.344 = (f32[1024,1024]{1,0:T(8,128)}, f32[1,1024]{1,0:T(1,128)}, f32[261,1024]{1,0:T(8,128)}, f32[1,1024]{1,0:T(1,128)}, f32[1,1024]{1,0:T(1,128)}, /*...) custom-call(bf16[256,1024]{1,0:T(8,128)(2,1)S(1)} %get-tuple-element.66.refs_0_, ...), custom_call_target="tpu_custom_call" | custom-call | flops 1476395008 | bytes 8388608 | tf_op jit(solution)/shard_map/pallas_call | solution.py:598
  68.5 0.6 reduce
  69.1 0.6 reduce.1
  69.7 0.0 collective-permute-done.5
  69.7 1.7 %slice_bitcast_fusion = (bf16[256,1024]{1,0:T(8,128)(2,1)S(1)}, bf16[256,1024]{1,0:T(8,128)(2,1)S(1)}, bf16[256,1024]{1,0:T(8,128)(2,1)S(1)}, bf16[256,1024]{1,0:T(8,128)(2,1)S(1)}) fusion(bf16[4,256,1024]{2,1,0:T(8,128)(2,1)} %collective-permute-done.5), kind=kLoop, calls=%fused_computation | loop fusion | bytes 4194304 | tf_op jit(solution)/shard_map/squeeze | solution.py:566
  71.4 0.0 collective-permute-done.7.refs_13_
  71.4 0.0 collective-permute-done.6.refs_3_.refs_5_
  71.4 6.7 %shard_map.345 = (f32[1024,1024]{1,0:T(8,128)}, f32[1,1024]{1,0:T(1,128)}, f32[1024,1024]{1,0:T(8,128)}, f32[1,1024]{1,0:T(1,128)}, f32[261,1024]{1,0:T(8,128)}, /*index=5*/f32[1,1024]{1,0:T(1,128)}) custom-call(bf16[256,1024]{1,0:T(8,128)(2,1)S(1)} %get-tuple-element.113.refs_0_, bf16[256,1024]{1,0:T(8,128)(2,1)S(1)} %get-tuple-element.109.refs_1_, ...), custom_call_target="tpu_custom_call" | custom-call | flops 2550136832 | bytes 16777216 | tf_op jit(solution)/shard_map/pallas_call | solution.py:569
  (12 shorter events, 0.0 us)
Async XLA Ops:
  1.3 0.7 copy-start.9
  2.0 0.7 copy-start.13
  3.7 20.0 %all-to-all-start = ((bf16[16,8,384]{2,1,0:T(8,128)(2,1)}), bf16[16,8,384]{2,1,0:T(8,128)(2,1)S(1)}, u32[]{:S(2)}, u32[]{:S(2)}) async-start(bf16[16,8,384]{2,1,0:T(8,128)(2,1)} %shard_map.340), calls=%async_computation | async-start | bytes 196608 | tf_op jit(solution)/shard_map/all_to_all | solution.py:494
  11.5 1.6 %copy-start = (bf16[1024,1024]{1,0:T(8,128)(2,1)S(1)}, bf16[1024,1024]{1,0:T(8,128)(2,1)}, u32[]{:S(2)}) copy-start(bf16[1024,1024]{1,0:T(8,128)(2,1)} %refs_11_.1) | copy-start | bytes 6291460
  13.0 1.0 %copy-start.1 = (bf16[261,1024]{1,0:T(8,128)(2,1)S(1)}, bf16[261,1024]{1,0:T(8,128)(2,1)}, u32[]{:S(2)}) copy-start(bf16[261,1024]{1,0:T(8,128)(2,1)} %refs_10_.1) | copy-start | bytes 1603588
  14.1 1.6 %copy-start.2 = (bf16[1024,1024]{1,0:T(8,128)(2,1)S(1)}, bf16[1024,1024]{1,0:T(8,128)(2,1)}, u32[]{:S(2)}) copy-start(bf16[1024,1024]{1,0:T(8,128)(2,1)} %refs_14_.1) | copy-start | bytes 6291460
  15.7 1.0 %copy-start.3 = (bf16[1,256,1024]{2,1,0:T(8,128)(2,1)S(1)}, bf16[1,256,1024]{2,1,0:T(8,128)(2,1)}, u32[]{:S(2)}) copy-start(bf16[1,256,1024]{2,1,0:T(8,128)(2,1)} %param.21) | copy-start | bytes 1572868
  16.7 1.0 %copy-start.5 = (bf16[1,256,1024]{2,1,0:T(8,128)(2,1)S(1)}, bf16[1,256,1024]{2,1,0:T(8,128)(2,1)}, u32[]{:S(2)}) copy-start(bf16[1,256,1024]{2,1,0:T(8,128)(2,1)} %param.40) | copy-start | bytes 1572868
  17.8 0.7 copy-start.7
  18.5 0.7 copy-start.11
  19.1 0.7 copy-start.12
  19.8 3.9 %copy-start.4 = (bf16[1,256,1024]{2,1,0:T(8,128)(2,1)S(1)}, bf16[1,256,1024]{2,1,0:T(8,128)(2,1)}, u32[]{:S(2)}) copy-start(bf16[1,256,1024]{2,1,0:T(8,128)(2,1)} %param.21) | copy-start | bytes 1572868
  19.8 3.9 %copy-start.15 = (f32[1024]{0:T(1024)S(1)}, f32[1024]{0:T(1024)}, u32[]{:S(2)}) copy-start(f32[1024]{0:T(1024)} %param.33) | copy-start | bytes 12292
  19.8 3.9 %copy-start.16 = (f32[1024]{0:T(1024)S(1)}, f32[1024]{0:T(1024)}, u32[]{:S(2)}) copy-start(f32[1024]{0:T(1024)} %param.34) | copy-start | bytes 12292
  19.8 3.9 %copy-start.17 = (f32[1024]{0:T(1024)S(1)}, f32[1024]{0:T(1024)}, u32[]{:S(2)}) copy-start(f32[1024]{0:T(1024)} %param.35) | copy-start | bytes 12292
  19.8 3.9 %copy-start.18 = (f32[1024]{0:T(1024)S(1)}, f32[1024]{0:T(1024)}, u32[]{:S(2)}) copy-start(f32[1024]{0:T(1024)} %param.37) | copy-start | bytes 12292
  19.9 3.9 %copy-start.19 = (f32[1024]{0:T(1024)S(1)}, f32[1024]{0:T(1024)}, u32[]{:S(2)}) copy-start(f32[1024]{0:T(1024)} %param.39) | copy-start | bytes 12292
  19.9 3.9 %copy-start.20 = (bf16[128,256]{1,0:T(8,128)(2,1)S(1)}, bf16[128,256]{1,0:T(8,128)(2,1)}, u32[]{:S(2)}) copy-start(bf16[128,256]{1,0:T(8,128)(2,1)} %constant.2.clone.refs_5_) | copy-start | bytes 196612
  22.7 1.0 %copy-start.14 = (f32[256,1024]{1,0:T(8,128)}, f32[256,1024]{1,0:T(8,128)S(1)}, u32[]{:S(2)}) copy-start(f32[256,1024]{1,0:T(8,128)S(1)} %get-tuple-element.54.refs_2_) | copy-start | bytes 3145732
  23.7 20.5 %copy-start.8 = (f32[1024]{0:T(1024)S(1)}, f32[1024]{0:T(1024)}, u32[]{:S(2)}) copy-start(f32[1024]{0:T(1024)} %param.25) | copy-start | bytes 12292
  23.8 20.5 %copy-start.10 = (s32[1,384]{1,0:T(1,128)S(1)}, s32[1,384]{1,0:T(1,128)}, u32[]{:S(2)}) copy-start(s32[1,384]{1,0:T(1,128)} %refs_1_.1) | copy-start | bytes 4612
  42.4 27.3 %collective-permute-start.5 = (bf16[4,256,1024]{2,1,0:T(8,128)(2,1)}, bf16[4,256,1024]{2,1,0:T(8,128)(2,1)}, u32[]{:S(2)}, u32[]{:S(2)}) collective-permute-start(bf16[4,256,1024]{2,1,0:T(8,128)(2,1)} %get-tuple-element.78), channel_id=1, source_target_pairs={{0,16},{16,0},{1,17},{17,1},{2,18},{18,2},{3,19},{19,3},{4,20},{20... | collective-permute-start | bytes 6291464 | tf_op jit(solution)/shard_map/ppermute | solution.py:488
  43.7 19.3 %collective-permute-start = (bf16[256,1024]{1,0:T(8,128)(2,1)S(1)}, bf16[256,1024]{1,0:T(8,128)(2,1)S(1)}, u32[]{:S(2)}, u32[]{:S(2)}) collective-permute-start(bf16[256,1024]{1,0:T(8,128)(2,1)S(1)} %get-tuple-element.66.refs_0_), channel_id=1, source_target_pairs={{0,16},{16,0},{1,17},{17,1},{2,18},{18,2},{3,19},{19,3},{4,20},{20... | collective-permute-start | bytes 1572872 | tf_op jit(solution)/shard_map/ppermute | solution.py:488
  43.8 19.6 %collective-permute-start.3 = (bf16[256,1024]{1,0:T(8,128)(2,1)}, bf16[256,1024]{1,0:T(8,128)(2,1)S(1)}, u32[]{:S(2)}, u32[]{:S(2)}) collective-permute-start(bf16[256,1024]{1,0:T(8,128)(2,1)} %get-tuple-element.69.refs_8_), channel_id=1, source_target_pairs={{0,16},{16,0},{1,17},{17,1},{2,18},{18,2},{3,19},{19,3},{4,20},{20... | collective-permute-start | bytes 1572872 | tf_op jit(solution)/shard_map/ppermute | solution.py:488
  44.2 17.9 %copy-start.6 = (bf16[1,256,1024]{2,1,0:T(8,128)(2,1)S(1)}, bf16[1,256,1024]{2,1,0:T(8,128)(2,1)}, u32[]{:S(2)}) copy-start(bf16[1,256,1024]{2,1,0:T(8,128)(2,1)} %param.40) | copy-start | bytes 1572868
  44.2 18.0 %copy-start.21 = (bf16[4,256,1024]{2,1,0:T(8,128)(2,1)S(1)}, bf16[4,256,1024]{2,1,0:T(8,128)(2,1)}, u32[]{:S(2)}) copy-start(bf16[4,256,1024]{2,1,0:T(8,128)(2,1)} %get-tuple-element.78) | copy-start | bytes 6291460
  58.6 4.8 %collective-permute-start.1 = (bf16[256,1024]{1,0:T(8,128)(2,1)S(1)}, bf16[256,1024]{1,0:T(8,128)(2,1)S(1)}, u32[]{:S(2)}, u32[]{:S(2)}) collective-permute-start(bf16[256,1024]{1,0:T(8,128)(2,1)S(1)} %get-tuple-element.67.refs_2_.refs_4_), channel_id=1, source_target_pairs={{0,16},{16,0},{1,17},{17,1},{2,18},{18,2},{3,19},{19,3},{4,20},{20... | collective-permute-start | bytes 1572872 | tf_op jit(solution)/shard_map/ppermute | solution.py:488
  58.8 1.9 %collective-permute-start.4 = (f32[8,1024]{1,0:T(8,128)S(1)}, f32[8,1024]{1,0:T(8,128)S(1)}, u32[]{:S(2)}, u32[]{:S(2)}) collective-permute-start(f32[8,1024]{1,0:T(8,128)S(1)} %get-tuple-element.70.refs_10_), channel_id=1, source_target_pairs={{0,16},{16,0},{1,17},{17,1},{2,18},{18,2},{3,19},{19,3},{4,20},{20... | collective-permute-start | bytes 98312 | tf_op jit(solution)/shard_map/ppermute | solution.py:488
  60.7 1.4 %collective-permute-start.2 = (bf16[256,384]{1,0:T(8,128)(2,1)S(1)}, bf16[256,384]{1,0:T(8,128)(2,1)S(1)}, u32[]{:S(2)}, u32[]{:S(2)}) collective-permute-start(bf16[256,384]{1,0:T(8,128)(2,1)S(1)} %get-tuple-element.68.refs_6_), channel_id=1, source_target_pairs={{0,16},{16,0},{1,17},{17,1},{2,18},{18,2},{3,19},{19,3},{4,20},{20... | collective-permute-start | bytes 589832 | tf_op jit(solution)/shard_map/ppermute | solution.py:488
  62.1 9.3 %collective-permute-start.6 = (bf16[256,1024]{1,0:T(8,128)(2,1)S(1)}, bf16[256,1024]{1,0:T(8,128)(2,1)}, u32[]{:S(2)}, u32[]{:S(2)}) collective-permute-start(bf16[256,1024]{1,0:T(8,128)(2,1)S(1)} %bitcast.46), channel_id=1, source_target_pairs={{0,16},{16,0},{1,17},{17,1},{2,18},{18,2},{3,19},{19,3},{4,20},{20... | collective-permute-start | bytes 1572872 | tf_op jit(solution)/shard_map/ppermute | solution.py:488
  63.0 8.3 %collective-permute-start.7 = (bf16[256,384]{1,0:T(8,128)(2,1)S(1)}, bf16[256,384]{1,0:T(8,128)(2,1)S(1)}, u32[]{:S(2)}, u32[]{:S(2)}) collective-permute-start(bf16[256,384]{1,0:T(8,128)(2,1)S(1)} %get-tuple-element.79.refs_12_), channel_id=1, source_target_pairs={{0,16},{16,0},{1,17},{17,1},{2,18},{18,2},{3,19},{19,3},{4,20},{20... | collective-permute-start | bytes 589832 | tf_op jit(solution)/shard_map/ppermute | solution.py:488

commit v3 on v2

--- a/solution.py
+++ b/solution.py
@@ -17,7 +17,7 @@
 BF = jnp.bfloat16
 F32 = jnp.float32
 VM = pl.BlockSpec(memory_space=pltpu.VMEM)
-ANY = pl.BlockSpec(memory_space=pl.ANY)
+HBM = pl.BlockSpec(memory_space=pltpu.HBM)
 MIB = 1 << 20
 
 
@@ -113,11 +113,31 @@
     return slot == lax.broadcasted_iota(jnp.int32, shape, 0).astype(F32)
 
 
+class Fetch:
+    def __init__(self, source, target, sem):
+        self.copy = pltpu.make_async_copy(source, target, sem)
+        self.target = target
+        self.waiting = True
+
+    def start(self):
+        self.copy.start()
+
+    def get(self):
+        if self.waiting:
+            self.copy.wait()
+            self.waiting = False
+        return self.target
+
+
+def row_of(fetch):
+    return fetch.get()[...].reshape(1, -1)
+
+
 def pack_kernel(pixels, coords, kept, packed, rows):
     rows[...] = jnp.zeros_like(rows)
-    rows[0:3, :] = pixels[...]
-    rows[3:5, :] = coords[...].astype(F32)
-    kept_row = kept[...].astype(F32)
+    rows[0:3, :] = pixels.get()[:, 0, :]
+    rows[3:5, :] = coords.get()[...].astype(F32)
+    kept_row = kept.get()[...].astype(F32)
     rows[5:6, :] = kept_row
     slots = jnp.where(slot_of(kept_row), 1.0, 0.0).astype(BF)
     squeezed = contract(rows[...].astype(BF), slots, 1, 1).astype(BF)
@@ -133,31 +153,28 @@
 
 
 def query_kernel(
-    features, latent, gain, shift, bias, weight_hbm, key_hbm, grad, down_hbm,
-    one, query, absorbed, hidden_grad, weight, key_raw, key, down, sems,
+    features, latent, gain, shift, bias, weight, key_raw, grad, down,
+    early, absorbed, hidden_grad, key,
 ):
-    copies = [
-        pltpu.make_async_copy(weight_hbm, weight, sems.at[0]),
-        pltpu.make_async_copy(key_hbm, key_raw, sems.at[1]),
-        pltpu.make_async_copy(down_hbm, down, sems.at[2]),
-    ]
-    for copy in copies:
-        copy.start()
+    latent = latent.get()
     count, dim = latent.shape
+    one, query, kept_grad = early.at[:, :dim], early.at[:, dim : 2 * dim], early.at[:, 2 * dim :]
+    gain, shift = row_of(gain), row_of(shift)
     step = 32
     for start in range(0, count, step):
         unit, _ = norm_stats(latent[start : start + step, :].astype(F32), 1)
-        one[start : start + step, :] = (unit * gain[...] + shift[...]).astype(BF)
-    copies[0].wait()
+        one[start : start + step, :] = (unit * gain + shift).astype(BF)
+    bias, weight = row_of(bias), weight.get()
     step = 256
     for start in range(0, dim, step):
         part = jnp.dot(one[...], weight[:, start : start + step], preferred_element_type=F32)
         query[:, start : start + step] = (part + bias[:, start : start + step]).astype(BF)
-    copies[1].wait()
-    pad_rows(key, key_raw)
+    pad_rows(key, key_raw.get())
     lifted = contract(query[...], key[...], 1, 1) * (1.0 / math.sqrt(dim))
     absorbed[...] = waves_first(lifted, features).astype(BF)
-    copies[2].wait()
+    grad = grad.get()
+    kept_grad[...] = grad[...]
+    down = down.get()
     for start in range(0, dim, step):
         hidden_grad[:, start : start + step] = contract(grad[...], down[start : start + step, :], 1, 1)
 
@@ -168,42 +185,34 @@
     return jnp.transpose(waves_first(tall, features))
 
 
+def segment_counts(segments, stop):
+    return [jnp.sum(segments[index][5:6, :].astype(F32)).astype(jnp.int32) for index in range(stop)]
+
+
 def forward_kernel(
     features, step,
     segments, absorbed, hidden_grad, latent, grad, table, in_gain, in_shift,
-    value_hbm, value_bias, gain, shift, up_hbm, up_bias, down_hbm, down_bias,
-    encoded, packs, mixed_grad, pool_out, lift_out, x_out, unit_out, spread_out, weight_out, stats, sums,
-    placed, gains, shifts, top, total, pooled, mixed, mix_unit, mix_spread,
-    value_raw, value, up, down, sems,
+    value_raw, value_bias, gain, shift, up, up_bias, down, down_bias,
+    encoded_out, packs, mixed_grad, lift_out, x_out, unit_out, spread_out, weight_out, stats, sums,
+    placed, gains, shifts, top, total, pooled, mixed, mix_unit, mix_spread, value, encoded, out_sem,
 ):
-    copies = [
-        pltpu.make_async_copy(value_hbm, value_raw, sems.at[0]),
-        pltpu.make_async_copy(up_hbm, up, sems.at[1]),
-        pltpu.make_async_copy(down_hbm, down, sems.at[2]),
-    ]
-    for copy in copies:
-        copy.start()
-    count, dim = latent.shape
     pix, _, own = segments.shape
     kept = x_out.shape[1]
     tall = x_out.shape[0]
-    rows = unit_out.shape[0]
     waves = 4 * BANDS
 
     placed[...] = jnp.zeros_like(placed)
-
-    def place(index, offset):
-        segment = segments[index].astype(F32)
-        wide = jnp.concatenate([segment, jnp.zeros((8, LANES), F32)], axis=1)
+    offset = jnp.int32(0)
+    for index, found in enumerate(segment_counts(segments, pix)):
+        wide = jnp.concatenate([segments[index].astype(F32), jnp.zeros((8, LANES), F32)], axis=1)
         inside = lax.rem(offset, LANES)
         base = pl.multiple_of(jnp.minimum(offset - inside, kept), LANES)
         placed[:, pl.ds(base, own + LANES)] += pltpu.roll(wide, inside, 1)
-        return offset + jnp.sum(segment[5:6, :]).astype(jnp.int32)
-
-    lax.fori_loop(0, pix, place, jnp.int32(0))
-    gains[...] = as_column(in_gain[...], tall, features)
-    shifts[...] = as_column(in_shift[...], tall, features)
+        offset = offset + found
+    gains[...] = as_column(row_of(in_gain), tall, features)
+    shifts[...] = as_column(row_of(in_shift), tall, features)
     top[...] = jnp.full_like(top, FLOOR)
+    table = table.get()
 
     def make(index, carry):
         lanes = pl.ds(pl.multiple_of(index * step, LANES), step)
@@ -268,24 +277,29 @@
     lax.fori_loop(0, kept // step, pool, 0)
     share = 1.0 / jnp.sum(total[...], axis=1, keepdims=True)
     pooled[...] = pooled[...] * share
+    latent, grad = latent.get(), grad.get()
+    count, dim = latent.shape
+    hidden, two, pre_grad, attn_grad = (packs.at[:, at * dim : (at + 1) * dim] for at in range(4))
+    pool_out = packs.at[:, 4 * dim : 4 * dim + tall]
+    packs[:, 4 * dim + tall :] = jnp.zeros((count, packs.shape[1] - 4 * dim - tall), BF)
     pool_out[...] = waves_last(pooled[...], features).astype(BF)
 
-    copies[0].wait()
-    pad_rows(value, value_raw)
+    pad_rows(value, value_raw.get())
+    value_bias = row_of(value_bias)
     wide = 256
     for start in range(0, dim, wide):
         span = slice(start, start + wide)
         attn = jnp.dot(pool_out[...], value[:, span], preferred_element_type=F32) + value_bias[:, span]
         mixed[:, span] = latent[:, span].astype(F32) + attn
     low = 32
-    hidden, two, pre_grad, attn_grad = packs.at[0], packs.at[1], packs.at[2], packs.at[3]
+    gain, shift = row_of(gain), row_of(shift)
     for start in range(0, count, low):
         span = slice(start, start + low)
         unit, spread = norm_stats(mixed[span, :], 1)
         mix_unit[span, :] = unit
         mix_spread[span, :] = jnp.broadcast_to(spread, (low, LANES))
-        two[span, :] = (unit * gain[...] + shift[...]).astype(BF)
-    copies[1].wait()
+        two[span, :] = (unit * gain + shift).astype(BF)
+    up, up_bias = up.get(), row_of(up_bias)
     for start in range(0, dim, wide):
         span = slice(start, start + wide)
         act = jnp.dot(two[...], up[:, span], preferred_element_type=F32) + up_bias[:, span]
@@ -293,11 +307,13 @@
         hidden[:, span] = (act * half).astype(BF)
         slope = half + act * jnp.exp(-0.5 * act * act) * (1.0 / math.sqrt(2.0 * math.pi))
         pre_grad[:, span] = (hidden_grad[:, span] * slope).astype(BF)
-    copies[2].wait()
+    down, down_bias = down.get(), row_of(down_bias)
     for start in range(0, dim, wide):
         span = slice(start, start + wide)
         part = jnp.dot(hidden[...], down[:, span], preferred_element_type=F32)
         encoded[:, span] = (mixed[:, span] + part + down_bias[:, span]).astype(BF)
+    leave = pltpu.make_async_copy(encoded, encoded_out, out_sem)
+    leave.start()
     for start in range(0, dim, wide):
         span = slice(start, start + wide)
         mixed[:, span] = contract(pre_grad[...], up[span, :], 1, 1)
@@ -307,7 +323,7 @@
         span = slice(start, start + low)
         upstream = mixed[span, :]
         unit = mix_unit[span, :]
-        full = grad[span, :].astype(F32) + norm_back(upstream, gain[...], unit, mix_spread[span, :1], 1)
+        full = grad[span, :].astype(F32) + norm_back(upstream, gain, unit, mix_spread[span, :1], 1)
         mixed_grad[span, :] = full
         attn_grad[span, :] = full.astype(BF)
         gain_sum = gain_sum + fold_rows(upstream * unit)
@@ -319,27 +335,24 @@
     delta = jnp.sum(lifted.astype(F32) * pooled[...], axis=1, keepdims=True)
     at = lane_ids(stats.shape)
     stats[...] = jnp.where(at == 0, share, delta)
+    leave.wait()
 
 
 def pull_kernel(
     features, step,
     segments, kept_row, absorbed, lifted, x_in, unit_in, spread_in, weight, stats, in_gain,
-    key_hbm, weight_hbm, latent, gain, mixed_grad, sums,
-    query_grad, pool_out, latent_grad, color_grad, vectors,
-    gains, factors, pooled, gain_sum, shift_sum, colors, back, key_raw, key, query_weight, sems,
+    key_raw, query_weight, latent, gain, mixed_grad, sums,
+    late, vectors, latent_out, color_out,
+    gains, factors, pooled, gain_sum, shift_sum, colors, back, key, latent_grad, color_grad, out_sems,
 ):
-    copies = [
-        pltpu.make_async_copy(key_hbm, key_raw, sems.at[0]),
-        pltpu.make_async_copy(weight_hbm, query_weight, sems.at[1]),
-    ]
-    for copy in copies:
-        copy.start()
-    count, dim = latent.shape
-    own = kept_row.shape[1]
+    count, dim = latent_grad.shape
+    own = segments.shape[2]
     tall, kept = x_in.shape
     rows = unit_in.shape[0]
     waves = 4 * BANDS
-    gains[...] = as_column(in_gain[...], tall, features)
+    query_grad, pool_out = late.at[:, :dim], late.at[:, dim : dim + tall]
+    late[:, dim + tall :] = jnp.zeros((count, late.shape[1] - dim - tall), BF)
+    gains[...] = as_column(row_of(in_gain), tall, features)
     factors[:, :count] = jnp.transpose(absorbed[...].astype(F32))[:rows].astype(BF)
     factors[:, count:] = jnp.transpose(lifted[...].astype(F32))[:rows].astype(BF)
     pooled[...] = jnp.zeros_like(pooled)
@@ -367,39 +380,48 @@
     lax.fori_loop(0, kept // step, pull, 0)
     colors[:, kept:] = jnp.zeros((8, own + LANES), F32)
 
-    def skip(index, offset):
-        return offset + jnp.sum(segments[index][5:6, :].astype(F32)).astype(jnp.int32)
-
-    offset = lax.fori_loop(0, lax.axis_index("pix"), skip, jnp.int32(0))
+    mine = lax.axis_index("pix")
+    offset = jnp.int32(0)
+    for index, found in enumerate(segment_counts(segments, segments.shape[0])):
+        offset = offset + jnp.where(index < mine, found, 0)
     inside = lax.rem(offset, LANES)
     base = pl.multiple_of(jnp.minimum(offset - inside, kept), LANES)
     window = pltpu.roll(colors[:, pl.ds(base, own + LANES)], own + LANES - inside, 1)[:, :own]
-    slots = jnp.where(slot_of(kept_row[...].astype(F32)), 1.0, 0.0)
+    slots = jnp.where(slot_of(kept_row.get()[...].astype(F32)), 1.0, 0.0)
     spread_back = jnp.dot(window, slots, precision=lax.Precision.HIGHEST, preferred_element_type=F32)
-    color_grad[...] = spread_back[:3]
+    color_grad[:, 0, :] = spread_back[:3]
+    leave = [pltpu.make_async_copy(color_grad, color_out, out_sems.at[0])]
+    leave[0].start()
 
     pool_out[...] = waves_last(pooled[...], features).astype(BF)
-    copies[0].wait()
-    pad_rows(key, key_raw)
+    pad_rows(key, key_raw.get())
     wide = 256
     for start in range(0, dim, wide):
         span = slice(start, start + wide)
         part = jnp.dot(pool_out[...], key[:, span], preferred_element_type=F32) * (1.0 / math.sqrt(dim))
         query_grad[:, span] = part.astype(BF)
-    copies[1].wait()
+    query_weight = query_weight.get()
     for start in range(0, dim, wide):
         span = slice(start, start + wide)
         back[:, span] = contract(query_grad[...], query_weight[span, :], 1, 1)
     low = 32
+    gain, latent = row_of(gain), latent.get()
     lat_gain_sum = jnp.zeros((8, dim), F32)
     lat_shift_sum = jnp.zeros((8, dim), F32)
+    parts = 4
     for start in range(0, count, low):
         span = slice(start, start + low)
         unit, spread = norm_stats(latent[span, :].astype(F32), 1)
         upstream = back[span, :]
-        latent_grad[span, :] = mixed_grad[span, :] + norm_back(upstream, gain[...], unit, spread, 1)
+        latent_grad[span, :] = mixed_grad[span, :] + norm_back(upstream, gain, unit, spread, 1)
         lat_gain_sum = lat_gain_sum + fold_rows(upstream * unit)
         lat_shift_sum = lat_shift_sum + fold_rows(upstream)
+        done = start + low
+        if done % (count // parts) == 0:
+            span = slice(done - count // parts, done)
+            at = len(leave)
+            leave.append(pltpu.make_async_copy(latent_grad.at[span, :], latent_out.at[span, :], out_sems.at[at]))
+            leave[-1].start()
     vectors[...] = jnp.zeros_like(vectors)
     vectors[0:1, :] = jnp.sum(lat_gain_sum, axis=0, keepdims=True)
     vectors[1:2, :] = jnp.sum(lat_shift_sum, axis=0, keepdims=True)
@@ -409,6 +431,8 @@
         flat = jnp.concatenate([flat, jnp.zeros((tall - rows, 1), F32)], axis=0)
         turned = jnp.transpose(jnp.broadcast_to(flat, (tall, LANES)))[:8]
         vectors[at : at + 1, :tall] = waves_last(turned, features)[:1]
+    for copy in leave:
+        copy.wait()
 
 
 def outer(left, right, left_other, right_other):
@@ -417,11 +441,11 @@
 
 def column_sum(own, far):
     rows = fold_rows(own[...].astype(F32)) + fold_rows(far[...].astype(F32))
-    return jnp.sum(rows, axis=0, keepdims=True)
+    return jnp.sum(rows, axis=0)
 
 
 def late_kernel(
-    features,
+    features, width,
     hidden, hidden_far, grad, grad_far, grad_cols, grad_cols_far, two, two_far, pre, pre_far, pre_cols, pre_cols_far,
     pool, pool_far, attn, attn_far,
     down_grad, down_bias, up_grad, up_bias, value_grad, value_bias,
@@ -435,33 +459,46 @@
 
 
 def last_kernel(
-    features,
-    one, one_far, back, back_far, back_cols, back_cols_far, pool, pool_far, query, query_far, vectors, vectors_far,
+    features, width,
+    one, one_far, back, back_far, back_cols, back_cols_far, pool, pool_far, query, query_far, vectors, vectors_far, _,
     query_grad, query_bias, key_grad, lat_gain, lat_shift, mlp_gain, mlp_shift, in_gain, in_shift,
 ):
     query_grad[...] = outer(one, back, one_far, back_far)
-    root = 1.0 / math.sqrt(back.shape[1])
-    key_grad[...] = outer(pool, query, pool_far, query_far)[:features] * root
+    key_grad[...] = outer(pool, query, pool_far, query_far)[:features] * (1.0 / math.sqrt(width))
     query_bias[...] = column_sum(back_cols, back_cols_far)
     sums = vectors[...] + vectors_far[...]
-    lat_gain[...] = sums[0:1]
-    lat_shift[...] = sums[1:2]
-    mlp_gain[...] = sums[2:3]
-    mlp_shift[...] = sums[3:4]
-    in_gain[...] = sums[4:5, :features]
-    in_shift[...] = sums[5:6, :features]
-
-
-def call(body, outs, args, specs, scratch, vmem, flops, moved):
+    lat_gain[...] = sums[0]
+    lat_shift[...] = sums[1]
+    mlp_gain[...] = sums[2]
+    mlp_shift[...] = sums[3]
+    in_gain[...] = sums[4, :features]
+    in_shift[...] = sums[5, :features]
+
+
+def call(body, outs, args, fetched, scratch, vmem, flops, moved):
+    places = [at for at in range(len(args)) if at in fetched]
+    buffers = [pltpu.VMEM(args[at].shape, args[at].dtype) for at in places]
+    shapes = tuple(out(shape, dtype) for shape, dtype, _ in outs)
+
+    def whole(*refs):
+        sources, rest = list(refs[: len(args)]), refs[len(args) :]
+        targets, sems, rest = rest[-len(buffers) - 1 : -1], rest[-1], rest[: -len(buffers) - 1]
+        for slot, (at, target) in enumerate(zip(places, targets)):
+            sources[at] = Fetch(sources[at], target, sems.at[slot])
+            sources[at].start()
+        body(*sources, *rest)
+        for at in places:
+            sources[at].get()
+
     return pl.pallas_call(
-        body,
-        out_shape=outs,
-        in_specs=specs,
-        out_specs=jax.tree.map(lambda _: VM, outs),
-        scratch_shapes=scratch,
+        whole,
+        out_shape=shapes if len(shapes) > 1 else shapes[0],
+        in_specs=tuple(HBM if at in fetched else VM for at in range(len(args))),
+        out_specs=tuple(place for _, _, place in outs) if len(outs) > 1 else outs[0][2],
+        scratch_shapes=list(scratch) + buffers + [pltpu.SemaphoreType.DMA((len(places),))],
         compiler_params=pltpu.CompilerParams(vmem_limit_bytes=vmem * MIB),
         cost_estimate=pl.CostEstimate(flops=flops, bytes_accessed=moved, transcendentals=0),
-    )(*args)
+    )(*(pltpu.with_memory_space_constraint(arg, pltpu.HBM) if at in fetched else arg for at, arg in enumerate(args)))
 
 
 def on_chip(
@@ -478,31 +515,23 @@
     rows = padded(features, 8)
     step = 512 if kept % 512 == 0 else LANES
     latent, out_grad = latents[0], cotangent[0]
-
-    def flat(vector):
-        return vector.reshape(1, -1)
-
     swap = [(0, 1), (1, 0)]
 
     def other(value):
         return lax.ppermute(value, "img", swap)
 
     packed = call(
-        pack_kernel, out((pix, 8, own), BF), (pixels[0], coords[0], kept_mask), (VM,) * 3,
-        [pltpu.VMEM((8, own), F32)], 16, 4 * 8 * own * own, 16 * 8 * own,
+        pack_kernel, [((pix, 8, own), BF, VM)], (pixels.transpose(1, 0, 2), coords[0], kept_mask), (0, 1, 2),
+        [pltpu.VMEM((8, own), F32)], 8, 4 * 8 * own * own, 16 * 8 * own,
     )
     segments = lax.all_to_all(packed, "pix", 0, 0)
 
-    grid_matrix = pltpu.VMEM((dim, dim), BF)
-    raw = pltpu.VMEM((features, dim), BF)
     wide = pltpu.VMEM((tall, dim), BF)
-    one, query, absorbed, hidden_grad = call(
+    early, absorbed, hidden_grad = call(
         lambda *refs: query_kernel(features, *refs),
-        (out((count, dim), BF), out((count, dim), BF), out((count, tall), BF), out((count, dim), F32)),
-        (latent, flat(lat_gain), flat(lat_shift), flat(query_bias), query_weight, key_weight, out_grad, down_weight),
-        (VM, VM, VM, VM, ANY, ANY, VM, ANY),
-        [grid_matrix, raw, wide, grid_matrix, pltpu.SemaphoreType.DMA((3,))],
-        32, 4 * count * dim * dim + 2 * count * dim * tall, 8 * MIB,
+        [((count, 3 * dim), BF, VM), ((count, tall), BF, VM), ((count, dim), F32, VM)],
+        (latent, lat_gain, lat_shift, query_bias, query_weight, key_weight, out_grad, down_weight),
+        tuple(range(8)), [wide], 14, 4 * count * dim * dim + 2 * count * dim * tall, 8 * MIB,
     )
 
     table = np.zeros((2 * BANDS, padded(GRID, LANES)), np.float32)
@@ -510,112 +539,114 @@
     column = pltpu.VMEM((tall, LANES), F32)
     narrow = pltpu.VMEM((count, LANES), F32)
     area = pltpu.VMEM((count, dim), F32)
+    spare = 512
     (
-        encoded, packs, mixed_grad, pooled, lifted, x_in, unit_in, spread_in, weight, stats, sums,
+        encoded, packs, mixed_grad, lifted, x_in, unit_in, spread_in, weight, stats, sums,
     ) = call(
         lambda *refs: forward_kernel(features, step, *refs),
+        [
+            ((count, dim), BF, HBM), ((count, 4 * dim + spare), BF, VM), ((count, dim), F32, VM),
+            ((count, tall), BF, VM), ((tall, kept), BF, VM), ((rows, kept), F32, VM), ((8, kept), F32, VM),
+            ((count, kept), F32, VM), ((count, LANES), F32, VM), ((8, dim), F32, VM),
+        ],
         (
-            out((count, dim), BF), out((4, count, dim), BF), out((count, dim), F32), out((count, tall), BF),
-            out((count, tall), BF), out((tall, kept), BF), out((rows, kept), F32), out((8, kept), F32),
-            out((count, kept), F32), out((count, LANES), F32), out((8, dim), F32),
+            segments, absorbed, hidden_grad, latent, out_grad, jnp.asarray(table, BF), in_gain, in_shift,
+            value_weight, value_bias, mlp_gain, mlp_shift, up_weight, up_bias, down_weight, down_bias,
         ),
-        (
-            segments, absorbed, hidden_grad, latent, out_grad, jnp.asarray(table, BF), flat(in_gain), flat(in_shift),
-            value_weight, flat(value_bias), flat(mlp_gain), flat(mlp_shift), up_weight, flat(up_bias), down_weight,
-            flat(down_bias),
-        ),
-        (VM,) * 8 + (ANY, VM, VM, VM, ANY, VM, ANY, VM),
+        tuple(range(3, 16)),
         [
             pltpu.VMEM((8, kept + own + LANES), F32), column, column, narrow, narrow, pltpu.VMEM((count, tall), F32),
-            area, area, narrow, raw, wide, grid_matrix, grid_matrix, pltpu.SemaphoreType.DMA((3,)),
+            area, area, narrow, wide, pltpu.VMEM((count, dim), BF), pltpu.SemaphoreType.DMA(()),
         ],
-        52, 6 * count * dim * dim + 4 * count * dim * tall + 6 * kept * count * tall, 8 * MIB,
-    )
-
-    query_grad, score_pool, latent_grad, color_grad, vectors = call(
+        20, 6 * count * dim * dim + 4 * count * dim * tall + 6 * kept * count * tall, 8 * MIB,
+    )
+
+    late, vectors, latent_grad, color_grad = call(
         lambda *refs: pull_kernel(features, step, *refs),
+        [
+            ((count, dim + spare), BF, VM), ((8, dim), F32, VM), ((count, dim), F32, HBM), ((3, 1, own), F32, HBM),
+        ],
         (
-            out((count, dim), BF), out((count, tall), BF), out((count, dim), F32), out((3, own), F32),
-            out((8, dim), F32),
+            segments, kept_mask, absorbed, lifted, x_in, unit_in, spread_in, weight, stats, in_gain,
+            key_weight, query_weight, latent, lat_gain, mixed_grad, sums,
         ),
-        (
-            segments, kept_mask, absorbed, lifted, x_in, unit_in, spread_in, weight, stats, flat(in_gain),
-            key_weight, query_weight, latent, flat(lat_gain), mixed_grad, sums,
-        ),
-        (VM,) * 10 + (ANY, ANY) + (VM,) * 4,
+        (1, 9, 10, 11, 12, 13),
         [
             column, pltpu.VMEM((rows, 2 * count), BF), pltpu.VMEM((count, tall), F32),
             pltpu.VMEM((rows, LANES), F32), pltpu.VMEM((rows, LANES), F32),
-            pltpu.VMEM((8, kept + own + LANES), F32), area, raw, wide, grid_matrix, pltpu.SemaphoreType.DMA((2,)),
+            pltpu.VMEM((8, kept + own + LANES), F32), area, wide, area, pltpu.VMEM((3, 1, own), F32),
+            pltpu.SemaphoreType.DMA((5,)),
         ],
-        52, 2 * count * dim * dim + 2 * count * dim * tall + 8 * kept * count * tall, 8 * MIB,
+        16, 2 * count * dim * dim + 2 * count * dim * tall + 8 * kept * count * tall, 8 * MIB,
     )
 
     block = 256
-    cols = pl.BlockSpec((count, block), lambda i: (0, i))
-    full = pl.BlockSpec((count, dim), lambda i: (0, 0))
-    pool_spec = pl.BlockSpec((count, tall), lambda i: (0, 0))
+    turns = dim // block
+
+    def cols(at):
+        return pl.BlockSpec((count, block), lambda i: (0, at * turns + i))
+
+    def full(at):
+        return pl.BlockSpec((count, dim), lambda i: (0, at))
+
+    def tail(at):
+        return pl.BlockSpec((count, spare), lambda i: (0, at * dim // spare))
+
     strip = pl.BlockSpec((block, dim), lambda i: (i, 0))
     slab = pl.BlockSpec((features, block), lambda i: (0, i))
-    line = pl.BlockSpec((1, block), lambda i: (0, i))
+    line = pl.BlockSpec((block,), lambda i: (i,))
     square = out((dim, dim), F32)
     slab_out = out((features, dim), F32)
-    line_out = out((1, dim), F32)
-    hidden, two, pre_grad, attn_grad = packs[0], packs[1], packs[2], packs[3]
+    line_out = out((dim,), F32)
+
+    def twice(specs):
+        return tuple(spec for spec in specs for _ in range(2))
+
+    early_far = other(early)
     packs_far = other(packs)
-    hidden_far, two_far, pre_far, attn_far = packs_far[0], packs_far[1], packs_far[2], packs_far[3]
-    grad_far = other(out_grad)
-    pooled_far = other(pooled)
+    late_far = other(late)
+    vectors_far = other(vectors)
     down_weight_grad, down_bias_grad, up_weight_grad, up_bias_grad, value_weight_grad, value_bias_grad = pl.pallas_call(
-        lambda *refs: late_kernel(features, *refs),
-        grid=(dim // block,),
+        lambda *refs: late_kernel(features, dim, *refs),
+        grid=(turns,),
         out_shape=(square, line_out, square, line_out, slab_out, line_out),
-        in_specs=(
-            cols, cols, full, full, cols, cols, cols, cols, full, full, cols, cols, pool_spec, pool_spec, cols, cols,
-        ),
+        in_specs=twice((cols(0), full(2), cols(2), cols(1), full(2), cols(2), tail(4), cols(3))),
         out_specs=(strip, line, strip, line, slab, line),
-        compiler_params=pltpu.CompilerParams(vmem_limit_bytes=40 * MIB),
+        compiler_params=pltpu.CompilerParams(vmem_limit_bytes=30 * MIB),
         cost_estimate=pl.CostEstimate(
             flops=8 * count * dim * dim + 4 * count * dim * tall, bytes_accessed=16 * MIB, transcendentals=0
         ),
     )(
-        hidden, hidden_far, out_grad, grad_far, out_grad, grad_far, two, two_far, pre_grad, pre_far, pre_grad, pre_far,
-        pooled, pooled_far, attn_grad, attn_far,
-    )
-
-    query_grad_far = other(query_grad)
-    score_pool_far = other(score_pool)
-    vectors_far = other(vectors)
-    one_far = other(one)
-    query_far = other(query)
+        packs, packs_far, early, early_far, early, early_far, packs, packs_far, packs, packs_far, packs, packs_far,
+        packs, packs_far, packs, packs_far,
+    )
+
     vector_spec = pl.BlockSpec((8, dim), lambda i: (0, 0))
-    full_line = pl.BlockSpec((1, dim), lambda i: (0, 0))
-    short_line = pl.BlockSpec((1, features), lambda i: (0, 0))
-    short_out = out((1, features), F32)
+    full_line = pl.BlockSpec((dim,), lambda i: (0,))
+    short_line = pl.BlockSpec((features,), lambda i: (0,))
+    short_out = out((features,), F32)
     (
         query_weight_grad, query_bias_grad, key_weight_grad, lat_gain_grad, lat_shift_grad, mlp_gain_grad,
         mlp_shift_grad, in_gain_grad, in_shift_grad,
     ) = pl.pallas_call(
-        lambda *refs: last_kernel(features, *refs),
-        grid=(dim // block,),
+        lambda *refs: last_kernel(features, dim, *refs),
+        grid=(turns,),
         out_shape=(square, line_out, slab_out) + (line_out,) * 4 + (short_out,) * 2,
-        in_specs=(
-            cols, cols, full, full, cols, cols, pool_spec, pool_spec, cols, cols, vector_spec, vector_spec,
-        ),
+        in_specs=twice((cols(0), full(0), cols(0), tail(1), cols(1), vector_spec)) + (HBM,),
         out_specs=(strip, line, slab) + (full_line,) * 4 + (short_line,) * 2,
-        compiler_params=pltpu.CompilerParams(vmem_limit_bytes=32 * MIB),
+        compiler_params=pltpu.CompilerParams(vmem_limit_bytes=20 * MIB),
         cost_estimate=pl.CostEstimate(
             flops=4 * count * dim * dim + 4 * count * dim * tall, bytes_accessed=8 * MIB, transcendentals=0
         ),
     )(
-        one, one_far, query_grad, query_grad_far, query_grad, query_grad_far, score_pool, score_pool_far, query,
-        query_far, vectors, vectors_far,
+        early, early_far, late, late_far, late, late_far, late, late_far, early, early_far, vectors, vectors_far,
+        pltpu.with_memory_space_constraint(value_bias_grad, pltpu.HBM),
     )
 
     return (
-        encoded[None], latent_grad[None], color_grad[None], lat_gain_grad[0], lat_shift_grad[0], query_weight_grad,
-        query_bias_grad[0], in_gain_grad[0], in_shift_grad[0], key_weight_grad, value_weight_grad, value_bias_grad[0],
-        mlp_gain_grad[0], mlp_shift_grad[0], up_weight_grad, up_bias_grad[0], down_weight_grad, down_bias_grad[0],
+        encoded[None], latent_grad[None], color_grad.transpose(1, 0, 2), lat_gain_grad, lat_shift_grad,
+        query_weight_grad, query_bias_grad, in_gain_grad, in_shift_grad, key_weight_grad, value_weight_grad,
+        value_bias_grad, mlp_gain_grad, mlp_shift_grad, up_weight_grad, up_bias_grad, down_weight_grad, down_bias_grad,
     )
 
 

time: 79 us -> 53.3 us (0.67)
  the two profiles are of different devices: /device:TPU:31 before, /device:TPU:0 now
where the time goes in v3:
time: 53.3 us; the launch traced here: 53.1 us
  Pallas kernels  39.1 us (73%)
  starting transfers between devices  9.47 us (18%)
  waiting for transfers between devices  3.74 us (7%)
  between operations  0.71 us (1%)
    pallas_call x4, Pallas kernels, call(): pl.pallas_call(whole, out_shape=shapes if len(shapes) > 1 else shapes[0],...  29 us
    all_to_all x1, starting transfers between devices, on_chip(): segments = lax.all_to_all(packed, 'pix', 0, 0)  8.32 us
    pallas_call x1, Pallas kernels, on_chip(): pl.pallas_call(lambda *refs: late_kernel(features, dim, *refs), grid=(tur...  5.97 us
    pallas_call x1, Pallas kernels, on_chip(): pl.pallas_call(lambda *refs: last_kernel(features, dim, *refs), grid=(tur...  4.21 us
    all_to_all x1, waiting for transfers between devices, on_chip(): segments = lax.all_to_all(packed, 'pix', 0, 0)  3.73 us
    ppermute x4, starting transfers between devices, other(): return lax.ppermute(value, 'img', swap)  1.14 us
  transfers between devices with their start and end apart: 5, of which 1 were waited for; matrix products, arithmetic and copies ran while one was open for 0% of the time, Pallas kernels for 36%

profile of v3, /device:TPU:0, one launch (start us, length us, event | category | flops | bytes accessed | tf_op | source)
XLA Modules:
  0.0 53.1 jit_solution(11379614367196980763)
XLA Ops:
  0.7 1.8 %shard_map.340 = bf16[16,8,384]{2,1,0:T(8,128)(2,1)} custom-call(f32[3,1,384]{2,1,0:T(1,128)} %bitcast.12, s32[2,384]{1,0:T(2,128)} %bitcast.13, s32[1,384]{1,0:T(1,128)} %refs_1_.3), custom_call_target="tpu_custom_call" | custom-call | flops 4718592 | bytes 49152 | tf_op jit(solution)/shard_map/pallas_call | solution.py:493
  2.4 8.3 %all-to-all-start = ((bf16[16,8,384]{2,1,0:T(8,128)(2,1)}), bf16[16,8,384]{2,1,0:T(8,128)(2,1)S(1)}, u32[]{:S(2)}, u32[]{:S(2)}) async-start(bf16[16,8,384]{2,1,0:T(8,128)(2,1)} %shard_map.340), calls=%async_computation | async-start | bytes 196608 | tf_op jit(solution)/shard_map/all_to_all | solution.py:527
  10.8 3.9 %shard_map.341 = (bf16[256,3072]{1,0:T(8,128)(2,1)S(1)}, bf16[256,384]{1,0:T(8,128)(2,1)S(1)}, f32[256,1024]{1,0:T(8,128)S(1)}) custom-call(bf16[256,1024]{1,0:T(8,128)(2,1)} %bitcast.7, f32[1024]{0:T(1024)} %refs_13_.3, f32[1024]{0:T(1024)} %refs_2_.3, f32[1024]{0:T(1024)} %refs_3_.1, bf16[1024,1024]{1,0:T(8,128)(2,1)} %refs_11_.3, ...), custom_call_target="tpu_custom_call" | custom-call | flops 1275068416 | bytes 8388608 | tf_op jit(solution)/shard_map/pallas_call | solution.py:493
  14.7 3.7 %all-to-all-done.refs_0_ = bf16[16,8,384]{2,1,0:T(8,128)(2,1)S(1)} async-done(((bf16[16,8,384]{2,1,0:T(8,128)(2,1)}), bf16[16,8,384]{2,1,0:T(8,128)(2,1)S(1)}, u32[]{:S(2)}, u32[]{:S(2)}) %all-to-all-start) | async-done | bytes 98336 | tf_op jit(solution)/shard_map/all_to_all | solution.py:527
  18.4 14.0 %shard_map.342 = (bf16[256,1024]{1,0:T(8,128)(2,1)}, bf16[256,4608]{1,0:T(8,128)(2,1)S(1)}, f32[256,1024]{1,0:T(8,128)S(1)}, bf16[256,384]{1,0:T(8,128)(2,1)S(1)...) custom-call(bf16[16,8,384]{2,1,0:T(8,128)(2,1)S(1)} %all-to-all-done, ...), custom_call_target="tpu_custom_call" | custom-call | flops 3825205248 | bytes 8388608 | tf_op jit(solution)/shard_map/pallas_call | solution.py:493
  32.4 0.1 collective-permute-start.3
  32.5 0.5 collective-permute-start
  33.0 9.3 %shard_map.343 = (bf16[256,1536]{1,0:T(8,128)(2,1)S(1)}, f32[8,1024]{1,0:T(8,128)S(1)}, f32[256,1024]{1,0:T(8,128)}, f32[3,1,384]{2,1,0:T(1,128)}) custom-call(bf16[16,8,384]{2,1,0:T(8,128)(2,1)S(1)} %all-to-all-done.refs_0_, s32[1,384]{1,0:T(1,128)} %refs_1_.3, bf16[256,384]{1,0:T(8,128)(2,1)S(1)} %get-tuple-element.50.refs_1_.refs_2_, ...), custom_call_target="tpu_custom_call" | custom-call | flops 3154116608 | bytes 8388608 | tf_op jit(solution)/shard_map/pallas_call | solution.py:493
  42.3 0.1 collective-permute-start.1
  42.4 0.4 collective-permute-start.2
  42.9 0.0 collective-permute-done.refs_3_.refs_5_.refs_1_.refs_9_
  42.9 0.0 collective-permute-done.3.refs_1_.refs_7_.refs_9_.refs_11_.refs_13_.refs_15_
  42.9 6.0 %shard_map.344 = (f32[1024,1024]{1,0:T(8,128)}, f32[1024]{0:T(1024)}, f32[1024,1024]{1,0:T(8,128)}, f32[1024]{0:T(1024)}, f32[261,1024]{1,0:T(8,128)}, /*index=5*/f32[1024]{0:T(1024)}) custom-call(bf16[256,4608]{1,0:T(8,128)(2,1)S(1)} %get-tuple-element.66.refs_0_.refs_6_.refs_8_.refs_10_.refs_12_.refs_14_, ...), custom_call_target="tpu_custom_call" | custom-call | flops 2550136832 | bytes 16777216 | tf_op jit(solution)/shard_map/pallas_call | solution.py:609
  48.9 0.0 collective-permute-done.2.refs_11_
  48.9 0.0 collective-permute-done.1.refs_3_.refs_5_.refs_7_
  48.9 4.2 %shard_map.345 = (f32[1024,1024]{1,0:T(8,128)}, f32[1024]{0:T(1024)}, f32[261,1024]{1,0:T(8,128)}, f32[1024]{0:T(1024)}, f32[1024]{0:T(1024)}, /*index=5*/f32[10...) custom-call(bf16[256,3072]{1,0:T(8,128)(2,1)S(1)} %get-tuple-element.63.refs_2_.refs_4_.refs_0_.refs_8_, ...), custom_call_target="tpu_custom_call" | custom-call | flops 1476395008 | bytes 8388608 | tf_op jit(solution)/shard_map/pallas_call | solution.py:631
Async XLA Ops:
  2.4 16.0 %all-to-all-start = ((bf16[16,8,384]{2,1,0:T(8,128)(2,1)}), bf16[16,8,384]{2,1,0:T(8,128)(2,1)S(1)}, u32[]{:S(2)}, u32[]{:S(2)}) async-start(bf16[16,8,384]{2,1,0:T(8,128)(2,1)} %shard_map.340), calls=%async_computation | async-start | bytes 196608 | tf_op jit(solution)/shard_map/all_to_all | solution.py:527
  32.4 10.5 %collective-permute-start.3 = (bf16[256,4608]{1,0:T(8,128)(2,1)S(1)}, bf16[256,4608]{1,0:T(8,128)(2,1)S(1)}, u32[]{:S(2)}, u32[]{:S(2)}) collective-permute-start(bf16[256,4608]{1,0:T(8,128)(2,1)S(1)} %get-tuple-element.66.refs_0_.refs_6_.refs_8_.refs_10_.refs_12_.refs_14_), channel_id=1, source_target_pairs={{0,16},{16,0},{1,17},{17,1},{2,18},{18,2},{3,19},{19,3},{4,20},{20... | collective-permute-start | bytes 7077896 | tf_op jit(solution)/shard_map/ppermute | solution.py:521
  32.5 10.4 %collective-permute-start = (bf16[256,3072]{1,0:T(8,128)(2,1)S(1)}, bf16[256,3072]{1,0:T(8,128)(2,1)S(1)}, u32[]{:S(2)}, u32[]{:S(2)}) collective-permute-start(bf16[256,3072]{1,0:T(8,128)(2,1)S(1)} %get-tuple-element.63.refs_2_.refs_4_.refs_0_.refs_8_), channel_id=1, source_target_pairs={{0,16},{16,0},{1,17},{17,1},{2,18},{18,2},{3,19},{19,3},{4,20},{20... | collective-permute-start | bytes 4718600 | tf_op jit(solution)/shard_map/ppermute | solution.py:521
  42.3 6.6 %collective-permute-start.1 = (bf16[256,1536]{1,0:T(8,128)(2,1)S(1)}, bf16[256,1536]{1,0:T(8,128)(2,1)S(1)}, u32[]{:S(2)}, u32[]{:S(2)}) collective-permute-start(bf16[256,1536]{1,0:T(8,128)(2,1)S(1)} %get-tuple-element.64.refs_2_.refs_4_.refs_6_), channel_id=1, source_target_pairs={{0,16},{16,0},{1,17},{17,1},{2,18},{18,2},{3,19},{19,3},{4,20},{20... | collective-permute-start | bytes 2359304 | tf_op jit(solution)/shard_map/ppermute | solution.py:521
  42.4 6.4 %collective-permute-start.2 = (f32[8,1024]{1,0:T(8,128)S(1)}, f32[8,1024]{1,0:T(8,128)S(1)}, u32[]{:S(2)}, u32[]{:S(2)}) collective-permute-start(f32[8,1024]{1,0:T(8,128)S(1)} %get-tuple-element.65.refs_10_), channel_id=1, source_target_pairs={{0,16},{16,0},{1,17},{17,1},{2,18},{18,2},{3,19},{19,3},{4,20},{20... | collective-permute-start | bytes 98312 | tf_op jit(solution)/shard_map/ppermute | solution.py:521

commit v4 on v3

v4 whole, which is shorter than its diff:
```python
import math

import jax
import jax.numpy as jnp
import numpy as np
from jax import lax
from jax.experimental import pallas as pl
from jax.experimental.pallas import tpu as pltpu
from jax.sharding import PartitionSpec as P

BANDS = 64
GRID = 224
EPSILON = 1e-05
FLOOR = -1e30
BLOCK = 16
LANES = 128
BF = jnp.bfloat16
F32 = jnp.float32
VM = pl.BlockSpec(memory_space=pltpu.VMEM)
HBM = pl.BlockSpec(memory_space=pltpu.HBM)
MIB = 1 << 20
MAKE, MAKEU = 256, 6
POOL, POOLU = 256, 6
PULL, PULLU = 1024, 3
STRIP = 256


def fourier_lookup():
    position = np.arange(GRID, dtype=np.float32) * np.float32(2.0 / (GRID - 1)) - np.float32(1.0)
    frequency = np.float32(1.0) + np.arange(BANDS, dtype=np.float32) * np.float32(
        (GRID / 2.0 - 1.0) / (BANDS - 1)
    )
    phases = position[None, :] * (np.float32(math.pi) * frequency)[:, None]
    waves = np.concatenate([np.sin(phases.astype(np.float64)), np.cos(phases.astype(np.float64))])
    return waves.astype(np.float32)


def split_numpy(values):
    parts = []
    for _ in range(3):
        part = values.astype(BF).astype(np.float64)
        parts.append(part)
        values = values - part
    return parts


def lookup_with_sums():
    waves = fourier_lookup().astype(BF).astype(np.float64)
    sums = split_numpy(waves.sum(axis=0)) + split_numpy((waves * waves).sum(axis=0))
    table = np.zeros((2 * BANDS + 16, GRID))
    table[: 2 * BANDS] = waves
    table[2 * BANDS : 2 * BANDS + 6] = np.stack(sums)
    return table


def split(values):
    parts = []
    for _ in range(3):
        part = values.astype(BF)
        parts.append(part)
        values = values - part.astype(F32)
    return parts


def contract(left, right, left_dim, right_dim):
    return lax.dot_general(
        left, right, (((left_dim,), (right_dim,)), ((), ())), preferred_element_type=F32
    )


def norm_stats(values, axis):
    centre = values - jnp.mean(values, axis=axis, keepdims=True)
    spread = lax.rsqrt(jnp.mean(centre * centre, axis=axis, keepdims=True) + EPSILON)
    return centre * spread, spread


def norm_back(upstream, gain, unit, spread, axis):
    inner = upstream * gain
    return spread * (
        inner
        - jnp.mean(inner, axis=axis, keepdims=True)
        - unit * jnp.mean(inner * unit, axis=axis, keepdims=True)
    )


def out(shape, dtype):
    return jax.ShapeDtypeStruct(shape, dtype)


def padded(rows, step):
    return -(-rows // step) * step


def lane_ids(shape):
    return lax.broadcasted_iota(jnp.int32, shape, len(shape) - 1)


def waves_first(values, features):
    width = values.shape[1]
    lead = features - 4 * BANDS
    at = lane_ids(values.shape)
    waves = pltpu.roll(values, width - lead, 1)
    rest = pltpu.roll(values, 4 * BANDS, 1)
    return jnp.where(at < 4 * BANDS, waves, jnp.where(at < features, rest, 0.0))


def waves_last(values, features):
    width = values.shape[1]
    lead = features - 4 * BANDS
    at = lane_ids(values.shape)
    rest = pltpu.roll(values, width - 4 * BANDS, 1)
    waves = pltpu.roll(values, lead, 1)
    return jnp.where(at < lead, rest, jnp.where(at < features, waves, 0.0))


def fold(values):
    total = values[:, :LANES]
    for start in range(LANES, values.shape[1], LANES):
        total = total + values[:, start : start + LANES]
    return total


def fold_max(values):
    total = values[:, :LANES]
    for start in range(LANES, values.shape[1], LANES):
        total = jnp.maximum(total, values[:, start : start + LANES])
    return total


def fold_rows(values):
    total = values[:8]
    for start in range(8, values.shape[0], 8):
        total = total + values[start : start + 8]
    return total


def slot_of(kept_row):
    own = kept_row.shape[1]
    shape = (own, own)
    upper = lax.broadcasted_iota(jnp.int32, shape, 0) <= lax.broadcasted_iota(jnp.int32, shape, 1)
    tall = jnp.broadcast_to(kept_row, (8, own)).astype(BF)
    rank = jnp.dot(tall, jnp.where(upper, 1.0, 0.0).astype(BF), preferred_element_type=F32)[:1]
    slot = jnp.where(kept_row > 0, rank - 1.0, -1.0)
    return slot == lax.broadcasted_iota(jnp.int32, shape, 0).astype(F32)


class Fetch:
    def __init__(self, source, target, sem):
        self.copy = pltpu.make_async_copy(source, target, sem)
        self.target = target
        self.waiting = True

    def start(self):
        self.copy.start()

    def get(self):
        if self.waiting:
            self.copy.wait()
            self.waiting = False
        return self.target


def row_of(fetch):
    return fetch.get()[...].reshape(1, -1)


def pack_kernel(pixels, coords, kept, packed, rows):
    rows[...] = jnp.zeros_like(rows)
    rows[0:3, :] = pixels.get()[:, 0, :]
    rows[3:5, :] = coords.get()[...].astype(F32)
    kept_row = kept.get()[...].astype(F32)
    rows[5:6, :] = kept_row
    slots = jnp.where(slot_of(kept_row), 1.0, 0.0).astype(BF)
    squeezed = contract(rows[...].astype(BF), slots, 1, 1).astype(BF)
    packed[...] = jnp.broadcast_to(squeezed[None], packed.shape)


def pad_rows(target, source):
    rows = source.shape[0]
    whole = rows // LANES * LANES
    target[:whole, :] = source[:whole, :]
    target[whole:, :] = jnp.zeros_like(target[whole:, :])
    target[whole:rows, :] = source[whole:, :]


def turn_blocks(target, source):
    size = source.shape[0]
    for start in range(0, source.shape[1], size):
        span = slice(start, start + size)
        target[:, span] = jnp.transpose(source[:, span].astype(F32)).astype(BF)


def turn_pool(target, pool):
    count, tall = pool.shape
    turned = jnp.transpose(pool).astype(BF)
    target[...] = jnp.zeros_like(target)
    for at, start in enumerate(range(0, tall, count)):
        height = min(count, tall - start)
        target[:height, at * count : (at + 1) * count] = turned[start : start + height]


def query_kernel(
    features, latent, gain, shift, weight, bias, key_raw, in_gain, grad, down, in_shift,
    value_bias, mlp_gain, mlp_shift, up_bias, down_bias, table,
    early, absorbed, scorer, hidden_grad, table_kept, rows, ends, one, key,
):
    latent = latent.get()
    count, dim = latent.shape
    tall = absorbed.shape[1]
    turned, query, kept_grad = (early.at[:, at * dim : (at + 1) * dim] for at in range(3))
    step = 32
    lat_gain, lat_shift = row_of(gain), row_of(shift)
    for start in range(0, count, step):
        unit, _ = norm_stats(latent[start : start + step, :].astype(F32), 1)
        one[start : start + step, :] = (unit * lat_gain + lat_shift).astype(BF)
    bias, weight = row_of(bias), weight.get()
    step = 256
    for start in range(0, dim, step):
        part = jnp.dot(one[...], weight[:, start : start + step], preferred_element_type=F32)
        query[:, start : start + step] = (part + bias[:, start : start + step]).astype(BF)
    turn_blocks(turned, one)
    pad_rows(key, key_raw.get())
    lifted = contract(query[...], key[...], 1, 1) * (1.0 / math.sqrt(dim))
    lifted = waves_first(lifted, features)
    absorbed[...] = lifted
    gains = gain_row(in_gain, tall, features)
    scorer[...] = (lifted * gains * math.log2(math.e)).astype(BF)
    ends[...] = jnp.zeros_like(ends)
    ends[0:1, :] = gains
    ends[1:2, :] = gain_row(in_shift, tall, features)
    grad = grad.get()
    kept_grad[...] = grad[...]
    table_kept[...] = table.get()[...]
    rows[...] = jnp.zeros_like(rows)
    for at, vector in enumerate((value_bias, mlp_gain, mlp_shift, up_bias, down_bias)):
        rows[at : at + 1, :] = row_of(vector)
    rows[5:6, :] = lat_gain
    down = down.get()
    for start in range(0, dim, step):
        hidden_grad[:, start : start + step] = contract(grad[...], down[start : start + step, :], 1, 1)


def gain_row(fetch, width, features):
    row = row_of(fetch)
    wide = jnp.concatenate([row, jnp.zeros((1, width - features), F32)], axis=1)
    return waves_first(jnp.broadcast_to(wide, (8, width)), features)[:1]


def segment_counts(segments, stop):
    return [jnp.sum(segments[index][5:6, :].astype(F32)).astype(jnp.int32) for index in range(stop)]


def forward_kernel(
    features,
    segments, scorer, hidden_grad, early, table, latent, value_raw, up, down, rows, ends,
    encoded_out, packs, mixed_grad, lift_out, puller, unit_out, spread_out, score_out, pool_unit, stats, sums,
    placed, places, top, pooled, mixed, mix_unit, mix_spread, value, hidden, two, pool_low, encoded, out_sem,
):
    pix, _, own = segments.shape
    tall, kept = unit_out.shape
    waves = 4 * BANDS
    ones = slice(features, waves + 8)

    placed[...] = jnp.zeros_like(placed)
    offset = jnp.int32(0)
    for index, found in enumerate(segment_counts(segments, pix)):
        wide = jnp.concatenate([segments[index].astype(F32), jnp.zeros((8, LANES), F32)], axis=1)
        inside = lax.rem(offset, LANES)
        base = pl.multiple_of(jnp.minimum(offset - inside, kept), LANES)
        placed[:, pl.ds(base, own + LANES)] += pltpu.roll(wide, inside, 1)
        offset = offset + found
    places[...] = lax.broadcasted_iota(jnp.int32, places.shape, 0).astype(F32).astype(BF)
    unit_out[waves + 16 :, :] = jnp.zeros((tall - waves - 16, kept), BF)
    top[...] = jnp.full_like(top, FLOOR)

    step = MAKE

    def make(index, carry):
        lanes = pl.ds(pl.multiple_of(index * step, LANES), step)
        raw = placed[:, lanes]
        column = jnp.concatenate([places[...]] * (step // LANES), axis=1)
        one, none = jnp.ones((), BF), jnp.zeros((), BF)
        row_hot = jnp.where(column == raw[3:4].astype(BF), one, none)
        col_hot = jnp.where(column == raw[4:5].astype(BF), one, none)
        row_waves = jnp.dot(table[...], row_hot, preferred_element_type=F32)
        col_waves = jnp.dot(table[...], col_hot, preferred_element_type=F32)
        at = lax.broadcasted_iota(jnp.int32, raw.shape, 0)
        position = (raw * (2.0 / (GRID - 1)) - 1.0).astype(BF).astype(F32)
        extra = jnp.where(at < 3, raw, jnp.where(at < 5, position, 0.0))
        both = row_waves[2 * BANDS :] + col_waves[2 * BANDS :]
        mean = (
            jnp.sum(both[0:3], axis=0, keepdims=True) + jnp.sum(extra, axis=0, keepdims=True)
        ) * (1.0 / features)
        square = (
            jnp.sum(both[3:6], axis=0, keepdims=True) + jnp.sum(extra * extra, axis=0, keepdims=True)
        ) * (1.0 / features)
        spread = lax.rsqrt(jnp.maximum(square - mean * mean, 0.0) + EPSILON)
        centre = mean * spread
        spread_out[:, lanes] = jnp.broadcast_to(spread, (8, step))
        for piece, start in (
            (row_waves[:BANDS], 0),
            (col_waves[:BANDS], BANDS),
            (row_waves[BANDS : 2 * BANDS], 2 * BANDS),
            (col_waves[BANDS : 2 * BANDS], 3 * BANDS),
        ):
            unit_out[start : start + BANDS, lanes] = (piece * spread - centre).astype(BF)
        tail = jnp.where(at < features - waves, extra * spread - centre, 1.0)
        tail = jnp.concatenate([tail, jnp.zeros((8, step), F32)], axis=0)
        unit_out[waves : waves + 16, lanes] = tail.astype(BF)
        score = jnp.dot(scorer[...], unit_out[:, lanes], preferred_element_type=F32)
        score_out[:, lanes] = score
        top[...] = jnp.maximum(top[...], fold_max(score))
        return carry

    lax.fori_loop(0, kept // step, make, 0, unroll=MAKEU)
    peak = jnp.max(top[...], axis=1, keepdims=True)
    top[...] = jnp.broadcast_to(peak, top.shape)
    pooled[...] = jnp.zeros_like(pooled)

    step = POOL

    def pool(index, carry):
        lanes = pl.ds(pl.multiple_of(index * step, LANES), step)
        weight = jnp.exp2(score_out[:, lanes] - top[:, :1])
        pooled[...] += contract(weight.astype(BF), unit_out[:, lanes], 1, 1)
        return carry

    lax.fori_loop(0, kept // step, pool, 0, unroll=POOLU)
    total = pooled[:, features : features + 1]
    pool_unit[...] = pooled[...] * (1.0 / total)
    latent, value_raw, up, down = latent.get(), value_raw.get(), up.get(), down.get()
    gains, shifts = ends[0:1, :], ends[1:2, :]
    count, dim = mixed.shape
    grad = early.at[:, 2 * dim :]
    value_bias, gain, shift, up_bias, down_bias = (rows[at : at + 1, :] for at in range(5))
    hidden_turned, two_turned, pre_grad, attn_grad = (packs.at[:, at * dim : (at + 1) * dim] for at in range(4))
    pool = waves_last(pool_unit[...] * gains + shifts, features)
    pool_low[...] = pool.astype(BF)
    turn_pool(packs.at[:, 4 * dim :], pool)

    pad_rows(value, value_raw)
    wide = 256
    for start in range(0, dim, wide):
        span = slice(start, start + wide)
        attn = jnp.dot(pool_low[...], value[:, span], preferred_element_type=F32) + value_bias[:, span]
        mixed[:, span] = latent[:, span].astype(F32) + attn
    low = 32
    for start in range(0, count, low):
        span = slice(start, start + low)
        unit, spread = norm_stats(mixed[span, :], 1)
        mix_unit[span, :] = unit
        mix_spread[span, :] = jnp.broadcast_to(spread, (low, LANES))
        two[span, :] = (unit * gain + shift).astype(BF)
    turn_blocks(two_turned, two)
    for start in range(0, dim, wide):
        span = slice(start, start + wide)
        act = jnp.dot(two[...], up[:, span], preferred_element_type=F32) + up_bias[:, span]
        half = 0.5 * (1.0 + lax.erf(act * (1.0 / math.sqrt(2.0))))
        active = act * half
        hidden[:, span] = active.astype(BF)
        hidden_turned[:, span] = jnp.transpose(active).astype(BF)
        slope = half + act * jnp.exp(-0.5 * act * act) * (1.0 / math.sqrt(2.0 * math.pi))
        pre_grad[:, span] = (hidden_grad[:, span] * slope).astype(BF)
    for start in range(0, dim, wide):
        span = slice(start, start + wide)
        part = jnp.dot(hidden[...], down[:, span], preferred_element_type=F32)
        encoded[:, span] = (mixed[:, span] + part + down_bias[:, span]).astype(BF)
    leave = pltpu.make_async_copy(encoded, encoded_out, out_sem)
    leave.start()
    for start in range(0, dim, wide):
        span = slice(start, start + wide)
        mixed[:, span] = contract(pre_grad[...], up[span, :], 1, 1)
    gain_sum = jnp.zeros((8, dim), F32)
    shift_sum = jnp.zeros((8, dim), F32)
    for start in range(0, count, low):
        span = slice(start, start + low)
        upstream = mixed[span, :]
        unit = mix_unit[span, :]
        full = grad[span, :].astype(F32) + norm_back(upstream, gain, unit, mix_spread[span, :1], 1)
        mixed_grad[span, :] = full
        attn_grad[span, :] = full.astype(BF)
        gain_sum = gain_sum + fold_rows(upstream * unit)
        shift_sum = shift_sum + fold_rows(upstream)
    sums[0:1, :] = jnp.sum(gain_sum, axis=0, keepdims=True)
    sums[1:2, :] = jnp.sum(shift_sum, axis=0, keepdims=True)
    lifted = waves_first(contract(attn_grad[...], value[...], 1, 1), features)
    lift_out[...] = lifted
    pulled = (lifted * gains).astype(BF)
    at = lane_ids(pulled.shape)
    inside = jnp.where(at < features, pulled.astype(F32) * pool_unit[...], 0.0)
    delta = jnp.sum(inside, axis=1, keepdims=True)
    for lane, part in enumerate(split(-delta)):
        pulled = jnp.where(at == features + lane, part, pulled)
    puller[...] = pulled
    at = lane_ids(stats.shape)
    stats[...] = jnp.where(at == 0, peak + jnp.log2(total), delta)
    leave.wait()


def pull_kernel(
    features,
    segments, kept_row, absorbed, lifted, puller, unit_in, spread_in, score, pool_unit, stats,
    key_raw, sums, ends, query_weight, latent, rows, mixed_grad,
    late, vectors, color_out, latent_out,
    pooled, key, color_grad, back, latent_grad, out_sems,
):
    count, dim = pooled.shape[0], key.shape[1]
    own = segments.shape[2]
    tall, kept = unit_in.shape
    waves = 4 * BANDS
    pooled[...] = jnp.zeros_like(pooled)

    def shares(lanes):
        inner = jnp.dot(puller[...], unit_in[:, lanes], preferred_element_type=F32)
        prob = jnp.exp2(score[:, lanes] - stats[:, :1])
        return inner, prob, (prob * inner).astype(BF)

    step = PULL

    def pull(index, carry):
        lanes = pl.ds(pl.multiple_of(index * step, LANES), step)
        pooled[...] += contract(shares(lanes)[2], unit_in[:, lanes], 1, 1)
        return carry

    lax.fori_loop(0, kept // step, pull, 0, unroll=PULLU)
    gains, shifts = ends[0:1, :], ends[1:2, :]
    kept_row, key_raw, query_weight, latent = kept_row.get(), key_raw.get(), query_weight.get(), latent.get()

    mine = lax.axis_index("pix")
    offset = jnp.int32(0)
    for index, found in enumerate(segment_counts(segments, segments.shape[0])):
        offset = offset + jnp.where(index < mine, found, 0)
    inside = lax.rem(offset, LANES)
    base = pl.multiple_of(jnp.minimum(offset - inside, kept - own - LANES), LANES)
    inside = offset - base
    lanes = pl.ds(base, own + LANES)
    inner, prob, score_grad = shares(lanes)
    tilt = score_grad.astype(F32) * score[:, lanes] * math.log(2.0) + prob * (inner + stats[:, 1:2])
    tilt = jnp.sum(tilt, axis=0, keepdims=True) * (1.0 / features)
    factors = []
    for held in (absorbed, lifted):
        scaled = held[...] * gains
        at = lane_ids((count, LANES))
        corner = jnp.where(at == 3, jnp.sum(scaled, axis=1, keepdims=True), scaled[:, waves : waves + LANES])
        factors.append(jnp.transpose(corner)[:8].astype(BF))
    both = jnp.concatenate([score_grad, prob.astype(BF)], axis=0)
    terms = jnp.dot(jnp.concatenate(factors, axis=1), both, preferred_element_type=F32)
    unit = unit_in[waves : waves + 16, lanes].astype(F32)[:8]
    colors = spread_in[:, lanes] * (terms - terms[3:4] * (1.0 / features) - unit * tilt)
    window = pltpu.roll(colors, own + LANES - inside, 1)[:, :own]
    slots = jnp.where(slot_of(kept_row[...].astype(F32)), 1.0, 0.0)
    spread_back = jnp.dot(window, slots, precision=lax.Precision.HIGHEST, preferred_element_type=F32)
    color_grad[:, 0, :] = spread_back[:3]

    held = pooled[...]
    total = held[:, features : features + 1]
    pool = waves_last(held * gains + shifts * total, features)
    turn_pool(late.at[:, dim:], pool)
    pool = pool.astype(BF)
    pad_rows(key, key_raw)
    gain_sum = absorbed[...] * held + lifted[...] * pool_unit[...]
    shift_sum = absorbed[...] * total + lifted[...]
    vectors[...] = jnp.zeros_like(vectors)
    for at, found in ((4, gain_sum), (5, shift_sum)):
        flat = jnp.sum(fold_rows(found), axis=0, keepdims=True)
        vectors[at : at + 1, :tall] = waves_last(jnp.broadcast_to(flat, (8, tall)), features)[:1]
    wide = 256
    for start in range(0, dim, wide):
        span = slice(start, start + wide)
        part = jnp.dot(pool, key[:, span], preferred_element_type=F32) * (1.0 / math.sqrt(dim))
        late[:, span] = part.astype(BF)
    vectors[2:4, :] = sums[0:2, :]
    for start in range(0, dim, wide):
        span = slice(start, start + wide)
        back[:, span] = contract(late[:, :dim], query_weight[span, :], 1, 1)
    low = 32
    gain = rows[5:6, :]
    gain_sum = jnp.zeros((8, dim), F32)
    shift_sum = jnp.zeros((8, dim), F32)
    for start in range(0, count, low):
        span = slice(start, start + low)
        unit, spread = norm_stats(latent[span, :].astype(F32), 1)
        upstream = back[span, :]
        latent_grad[span, :] = mixed_grad[span, :] + norm_back(upstream, gain, unit, spread, 1)
        gain_sum = gain_sum + fold_rows(upstream * unit)
        shift_sum = shift_sum + fold_rows(upstream)
    vectors[0:1, :] = jnp.sum(gain_sum, axis=0, keepdims=True)
    vectors[1:2, :] = jnp.sum(shift_sum, axis=0, keepdims=True)
    leave = [
        pltpu.make_async_copy(color_grad, color_out, out_sems.at[0]),
        pltpu.make_async_copy(latent_grad, latent_out, out_sems.at[1]),
    ]
    for copy in leave:
        copy.start()
    for copy in leave:
        copy.wait()


class Leaving:
    def __init__(self, buffers, sems):
        self.buffers, self.sems, self.flying, self.turn = buffers, sems, {}, 0

    def free(self):
        slot = self.turn % self.buffers.shape[0]
        if slot in self.flying:
            self.flying[slot].wait()
        return self.buffers.at[slot]

    def send(self, target):
        slot = self.turn % self.buffers.shape[0]
        self.turn += 1
        self.flying[slot] = pltpu.make_async_copy(self.buffers.at[slot], target, self.sems.at[slot])
        self.flying[slot].start()

    def end(self):
        for copy in self.flying.values():
            copy.wait()


def parts_of(ref, dim):
    squares = ref.shape[1] // dim
    parts = [ref.at[:, at * dim : (at + 1) * dim] for at in range(squares)]
    return parts + ([ref.at[:, squares * dim :]] if ref.shape[1] % dim else [])


def products(leaving, left, left_far, right, right_far, target, bias):
    count = left.shape[0]
    size = leaving.buffers.shape[1]
    for start in range(0, left.shape[1], size):
        buffer = leaving.free()
        at, inner = start // count * count, start % count
        rows, lanes = slice(inner, inner + size), slice(at, at + count)
        strip = jnp.concatenate([left[rows, lanes], left_far[rows, lanes]], axis=1)
        if bias is not None and start == 0:
            strip = jnp.concatenate([strip, jnp.ones((16, 2 * count), BF)], axis=0)
        found = jnp.dot(strip, jnp.concatenate([right[...], right_far[...]], axis=0), preferred_element_type=F32)
        buffer[...] = found[:size]
        if bias is not None and start == 0:
            bias[...] = found[size]
        leaving.send(target.at[start : start + size, :])


def short_product(held, left, left_far, right, right_far, bias, scale):
    features, count = held.shape[0], left.shape[0]
    pieces = []
    for at, start in enumerate(range(0, features, count)):
        height = min(count, padded(features - start, 16))
        lanes = slice(at * count, (at + 1) * count)
        pieces.append(jnp.concatenate([left[:height, lanes], left_far[:height, lanes]], axis=1))
    high = sum(piece.shape[0] for piece in pieces)
    pieces.append(jnp.ones((16, 2 * count), BF))
    both = jnp.concatenate([right[...], right_far[...]], axis=0)
    found = jnp.dot(jnp.concatenate(pieces, axis=0), both, preferred_element_type=F32)
    held[...] = found[:features] if scale is None else found[:features] * scale
    if bias is not None:
        bias[...] = found[high]


def late_kernel(
    features,
    packs, packs_far, early, early_far,
    down_out, down_bias, up_out, up_bias, value_out, value_bias,
    buffers, held, sems, held_sem,
):
    dim = down_out.shape[1]
    hidden, two, pre, attn, pool = parts_of(packs, dim)
    hidden_far, two_far, pre_far, attn_far, pool_far = parts_of(packs_far, dim)
    grad, grad_far = parts_of(early, dim)[2], parts_of(early_far, dim)[2]
    leaving = Leaving(buffers, sems)
    products(leaving, hidden, hidden_far, grad, grad_far, down_out, down_bias)
    short_product(held, pool, pool_far, attn, attn_far, value_bias, None)
    leave = pltpu.make_async_copy(held, value_out, held_sem)
    leave.start()
    products(leaving, two, two_far, pre, pre_far, up_out, up_bias)
    leave.wait()
    leaving.end()


def last_kernel(
    features,
    early, early_far, late, late_far, vectors, vectors_far, _,
    query_out, query_bias, key_out, lat_gain, lat_shift, mlp_gain, mlp_shift, in_gain, in_shift,
    buffers, held, sems, held_sem,
):
    dim = query_out.shape[1]
    one, query, _ = parts_of(early, dim)
    one_far, query_far, _ = parts_of(early_far, dim)
    grad, pool = parts_of(late, dim)
    grad_far, pool_far = parts_of(late_far, dim)
    leaving = Leaving(buffers, sems)
    products(leaving, one, one_far, grad, grad_far, query_out, query_bias)
    short_product(held, pool, pool_far, query, query_far, None, 1.0 / math.sqrt(dim))
    short = pltpu.make_async_copy(held, key_out, held_sem)
    short.start()
    sums = vectors[...] + vectors_far[...]
    lat_gain[...] = sums[0]
    lat_shift[...] = sums[1]
    mlp_gain[...] = sums[2]
    mlp_shift[...] = sums[3]
    in_gain[...] = sums[4, :features]
    in_shift[...] = sums[5, :features]
    leaving.end()
    short.wait()


def call(body, outs, args, fetched, scratch, vmem, flops, moved, unread=()):
    places = [at for at in range(len(args)) if at in fetched]
    buffers = [pltpu.VMEM(args[at].shape, args[at].dtype) for at in places]
    shapes = tuple(out(shape, dtype) for shape, dtype, _ in outs)

    def whole(*refs):
        sources, rest = list(refs[: len(args)]), refs[len(args) :]
        targets = ()
        if places:
            targets, sems, rest = rest[-len(buffers) - 1 : -1], rest[-1], rest[: -len(buffers) - 1]
        for slot, (at, target) in enumerate(zip(places, targets)):
            sources[at] = Fetch(sources[at], target, sems.at[slot])
            sources[at].start()
        body(*sources, *rest)
        for at in places:
            sources[at].get()

    return pl.pallas_call(
        whole,
        out_shape=shapes if len(shapes) > 1 else shapes[0],
        in_specs=tuple(HBM if at in fetched or at in unread else VM for at in range(len(args))),
        out_specs=tuple(place for _, _, place in outs) if len(outs) > 1 else outs[0][2],
        scratch_shapes=list(scratch) + buffers + ([pltpu.SemaphoreType.DMA((len(places),))] if places else []),
        compiler_params=pltpu.CompilerParams(vmem_limit_bytes=vmem * MIB),
        cost_estimate=pl.CostEstimate(flops=flops, bytes_accessed=moved, transcendentals=0),
    )(*(pltpu.with_memory_space_constraint(arg, pltpu.HBM) if at in fetched or at in unread else arg for at, arg in enumerate(args)))


def on_chip(
    latents, pixels, coords, kept_mask, lat_gain, lat_shift, query_weight, query_bias, in_gain, in_shift,
    key_weight, value_weight, value_bias, mlp_gain, mlp_shift, up_weight, up_bias, down_weight, down_bias,
    cotangent,
):
    pix = lax.axis_size("pix")
    own = pixels.shape[2]
    kept = pix * own // 2
    _, count, dim = latents.shape
    features = in_gain.shape[0]
    tall = padded(features, LANES)
    latent, out_grad = latents[0], cotangent[0]
    swap = [(0, 1), (1, 0)]

    def other(value):
        return lax.ppermute(value, "img", swap)

    packed = call(
        pack_kernel, [((pix, 8, own), BF, VM)], (pixels.transpose(1, 0, 2), coords[0], kept_mask), (0, 1, 2),
        [pltpu.VMEM((8, own), F32)], 8, 4 * 8 * own * own, 16 * 8 * own,
    )
    segments = lax.all_to_all(packed, "pix", 0, 0)

    table = jnp.asarray(lookup_with_sums(), BF)
    wide = pltpu.VMEM((tall, dim), BF)
    early, absorbed, scorer, hidden_grad, table_kept, rows, ends = call(
        lambda *refs: query_kernel(features, *refs),
        [
            ((count, 3 * dim), BF, VM), ((count, tall), F32, VM), ((count, tall), BF, VM), ((count, dim), F32, VM),
            (table.shape, BF, VM), ((8, dim), F32, VM), ((8, tall), F32, VM),
        ],
        (
            latent, lat_gain, lat_shift, query_weight, query_bias, key_weight, in_gain, out_grad, down_weight,
            in_shift, value_bias, mlp_gain, mlp_shift, up_bias, down_bias, table,
        ),
        tuple(range(16)), [pltpu.VMEM((count, dim), BF), wide],
        14, 4 * count * dim * dim + 2 * count * dim * tall, 8 * MIB,
    )

    narrow = pltpu.VMEM((count, LANES), F32)
    area = pltpu.VMEM((count, dim), F32)
    low = pltpu.VMEM((count, dim), BF)
    spare = 512
    (
        encoded, packs, mixed_grad, lifted, puller, unit_in, spread_in, score, pool_unit, stats, sums,
    ) = call(
        lambda *refs: forward_kernel(features, *refs),
        [
            ((count, dim), BF, HBM), ((count, 4 * dim + spare), BF, VM), ((count, dim), F32, VM),
            ((count, tall), F32, VM), ((count, tall), BF, VM), ((tall, kept), BF, VM), ((8, kept), F32, VM),
            ((count, kept), F32, VM), ((count, tall), F32, VM), ((count, LANES), F32, VM), ((8, dim), F32, VM),
        ],
        (
            segments, scorer, hidden_grad, early, table_kept, latent, value_weight, up_weight, down_weight, rows, ends,
        ),
        (5, 6, 7, 8),
        [
            pltpu.VMEM((8, kept + own + LANES), F32), pltpu.VMEM((GRID, LANES), BF), narrow,
            pltpu.VMEM((count, tall), F32), area, area, narrow, wide, low, low, pltpu.VMEM((count, tall), BF), low,
            pltpu.SemaphoreType.DMA(()),
        ],
        20, 6 * count * dim * dim + 4 * count * dim * tall + 6 * kept * count * tall, 8 * MIB,
    )

    late, vectors, color_grad, latent_grad = call(
        lambda *refs: pull_kernel(features, *refs),
        [((count, dim + spare), BF, VM), ((8, dim), F32, VM), ((3, 1, own), F32, HBM), ((count, dim), F32, HBM)],
        (
            segments, kept_mask, absorbed, lifted, puller, unit_in, spread_in, score, pool_unit, stats, key_weight,
            sums, ends, query_weight, latent, rows, mixed_grad,
        ),
        (1, 10, 13, 14),
        [
            pltpu.VMEM((count, tall), F32), wide, pltpu.VMEM((3, 1, own), F32), area, area,
            pltpu.SemaphoreType.DMA((2,)),
        ],
        16, 2 * count * dim * dim + 4 * kept * count * tall, 8 * MIB,
    )

    early_far = other(early)
    packs_far = other(packs)
    late_far = other(late)
    vectors_far = other(vectors)
    square = ((dim, dim), F32, HBM)
    slab = ((features, dim), F32, HBM)
    line = ((dim,), F32, VM)
    short = ((features,), F32, VM)
    slots = [
        pltpu.VMEM((4, STRIP, dim), F32), pltpu.VMEM((features, dim), F32),
    ]
    sems = [pltpu.SemaphoreType.DMA((4,)), pltpu.SemaphoreType.DMA(())]
    down_weight_grad, down_bias_grad, up_weight_grad, up_bias_grad, value_weight_grad, value_bias_grad = call(
        lambda *refs: late_kernel(features, *refs),
        [square, line, square, line, slab, line], (packs, packs_far, early, early_far), (),
        slots + sems, 12, 8 * count * dim * dim + 4 * count * dim * tall, 10 * MIB,
    )
    (
        query_weight_grad, query_bias_grad, key_weight_grad, lat_gain_grad, lat_shift_grad, mlp_gain_grad,
        mlp_shift_grad, in_gain_grad, in_shift_grad,
    ) = call(
        lambda *refs: last_kernel(features, *refs),
        [square, line, slab, line, line, line, line, short, short],
        (
            early, early_far, late, late_far, vectors, vectors_far, down_weight_grad,
        ),
        (), slots + sems, 12, 4 * count * dim * dim + 4 * count * dim * tall, 6 * MIB, (6,),
    )

    return (
        encoded[None], latent_grad[None], color_grad.transpose(1, 0, 2), lat_gain_grad, lat_shift_grad,
        query_weight_grad, query_bias_grad, in_gain_grad, in_shift_grad, key_weight_grad, value_weight_grad,
        value_bias_grad, mlp_gain_grad, mlp_shift_grad, up_weight_grad, up_bias_grad, down_weight_grad, down_bias_grad,
    )


def in_blocks(
    latents,
    pixels,
    coords,
    kept_mask,
    lat_gain,
    lat_shift,
    query_weight,
    query_bias,
    in_gain,
    in_shift,
    key_weight,
    value_weight,
    value_bias,
    mlp_gain,
    mlp_shift,
    up_weight,
    up_bias,
    down_weight,
    down_bias,
    cotangent,
):
    pix = lax.axis_size("pix")
    mine = lax.axis_index("pix")
    own = pixels.shape[2]
    packed = jnp.concatenate(
        [
            pixels[0].astype(BF),
            coords[0].astype(BF),
            kept_mask.astype(BF),
            jnp.zeros((2, own), BF),
        ],
        axis=0,
    )
    gathered = lax.all_to_all(jnp.broadcast_to(packed[None], (pix,) + packed.shape), "pix", 0, 0)
    every = gathered.transpose(1, 0, 2).reshape(packed.shape[0], pix * own)
    swap = [(0, 1), (1, 0)]

    def other(value):
        return lax.ppermute(value, "img", swap)

    root = math.sqrt(latents.shape[2])
    latent = latents[0].astype(F32)
    lat_unit, lat_spread = norm_stats(latent, 1)
    norm_one = (lat_unit * lat_gain + lat_shift).astype(BF)
    query = (jnp.dot(norm_one, query_weight, preferred_element_type=F32) + query_bias).astype(BF)
    absorbed = (contract(query, key_weight, 1, 1) * (1.0 / root)).astype(BF)

    waves = jnp.asarray(fourier_lookup(), BF)
    places = jnp.arange(GRID, dtype=F32)[:, None]

    def features(part):
        cells = part[3:5].astype(F32)
        position = (cells * (2.0 / (GRID - 1)) - 1.0).astype(BF)
        row_waves = jnp.dot(waves, (cells[0:1] == places).astype(BF), preferred_element_type=F32).astype(BF)
        col_waves = jnp.dot(waves, (cells[1:2] == places).astype(BF), preferred_element_type=F32).astype(BF)
        table = jnp.concatenate(
            [part[0:3], position, row_waves[:BANDS], col_waves[:BANDS], row_waves[BANDS:], col_waves[BANDS:]],
            axis=0,
        ).astype(F32)
        unit, spread = norm_stats(table, 0)
        x_in = (unit * in_gain[:, None] + in_shift[:, None]).astype(BF)
        score = jnp.dot(absorbed, x_in, preferred_element_type=F32)
        return unit, spread, x_in, jnp.where(part[5:6] > 0, score, FLOOR), part[5:6] > 0

    def pool(part, feats):
        unit, spread, x_in, score, live = feats
        top = jnp.max(score, axis=1, keepdims=True)
        weight = jnp.where(live, jnp.exp(score - top), 0.0)
        return top, jnp.sum(weight, axis=1, keepdims=True), contract(weight.astype(BF), x_in, 1, 1)

    blocks = max(1, pix // BLOCK)
    parts = every.reshape(packed.shape[0], blocks, -1).transpose(1, 0, 2)
    if blocks == 1:
        feats = features(parts[0])
        row_top, row_total, pooled = pool(parts[0], feats)
    else:

        def merge(carry, part):
            top, total, sums = pool(part, features(part))
            new_top = jnp.maximum(carry[0], top)
            old_scale, new_scale = jnp.exp(carry[0] - new_top), jnp.exp(top - new_top)
            return (
                new_top,
                carry[1] * old_scale + total * new_scale,
                carry[2] * old_scale + sums * new_scale,
            ), None

        start = (
            jnp.full((latent.shape[0], 1), FLOOR, F32),
            jnp.zeros((latent.shape[0], 1), F32),
            jnp.zeros((latent.shape[0], in_gain.shape[0]), F32),
        )
        row_top, row_total, pooled = lax.scan(merge, start, parts)[0]
    pooled = pooled / row_total
    pooled_low = pooled.astype(BF)
    attn = jnp.dot(pooled_low, value_weight, preferred_element_type=F32) + value_bias
    mixed = latent + attn
    mix_unit, mix_spread = norm_stats(mixed, 1)
    norm_two = (mix_unit * mlp_gain + mlp_shift).astype(BF)
    pre_act = jnp.dot(norm_two, up_weight, preferred_element_type=F32) + up_bias
    half_erf = 0.5 * (1.0 + lax.erf(pre_act * (1.0 / math.sqrt(2.0))))
    hidden = (pre_act * half_erf).astype(BF)
    encoded = (
        mixed + jnp.dot(hidden, down_weight, preferred_element_type=F32) + down_bias
    ).astype(BF)

    out_grad = cotangent[0]
    out_grad_full = out_grad.astype(F32)
    hidden_grad = contract(out_grad, down_weight, 1, 1)
    slope = half_erf + pre_act * jnp.exp(-0.5 * pre_act * pre_act) * (1.0 / math.sqrt(2.0 * math.pi))
    pre_grad = (hidden_grad * slope).astype(BF)
    norm_two_grad = contract(pre_grad, up_weight, 1, 1)
    mixed_grad = out_grad_full + norm_back(norm_two_grad, mlp_gain, mix_unit, mix_spread, 1)
    attn_grad = mixed_grad.astype(BF)

    lifted = contract(attn_grad, value_weight, 1, 1).astype(BF)
    row_delta = jnp.sum(lifted.astype(F32) * pooled, axis=1, keepdims=True)

    def pull(part, feats):
        unit, spread, x_in, score, live = feats
        prob = jnp.where(live, jnp.exp(score - row_top), 0.0) / row_total
        score_grad = (prob * (jnp.dot(lifted, x_in, preferred_element_type=F32) - row_delta)).astype(BF)
        score_pool = contract(score_grad, x_in, 1, 1)
        x_in_grad = contract(absorbed, score_grad, 0, 0) + contract(lifted, prob.astype(BF), 0, 0)
        gain_part = jnp.sum(x_in_grad * unit, axis=1)
        shift_part = jnp.sum(x_in_grad, axis=1)
        colour_part = norm_back(x_in_grad, in_gain[:, None], unit, spread, 0)[:3]
        return score_pool, gain_part, shift_part, colour_part

    if blocks == 1:
        score_pool, in_gain_grad, in_shift_grad, all_colors = pull(parts[0], feats)
    else:

        def gather_up(carry, part):
            found = pull(part, features(part))
            return tuple(kept + new for kept, new in zip(carry, found[:3])), found[3]

        start = (
            jnp.zeros((latent.shape[0], in_gain.shape[0]), F32),
            jnp.zeros_like(in_gain),
            jnp.zeros_like(in_shift),
        )
        (score_pool, in_gain_grad, in_shift_grad), stacked = lax.scan(gather_up, start, parts)
        all_colors = stacked.transpose(1, 0, 2).reshape(3, -1)
    color_grad = lax.dynamic_slice(all_colors, (0, mine * own), (3, own))
    score_pool_low = score_pool.astype(BF)
    query_grad = (
        jnp.dot(score_pool_low, key_weight, preferred_element_type=F32) * (1.0 / root)
    ).astype(BF)
    norm_one_grad = contract(query_grad, query_weight, 1, 1)
    latent_grad = mixed_grad + norm_back(norm_one_grad, lat_gain, lat_unit, lat_spread, 1)

    def both(value):
        return jnp.concatenate([value, other(value)], axis=0)

    out_both = both(out_grad)
    hidden_both = both(hidden)
    two_both = both(norm_two)
    pre_both = both(pre_grad)
    attn_both = both(attn_grad)
    one_both = both(norm_one)
    query_both = both(query)
    query_grad_both = both(query_grad)
    pool_both = both(pooled_low)
    score_both = both(score_pool_low)
    wide = jnp.stack(
        [
            jnp.sum(norm_one_grad * lat_unit, axis=0),
            jnp.sum(norm_one_grad, axis=0),
            jnp.sum(norm_two_grad * mix_unit, axis=0),
            jnp.sum(norm_two_grad, axis=0),
        ]
    )
    narrow = jnp.stack([in_gain_grad, in_shift_grad])
    wide = wide + other(wide)
    narrow = narrow + other(narrow)
    return (
        encoded[None],
        latent_grad[None],
        color_grad[None],
        wide[0],
        wide[1],
        contract(one_both, query_grad_both, 0, 0),
        jnp.sum(query_grad_both.astype(F32), axis=0),
        narrow[0],
        narrow[1],
        contract(score_both, query_both, 0, 0) * (1.0 / root),
        contract(pool_both, attn_both, 0, 0),
        jnp.sum(attn_both.astype(F32), axis=0),
        wide[2],
        wide[3],
        contract(two_both, pre_both, 0, 0),
        jnp.sum(pre_both.astype(F32), axis=0),
        contract(hidden_both, out_both, 0, 0),
        jnp.sum(out_both.astype(F32), axis=0),
    )


def shards(*args):
    pixels = args[1]
    kept = lax.axis_size("pix") * pixels.shape[2] // 2
    fits = kept <= 4096 and kept % (3 * PULL) == 0 and pixels.shape[2] % LANES == 0
    return (on_chip if fits else in_blocks)(*args)


def solution(mesh):
    lat = P("img", None, None)
    whole = P()
    return jax.shard_map(
        shards,
        mesh=mesh,
        in_specs=(lat, P("img", None, "pix"), P("img", None, "pix"), P("img", "pix"))
        + (whole,) * 15
        + (lat,),
        out_specs=(lat, lat, P("img", None, "pix")) + (whole,) * 15,
        check_vma=False,
    )
```

time: 53.3 us -> 43.3 us (0.81)
  Pallas kernels: 39.1 us -> 29.2 us
    pallas_call x2 -> x0, Pallas kernels: 10.2 us -> none  [the longest x1 5.97 us: on_chip(): pl.pallas_call(lambda *refs: late_kernel(features, dim, *refs), grid=(tur...]
    pallas_call x4 -> x6, Pallas kernels: 29 us -> 29.2 us  [call(): pl.pallas_call(whole, out_shape=shapes if len(shapes) > 1 else shapes[0],...]
  transfers between devices with their start and end apart: 5 -> 5, of which waited for: 1 -> 2; matrix products, arithmetic and copies ran while one was open for 0% -> 0% of each run, Pallas kernels for 36% -> 34%
where the time goes in v4:
time: 43.3 us; the launch traced here: 43.1 us
  Pallas kernels  29.2 us (67%)
  starting transfers between devices  9.47 us (22%)
  waiting for transfers between devices  3.54 us (8%)
  between operations  0.89 us (2%)
    pallas_call x6, Pallas kernels, call(): pl.pallas_call(whole, out_shape=shapes if len(shapes) > 1 else shapes[0],...  29.2 us
    all_to_all x1, starting transfers between devices, on_chip(): segments = lax.all_to_all(packed, 'pix', 0, 0)  8.32 us
    all_to_all x1, waiting for transfers between devices, on_chip(): segments = lax.all_to_all(packed, 'pix', 0, 0)  3.45 us
    ppermute x4, starting transfers between devices, other(): return lax.ppermute(value, 'img', swap)  1.14 us
  transfers between devices with their start and end apart: 5, of which 2 were waited for; matrix products, arithmetic and copies ran while one was open for 0% of the time, Pallas kernels for 34%

profile of v4, /device:TPU:0, one launch (start us, length us, event | category | flops | bytes accessed | tf_op | source)
XLA Modules:
  0.0 43.1 jit_solution(10268835251581274808)
XLA Ops:
  0.7 1.8 %shard_map.340 = bf16[16,8,384]{2,1,0:T(8,128)(2,1)} custom-call(f32[3,1,384]{2,1,0:T(1,128)} %bitcast.11, s32[2,384]{1,0:T(2,128)} %bitcast.12, s32[1,384]{1,0:T(1,128)} %refs_1_.3), custom_call_target="tpu_custom_call" | custom-call | flops 4718592 | bytes 49152 | tf_op jit(solution)/shard_map/pallas_call | solution.py:623
  2.4 8.3 %all-to-all-start = ((bf16[16,8,384]{2,1,0:T(8,128)(2,1)}), bf16[16,8,384]{2,1,0:T(8,128)(2,1)S(1)}, u32[]{:S(2)}, u32[]{:S(2)}) async-start(bf16[16,8,384]{2,1,0:T(8,128)(2,1)} %shard_map.340), calls=%async_computation | async-start | bytes 196608 | tf_op jit(solution)/shard_map/all_to_all | solution.py:655
  10.8 4.2 %shard_map.341 = (bf16[256,3072]{1,0:T(8,128)(2,1)S(1)}, f32[256,384]{1,0:T(8,128)S(1)}, bf16[256,384]{1,0:T(8,128)(2,1)S(1)}, f32[256,1024]{1,0:T(8,128)S(1)}, ...) custom-call(bf16[256,1024]{1,0:T(8,128)(2,1)} %bitcast.7, f32[1024]{0:T(1024)} %refs_1_.2, ...), custom_call_target="tpu_custom_call" | custom-call | flops 1275068416 | bytes 8388608 | tf_op jit(solution)/shard_map/pallas_call | solution.py:623
  15.0 3.5 %all-to-all-done.refs_0_ = bf16[16,8,384]{2,1,0:T(8,128)(2,1)S(1)} async-done(((bf16[16,8,384]{2,1,0:T(8,128)(2,1)}), bf16[16,8,384]{2,1,0:T(8,128)(2,1)S(1)}, u32[]{:S(2)}, u32[]{:S(2)}) %all-to-all-start) | async-done | bytes 98336 | tf_op jit(solution)/shard_map/all_to_all | solution.py:655
  18.4 9.1 %shard_map.342 = (bf16[256,1024]{1,0:T(8,128)(2,1)}, bf16[256,4608]{1,0:T(8,128)(2,1)S(1)}, f32[256,1024]{1,0:T(8,128)S(1)}, f32[256,384]{1,0:T(8,128)S(1)}, bf1...) custom-call(bf16[16,8,384]{2,1,0:T(8,128)(2,1)S(1)} %all-to-all-done, ...), custom_call_target="tpu_custom_call" | custom-call | flops 3825205248 | bytes 8388608 | tf_op jit(solution)/shard_map/pallas_call | solution.py:623
  27.5 0.1 collective-permute-start.3
  27.6 0.5 %collective-permute-start = (bf16[256,3072]{1,0:T(8,128)(2,1)S(1)}, bf16[256,3072]{1,0:T(8,128)(2,1)S(1)}, u32[]{:S(2)}, u32[]{:S(2)}) collective-permute-start(bf16[256,3072]{1,0:T(8,128)(2,1)S(1)} %get-tuple-element.57.refs_3_.refs_2_.refs_0_), channel_id=1, source_target_pairs={{0,16},{16,0},{1,17},{17,1},{2,18},{18,2},{3,19},{19,3},{4,20},{20... | collective-permute-start | bytes 4718600 | tf_op jit(solution)/shard_map/ppermute | solution.py:649
  28.1 5.6 %shard_map.343 = (bf16[256,1536]{1,0:T(8,128)(2,1)S(1)}, f32[8,1024]{1,0:T(8,128)S(1)}, f32[3,1,384]{2,1,0:T(1,128)}, f32[256,1024]{1,0:T(8,128)}) custom-call(bf16[16,8,384]{2,1,0:T(8,128)(2,1)S(1)} %all-to-all-done.refs_0_, s32[1,384]{1,0:T(1,128)} %refs_1_.3, f32[256,384]{1,0:T(8,128)S(1)} %get-tuple-element.62.refs_2_, ...), custom_call_target="tpu_custom_call" | custom-call | flops 1744830464 | bytes 8388608 | tf_op jit(solution)/shard_map/pallas_call | solution.py:623
  33.7 0.1 collective-permute-start.1
  33.9 0.4 %collective-permute-start.2 = (f32[8,1024]{1,0:T(8,128)S(1)}, f32[8,1024]{1,0:T(8,128)S(1)}, u32[]{:S(2)}, u32[]{:S(2)}) collective-permute-start(f32[8,1024]{1,0:T(8,128)S(1)} %get-tuple-element.75.refs_4_), channel_id=1, source_target_pairs={{0,16},{16,0},{1,17},{17,1},{2,18},{18,2},{3,19},{19,3},{4,20},{20... | collective-permute-start | bytes 98312 | tf_op jit(solution)/shard_map/ppermute | solution.py:649
  34.3 0.1 collective-permute-done.refs_3_.refs_1_
  34.4 0.0 collective-permute-done.3.refs_1_
  34.4 5.0 %shard_map.344 = (f32[1024,1024]{1,0:T(8,128)}, f32[1024]{0:T(1024)}, f32[1024,1024]{1,0:T(8,128)}, f32[1024]{0:T(1024)}, f32[261,1024]{1,0:T(8,128)}, /*index=5*/f32[1024]{0:T(1024)}) custom-call(bf16[256,4608]{1,0:T(8,128)(2,1)S(1)} %get-tuple-element.76.refs_0_, bf16[256,4608]{1,0:T(8,128)(2,1)S(1)} %collective-permute-done.3.refs_1_, ...), custom_call_target="tpu_custom_call" | custom-call | flops 2550136832 | bytes 10485760 | tf_op jit(solution)/shard_map/pallas_call | solution.py:623
  39.4 0.0 collective-permute-done.2.refs_5_
  39.4 0.0 collective-permute-done.1.refs_3_
  39.4 3.5 %shard_map.345 = (f32[1024,1024]{1,0:T(8,128)}, f32[1024]{0:T(1024)}, f32[261,1024]{1,0:T(8,128)}, f32[1024]{0:T(1024)}, f32[1024]{0:T(1024)}, /*index=5*/f32[10...) custom-call(bf16[256,3072]{1,0:T(8,128)(2,1)S(1)} %get-tuple-element.57.refs_3_.refs_2_.refs_0_, ...), custom_call_target="tpu_custom_call" | custom-call | flops 1476395008 | bytes 6291456 | tf_op jit(solution)/shard_map/pallas_call | solution.py:623
Async XLA Ops:
  2.4 16.0 %all-to-all-start = ((bf16[16,8,384]{2,1,0:T(8,128)(2,1)}), bf16[16,8,384]{2,1,0:T(8,128)(2,1)S(1)}, u32[]{:S(2)}, u32[]{:S(2)}) async-start(bf16[16,8,384]{2,1,0:T(8,128)(2,1)} %shard_map.340), calls=%async_computation | async-start | bytes 196608 | tf_op jit(solution)/shard_map/all_to_all | solution.py:655
  27.5 6.9 %collective-permute-start.3 = (bf16[256,4608]{1,0:T(8,128)(2,1)S(1)}, bf16[256,4608]{1,0:T(8,128)(2,1)S(1)}, u32[]{:S(2)}, u32[]{:S(2)}) collective-permute-start(bf16[256,4608]{1,0:T(8,128)(2,1)S(1)} %get-tuple-element.76.refs_0_), channel_id=1, source_target_pairs={{0,16},{16,0},{1,17},{17,1},{2,18},{18,2},{3,19},{19,3},{4,20},{20... | collective-permute-start | bytes 7077896 | tf_op jit(solution)/shard_map/ppermute | solution.py:649
  27.6 6.8 %collective-permute-start = (bf16[256,3072]{1,0:T(8,128)(2,1)S(1)}, bf16[256,3072]{1,0:T(8,128)(2,1)S(1)}, u32[]{:S(2)}, u32[]{:S(2)}) collective-permute-start(bf16[256,3072]{1,0:T(8,128)(2,1)S(1)} %get-tuple-element.57.refs_3_.refs_2_.refs_0_), channel_id=1, source_target_pairs={{0,16},{16,0},{1,17},{17,1},{2,18},{18,2},{3,19},{19,3},{4,20},{20... | collective-permute-start | bytes 4718600 | tf_op jit(solution)/shard_map/ppermute | solution.py:649
  33.7 5.7 %collective-permute-start.1 = (bf16[256,1536]{1,0:T(8,128)(2,1)S(1)}, bf16[256,1536]{1,0:T(8,128)(2,1)S(1)}, u32[]{:S(2)}, u32[]{:S(2)}) collective-permute-start(bf16[256,1536]{1,0:T(8,128)(2,1)S(1)} %get-tuple-element.74.refs_2_), channel_id=1, source_target_pairs={{0,16},{16,0},{1,17},{17,1},{2,18},{18,2},{3,19},{19,3},{4,20},{20... | collective-permute-start | bytes 2359304 | tf_op jit(solution)/shard_map/ppermute | solution.py:649
  33.9 5.5 %collective-permute-start.2 = (f32[8,1024]{1,0:T(8,128)S(1)}, f32[8,1024]{1,0:T(8,128)S(1)}, u32[]{:S(2)}, u32[]{:S(2)}) collective-permute-start(f32[8,1024]{1,0:T(8,128)S(1)} %get-tuple-element.75.refs_4_), channel_id=1, source_target_pairs={{0,16},{16,0},{1,17},{17,1},{2,18},{18,2},{3,19},{19,3},{4,20},{20... | collective-permute-start | bytes 98312 | tf_op jit(solution)/shard_map/ppermute | solution.py:649

commit v5 on v4

--- a/solution.py
+++ b/solution.py
@@ -19,9 +19,11 @@
 VM = pl.BlockSpec(memory_space=pltpu.VMEM)
 HBM = pl.BlockSpec(memory_space=pltpu.HBM)
 MIB = 1 << 20
-MAKE, MAKEU = 256, 6
-POOL, POOLU = 256, 6
-PULL, PULLU = 1024, 3
+MAKE = 256
+SCORE = 1024
+POOL = 512
+PULL = 1024
+WIDE = 256
 STRIP = 256
 
 
@@ -201,9 +203,11 @@
 
 def query_kernel(
     features, latent, gain, shift, weight, bias, key_raw, in_gain, grad, down, in_shift,
-    value_bias, mlp_gain, mlp_shift, up_bias, down_bias, table,
-    early, absorbed, scorer, hidden_grad, table_kept, rows, ends, one, key,
+    value_bias, mlp_gain, mlp_shift, up_bias, down_bias, table, up_hbm,
+    early_out, absorbed_out, scorer, hidden_grad, table_kept, rows, ends, up,
+    one, key, early, absorbed, sems,
 ):
+    bring = [pltpu.make_async_copy(up_hbm, up, sems.at[0])]
     latent = latent.get()
     count, dim = latent.shape
     tall = absorbed.shape[1]
@@ -214,6 +218,8 @@
         unit, _ = norm_stats(latent[start : start + step, :].astype(F32), 1)
         one[start : start + step, :] = (unit * lat_gain + lat_shift).astype(BF)
     bias, weight = row_of(bias), weight.get()
+    for copy in bring:
+        copy.start()
     step = 256
     for start in range(0, dim, step):
         part = jnp.dot(one[...], weight[:, start : start + step], preferred_element_type=F32)
@@ -230,6 +236,12 @@
     ends[1:2, :] = gain_row(in_shift, tall, features)
     grad = grad.get()
     kept_grad[...] = grad[...]
+    leave = [
+        pltpu.make_async_copy(early, early_out, sems.at[2]),
+        pltpu.make_async_copy(absorbed, absorbed_out, sems.at[3]),
+    ]
+    for copy in leave:
+        copy.start()
     table_kept[...] = table.get()[...]
     rows[...] = jnp.zeros_like(rows)
     for at, vector in enumerate((value_bias, mlp_gain, mlp_shift, up_bias, down_bias)):
@@ -237,7 +249,10 @@
     rows[5:6, :] = lat_gain
     down = down.get()
     for start in range(0, dim, step):
-        hidden_grad[:, start : start + step] = contract(grad[...], down[start : start + step, :], 1, 1)
+        part = contract(grad[...], down[start : start + step, :], 1, 1)
+        hidden_grad[:, start : start + step] = part.astype(BF)
+    for copy in bring + leave:
+        copy.wait()
 
 
 def gain_row(fetch, width, features):
@@ -252,9 +267,9 @@
 
 def forward_kernel(
     features,
-    segments, scorer, hidden_grad, early, table, latent, value_raw, up, down, rows, ends,
-    encoded_out, packs, mixed_grad, lift_out, puller, unit_out, spread_out, score_out, pool_unit, stats, sums,
-    placed, places, top, pooled, mixed, mix_unit, mix_spread, value, hidden, two, pool_low, encoded, out_sem,
+    segments, scorer, hidden_grad, table, latent, value_raw, up, rows, ends, grad,
+    hidden, mixed, packs, mixed_grad, lift_out, puller, unit_out, spread_out, score_out, pool_unit, stats, sums,
+    placed, places, top, weight, pooled, back, mix_unit, mix_spread, value, two, pool_low,
 ):
     pix, _, own = segments.shape
     tall, kept = unit_out.shape
@@ -273,10 +288,9 @@
     unit_out[waves + 16 :, :] = jnp.zeros((tall - waves - 16, kept), BF)
     top[...] = jnp.full_like(top, FLOOR)
 
-    step = MAKE
-
-    def make(index, carry):
-        lanes = pl.ds(pl.multiple_of(index * step, LANES), step)
+    for start in range(0, kept, MAKE):
+        step = MAKE
+        lanes = slice(start, start + step)
         raw = placed[:, lanes]
         column = jnp.concatenate([places[...]] * (step // LANES), axis=1)
         one, none = jnp.ones((), BF), jnp.zeros((), BF)
@@ -297,49 +311,40 @@
         spread = lax.rsqrt(jnp.maximum(square - mean * mean, 0.0) + EPSILON)
         centre = mean * spread
         spread_out[:, lanes] = jnp.broadcast_to(spread, (8, step))
-        for piece, start in (
+        for piece, low in (
             (row_waves[:BANDS], 0),
             (col_waves[:BANDS], BANDS),
             (row_waves[BANDS : 2 * BANDS], 2 * BANDS),
             (col_waves[BANDS : 2 * BANDS], 3 * BANDS),
         ):
-            unit_out[start : start + BANDS, lanes] = (piece * spread - centre).astype(BF)
+            unit_out[low : low + BANDS, lanes] = (piece * spread - centre).astype(BF)
         tail = jnp.where(at < features - waves, extra * spread - centre, 1.0)
         tail = jnp.concatenate([tail, jnp.zeros((8, step), F32)], axis=0)
         unit_out[waves : waves + 16, lanes] = tail.astype(BF)
+    for start in range(0, kept, SCORE):
+        lanes = slice(start, start + SCORE)
         score = jnp.dot(scorer[...], unit_out[:, lanes], preferred_element_type=F32)
         score_out[:, lanes] = score
         top[...] = jnp.maximum(top[...], fold_max(score))
-        return carry
-
-    lax.fori_loop(0, kept // step, make, 0, unroll=MAKEU)
     peak = jnp.max(top[...], axis=1, keepdims=True)
     top[...] = jnp.broadcast_to(peak, top.shape)
-    pooled[...] = jnp.zeros_like(pooled)
-
-    step = POOL
-
-    def pool(index, carry):
-        lanes = pl.ds(pl.multiple_of(index * step, LANES), step)
-        weight = jnp.exp2(score_out[:, lanes] - top[:, :1])
-        pooled[...] += contract(weight.astype(BF), unit_out[:, lanes], 1, 1)
-        return carry
-
-    lax.fori_loop(0, kept // step, pool, 0, unroll=POOLU)
+    for start in range(0, kept, POOL):
+        lanes = slice(start, start + POOL)
+        weight[:, lanes] = jnp.exp2(score_out[:, lanes] - top[:, :1]).astype(BF)
+    pooled[...] = contract(weight[...], unit_out[...], 1, 1)
     total = pooled[:, features : features + 1]
     pool_unit[...] = pooled[...] * (1.0 / total)
-    latent, value_raw, up, down = latent.get(), value_raw.get(), up.get(), down.get()
     gains, shifts = ends[0:1, :], ends[1:2, :]
     count, dim = mixed.shape
-    grad = early.at[:, 2 * dim :]
-    value_bias, gain, shift, up_bias, down_bias = (rows[at : at + 1, :] for at in range(5))
+    value_bias, gain, shift, up_bias = (rows[at : at + 1, :] for at in range(4))
     hidden_turned, two_turned, pre_grad, attn_grad = (packs.at[:, at * dim : (at + 1) * dim] for at in range(4))
     pool = waves_last(pool_unit[...] * gains + shifts, features)
     pool_low[...] = pool.astype(BF)
     turn_pool(packs.at[:, 4 * dim :], pool)
 
-    pad_rows(value, value_raw)
-    wide = 256
+    latent = latent.get()
+    pad_rows(value, value_raw.get())
+    wide = WIDE
     for start in range(0, dim, wide):
         span = slice(start, start + wide)
         attn = jnp.dot(pool_low[...], value[:, span], preferred_element_type=F32) + value_bias[:, span]
@@ -360,21 +365,16 @@
         hidden[:, span] = active.astype(BF)
         hidden_turned[:, span] = jnp.transpose(active).astype(BF)
         slope = half + act * jnp.exp(-0.5 * act * act) * (1.0 / math.sqrt(2.0 * math.pi))
-        pre_grad[:, span] = (hidden_grad[:, span] * slope).astype(BF)
+        pre_grad[:, span] = (hidden_grad[:, span].astype(F32) * slope).astype(BF)
     for start in range(0, dim, wide):
         span = slice(start, start + wide)
-        part = jnp.dot(hidden[...], down[:, span], preferred_element_type=F32)
-        encoded[:, span] = (mixed[:, span] + part + down_bias[:, span]).astype(BF)
-    leave = pltpu.make_async_copy(encoded, encoded_out, out_sem)
-    leave.start()
-    for start in range(0, dim, wide):
-        span = slice(start, start + wide)
-        mixed[:, span] = contract(pre_grad[...], up[span, :], 1, 1)
+        back[:, span] = contract(pre_grad[...], up[span, :], 1, 1)
+    grad = grad.get()
     gain_sum = jnp.zeros((8, dim), F32)
     shift_sum = jnp.zeros((8, dim), F32)
     for start in range(0, count, low):
         span = slice(start, start + low)
-        upstream = mixed[span, :]
+        upstream = back[span, :]
         unit = mix_unit[span, :]
         full = grad[span, :].astype(F32) + norm_back(upstream, gain, unit, mix_spread[span, :1], 1)
         mixed_grad[span, :] = full
@@ -394,37 +394,56 @@
     puller[...] = pulled
     at = lane_ids(stats.shape)
     stats[...] = jnp.where(at == 0, peak + jnp.log2(total), delta)
-    leave.wait()
+
+
+def write_vectors(array, lines, vectors):
+    width = array.shape[0]
+    lines[...] = jnp.zeros_like(lines)
+    row = 0
+    for vector in vectors:
+        for part in split(vector):
+            for start in range(0, vector.shape[1], width):
+                lines[row : row + 1, :] = part[:, start : start + width].astype(F32)
+                row += 1
+    array[LANES : LANES + lines.shape[0], array.shape[1] - width :] = lines[...].astype(BF)
+
+
+def read_vectors(array, dim, number):
+    width = array.shape[0]
+    turns = dim // width
+    high = padded(3 * number * turns, 16)
+    lines = array[LANES : LANES + high, array.shape[1] - width :].astype(F32)
+    vectors = []
+    for at in range(number):
+        first = 3 * at * turns
+        total = sum(lines[first + part * turns : first + (part + 1) * turns] for part in range(3))
+        vectors.append(jnp.concatenate([total[turn : turn + 1] for turn in range(turns)], axis=1))
+    return vectors
 
 
 def pull_kernel(
     features,
     segments, kept_row, absorbed, lifted, puller, unit_in, spread_in, score, pool_unit, stats,
     key_raw, sums, ends, query_weight, latent, rows, mixed_grad,
-    late, vectors, color_out, latent_out,
-    pooled, key, color_grad, back, latent_grad, out_sems,
+    late, color_out, latent_out,
+    pulls, pooled, key, color_grad, back, latent_grad, lines, out_sems,
 ):
     count, dim = pooled.shape[0], key.shape[1]
     own = segments.shape[2]
     tall, kept = unit_in.shape
     waves = 4 * BANDS
-    pooled[...] = jnp.zeros_like(pooled)
-
     def shares(lanes):
         inner = jnp.dot(puller[...], unit_in[:, lanes], preferred_element_type=F32)
         prob = jnp.exp2(score[:, lanes] - stats[:, :1])
         return inner, prob, (prob * inner).astype(BF)
 
-    step = PULL
-
-    def pull(index, carry):
-        lanes = pl.ds(pl.multiple_of(index * step, LANES), step)
-        pooled[...] += contract(shares(lanes)[2], unit_in[:, lanes], 1, 1)
-        return carry
-
-    lax.fori_loop(0, kept // step, pull, 0, unroll=PULLU)
+    for start in range(0, kept, PULL):
+        lanes = slice(start, start + PULL)
+        pulls[:, lanes] = shares(lanes)[2]
+    pooled[...] = contract(pulls[...], unit_in[...], 1, 1)
     gains, shifts = ends[0:1, :], ends[1:2, :]
-    kept_row, key_raw, query_weight, latent = kept_row.get(), key_raw.get(), query_weight.get(), latent.get()
+    kept_row, key_raw, query_weight = kept_row.get(), key_raw.get(), query_weight.get()
+    latent, absorbed = latent.get(), absorbed.get()
 
     mine = lax.axis_index("pix")
     offset = jnp.int32(0)
@@ -460,16 +479,17 @@
     pad_rows(key, key_raw)
     gain_sum = absorbed[...] * held + lifted[...] * pool_unit[...]
     shift_sum = absorbed[...] * total + lifted[...]
-    vectors[...] = jnp.zeros_like(vectors)
-    for at, found in ((4, gain_sum), (5, shift_sum)):
+    vectors = []
+    for found in (gain_sum, shift_sum):
         flat = jnp.sum(fold_rows(found), axis=0, keepdims=True)
-        vectors[at : at + 1, :tall] = waves_last(jnp.broadcast_to(flat, (8, tall)), features)[:1]
-    wide = 256
+        flat = waves_last(jnp.broadcast_to(flat, (8, tall)), features)[:1]
+        vectors.append(jnp.concatenate([flat, jnp.zeros((1, dim - tall), F32)], axis=1))
+    vectors += [sums[0:1, :], sums[1:2, :]]
+    wide = WIDE
     for start in range(0, dim, wide):
         span = slice(start, start + wide)
         part = jnp.dot(pool, key[:, span], preferred_element_type=F32) * (1.0 / math.sqrt(dim))
         late[:, span] = part.astype(BF)
-    vectors[2:4, :] = sums[0:2, :]
     for start in range(0, dim, wide):
         span = slice(start, start + wide)
         back[:, span] = contract(late[:, :dim], query_weight[span, :], 1, 1)
@@ -484,8 +504,8 @@
         latent_grad[span, :] = mixed_grad[span, :] + norm_back(upstream, gain, unit, spread, 1)
         gain_sum = gain_sum + fold_rows(upstream * unit)
         shift_sum = shift_sum + fold_rows(upstream)
-    vectors[0:1, :] = jnp.sum(gain_sum, axis=0, keepdims=True)
-    vectors[1:2, :] = jnp.sum(shift_sum, axis=0, keepdims=True)
+    vectors += [jnp.sum(gain_sum, axis=0, keepdims=True), jnp.sum(shift_sum, axis=0, keepdims=True)]
+    write_vectors(late, lines, vectors)
     leave = [
         pltpu.make_async_copy(color_grad, color_out, out_sems.at[0]),
         pltpu.make_async_copy(latent_grad, latent_out, out_sems.at[1]),
@@ -578,9 +598,9 @@
 
 def last_kernel(
     features,
-    early, early_far, late, late_far, vectors, vectors_far, _,
-    query_out, query_bias, key_out, lat_gain, lat_shift, mlp_gain, mlp_shift, in_gain, in_shift,
-    buffers, held, sems, held_sem,
+    early, early_far, late, late_far, hidden, mixed, down, rows, _,
+    encoded_out, query_out, query_bias, key_out, lat_gain, lat_shift, mlp_gain, mlp_shift, in_gain, in_shift,
+    buffers, held, encoded, sems, held_sem, encoded_sem,
 ):
     dim = query_out.shape[1]
     one, query, _ = parts_of(early, dim)
@@ -592,21 +612,25 @@
     short_product(held, pool, pool_far, query, query_far, None, 1.0 / math.sqrt(dim))
     short = pltpu.make_async_copy(held, key_out, held_sem)
     short.start()
-    sums = vectors[...] + vectors_far[...]
-    lat_gain[...] = sums[0]
-    lat_shift[...] = sums[1]
-    mlp_gain[...] = sums[2]
-    mlp_shift[...] = sums[3]
-    in_gain[...] = sums[4, :features]
-    in_shift[...] = sums[5, :features]
+    for start in range(0, dim, WIDE):
+        span = slice(start, start + WIDE)
+        part = jnp.dot(hidden[...], down[:, span], preferred_element_type=F32)
+        encoded[:, span] = (mixed[:, span] + part + rows[4:5, span]).astype(BF)
+    leave = pltpu.make_async_copy(encoded, encoded_out, encoded_sem)
+    leave.start()
+    pairs = zip(read_vectors(late, dim, 6), read_vectors(late_far, dim, 6))
+    places = (in_gain, in_shift, mlp_gain, mlp_shift, lat_gain, lat_shift)
+    for place, (own, far) in zip(places, pairs):
+        place[...] = (own + far)[0, : place.shape[0]]
     leaving.end()
     short.wait()
+    leave.wait()
 
 
 def call(body, outs, args, fetched, scratch, vmem, flops, moved, unread=()):
     places = [at for at in range(len(args)) if at in fetched]
     buffers = [pltpu.VMEM(args[at].shape, args[at].dtype) for at in places]
-    shapes = tuple(out(shape, dtype) for shape, dtype, _ in outs)
+    shapes = tuple(pltpu.HBM(shape, dtype) if place is HBM else out(shape, dtype) for shape, dtype, place in outs)
 
     def whole(*refs):
         sources, rest = list(refs[: len(args)]), refs[len(args) :]
@@ -656,18 +680,22 @@
 
     table = jnp.asarray(lookup_with_sums(), BF)
     wide = pltpu.VMEM((tall, dim), BF)
-    early, absorbed, scorer, hidden_grad, table_kept, rows, ends = call(
+    early, absorbed, scorer, hidden_grad, table_kept, rows, ends, up_kept = call(
         lambda *refs: query_kernel(features, *refs),
         [
-            ((count, 3 * dim), BF, VM), ((count, tall), F32, VM), ((count, tall), BF, VM), ((count, dim), F32, VM),
-            (table.shape, BF, VM), ((8, dim), F32, VM), ((8, tall), F32, VM),
+            ((count, 3 * dim), BF, HBM), ((count, tall), F32, HBM), ((count, tall), BF, VM), ((count, dim), BF, VM),
+            (table.shape, BF, VM), ((8, dim), F32, VM), ((8, tall), F32, VM), ((dim, dim), BF, VM),
         ],
         (
             latent, lat_gain, lat_shift, query_weight, query_bias, key_weight, in_gain, out_grad, down_weight,
-            in_shift, value_bias, mlp_gain, mlp_shift, up_bias, down_bias, table,
+            in_shift, value_bias, mlp_gain, mlp_shift, up_bias, down_bias, table, up_weight,
         ),
-        tuple(range(16)), [pltpu.VMEM((count, dim), BF), wide],
-        14, 4 * count * dim * dim + 2 * count * dim * tall, 8 * MIB,
+        tuple(range(16)),
+        [
+            pltpu.VMEM((count, dim), BF), wide, pltpu.VMEM((count, 3 * dim), BF), pltpu.VMEM((count, tall), F32),
+            pltpu.SemaphoreType.DMA((4,)),
+        ],
+        16, 4 * count * dim * dim + 2 * count * dim * tall, 8 * MIB, (16,),
     )
 
     narrow = pltpu.VMEM((count, LANES), F32)
@@ -675,37 +703,40 @@
     low = pltpu.VMEM((count, dim), BF)
     spare = 512
     (
-        encoded, packs, mixed_grad, lifted, puller, unit_in, spread_in, score, pool_unit, stats, sums,
+        hidden, mixed, packs, mixed_grad, lifted, puller, unit_in, spread_in, score, pool_unit, stats, sums,
     ) = call(
         lambda *refs: forward_kernel(features, *refs),
         [
-            ((count, dim), BF, HBM), ((count, 4 * dim + spare), BF, VM), ((count, dim), F32, VM),
+            ((count, dim), BF, VM), ((count, dim), F32, VM), ((count, 4 * dim + spare), BF, VM),
+            ((count, dim), F32, VM),
             ((count, tall), F32, VM), ((count, tall), BF, VM), ((tall, kept), BF, VM), ((8, kept), F32, VM),
             ((count, kept), F32, VM), ((count, tall), F32, VM), ((count, LANES), F32, VM), ((8, dim), F32, VM),
         ],
         (
-            segments, scorer, hidden_grad, early, table_kept, latent, value_weight, up_weight, down_weight, rows, ends,
+            segments, scorer, hidden_grad, table_kept, latent, value_weight, up_kept, rows, ends, out_grad,
         ),
-        (5, 6, 7, 8),
+        (4, 5, 9),
         [
             pltpu.VMEM((8, kept + own + LANES), F32), pltpu.VMEM((GRID, LANES), BF), narrow,
-            pltpu.VMEM((count, tall), F32), area, area, narrow, wide, low, low, pltpu.VMEM((count, tall), BF), low,
-            pltpu.SemaphoreType.DMA(()),
+            pltpu.VMEM((count, kept), BF), pltpu.VMEM((count, tall), F32), area, area, narrow, wide, low,
+            pltpu.VMEM((count, tall), BF),
         ],
         20, 6 * count * dim * dim + 4 * count * dim * tall + 6 * kept * count * tall, 8 * MIB,
     )
 
-    late, vectors, color_grad, latent_grad = call(
+    late, color_grad, latent_grad = call(
         lambda *refs: pull_kernel(features, *refs),
-        [((count, dim + spare), BF, VM), ((8, dim), F32, VM), ((3, 1, own), F32, HBM), ((count, dim), F32, HBM)],
+        [
+            ((count, dim + spare), BF, VM), ((3, 1, own), F32, HBM), ((count, dim), F32, HBM),
+        ],
         (
             segments, kept_mask, absorbed, lifted, puller, unit_in, spread_in, score, pool_unit, stats, key_weight,
             sums, ends, query_weight, latent, rows, mixed_grad,
         ),
-        (1, 10, 13, 14),
+        (1, 2, 10, 13, 14),
         [
-            pltpu.VMEM((count, tall), F32), wide, pltpu.VMEM((3, 1, own), F32), area, area,
-            pltpu.SemaphoreType.DMA((2,)),
+            pltpu.VMEM((count, kept), BF), pltpu.VMEM((count, tall), F32), wide, pltpu.VMEM((3, 1, own), F32), area,
+            area, pltpu.VMEM((80, count), F32), pltpu.SemaphoreType.DMA((2,)),
         ],
         16, 2 * count * dim * dim + 4 * kept * count * tall, 8 * MIB,
     )
@@ -713,7 +744,6 @@
     early_far = other(early)
     packs_far = other(packs)
     late_far = other(late)
-    vectors_far = other(vectors)
     square = ((dim, dim), F32, HBM)
     slab = ((features, dim), F32, HBM)
     line = ((dim,), F32, VM)
@@ -728,15 +758,16 @@
         slots + sems, 12, 8 * count * dim * dim + 4 * count * dim * tall, 10 * MIB,
     )
     (
-        query_weight_grad, query_bias_grad, key_weight_grad, lat_gain_grad, lat_shift_grad, mlp_gain_grad,
+        encoded, query_weight_grad, query_bias_grad, key_weight_grad, lat_gain_grad, lat_shift_grad, mlp_gain_grad,
         mlp_shift_grad, in_gain_grad, in_shift_grad,
     ) = call(
         lambda *refs: last_kernel(features, *refs),
-        [square, line, slab, line, line, line, line, short, short],
+        [((count, dim), BF, HBM), square, line, slab, line, line, line, line, short, short],
         (
-            early, early_far, late, late_far, vectors, vectors_far, down_weight_grad,
+            early, early_far, late, late_far, hidden, mixed, down_weight, rows,
+            down_weight_grad,
         ),
-        (), slots + sems, 12, 4 * count * dim * dim + 4 * count * dim * tall, 6 * MIB, (6,),
+        (), slots + [low] + sems + [pltpu.SemaphoreType.DMA(())], 12, 4 * count * dim * dim + 4 * count * dim * tall, 6 * MIB, (8,),
     )
 
     return (

time: 43.3 us -> 42 us (0.970)
  Pallas kernels: 29.2 us -> 28.7 us
  waiting for transfers between devices: 3.54 us -> 3.1 us
    all_to_all x1, waiting for transfers between devices: 3.45 us -> 2.92 us  [on_chip(): segments = lax.all_to_all(packed, 'pix', 0, 0)]
    pallas_call x6, Pallas kernels: 29.2 us -> 28.7 us  [call(): pl.pallas_call(whole, out_shape=shapes if len(shapes) > 1 else shapes[0],...]
    ppermute x4 -> x3, starting transfers between devices: 1.14 us -> 0.71 us  [other(): return lax.ppermute(value, 'img', swap)]
  transfers between devices with their start and end apart: 5 -> 4, of which waited for: 2 -> 2; matrix products, arithmetic and copies ran while one was open for 0% -> 0% of each run, Pallas kernels for 34% -> 37%
where the time goes in v5:
time: 42 us; the launch traced here: 41.7 us
  Pallas kernels  28.7 us (68%)
  starting transfers between devices  9.04 us (22%)
  waiting for transfers between devices  3.1 us (7%)
  between operations  0.91 us (2%)
    pallas_call x6, Pallas kernels, call(): pl.pallas_call(whole, out_shape=shapes if len(shapes) > 1 else shapes[0],...  28.7 us
    all_to_all x1, starting transfers between devices, on_chip(): segments = lax.all_to_all(packed, 'pix', 0, 0)  8.32 us
    all_to_all x1, waiting for transfers between devices, on_chip(): segments = lax.all_to_all(packed, 'pix', 0, 0)  2.92 us
  transfers between devices with their start and end apart: 4, of which 2 were waited for; matrix products, arithmetic and copies ran while one was open for 0% of the time, Pallas kernels for 37%

profile of v5, /device:TPU:0, one launch (start us, length us, event | category | flops | bytes accessed | tf_op | source)
XLA Modules:
  0.0 41.7 jit_solution(2374084315858485053)
XLA Ops:
  0.7 1.8 %shard_map.341 = bf16[16,8,384]{2,1,0:T(8,128)(2,1)} custom-call(f32[3,1,384]{2,1,0:T(1,128)} %bitcast.12, s32[2,384]{1,0:T(2,128)} %bitcast.13, s32[1,384]{1,0:T(1,128)} %refs_1_.3), custom_call_target="tpu_custom_call" | custom-call | flops 4718592 | bytes 49152 | tf_op jit(solution)/shard_map/pallas_call | solution.py:647
  2.4 8.3 %all-to-all-start = ((bf16[16,8,384]{2,1,0:T(8,128)(2,1)}), bf16[16,8,384]{2,1,0:T(8,128)(2,1)S(1)}, u32[]{:S(2)}, u32[]{:S(2)}) async-start(bf16[16,8,384]{2,1,0:T(8,128)(2,1)} %shard_map.341), calls=%async_computation | async-start | bytes 196608 | tf_op jit(solution)/shard_map/all_to_all | solution.py:679
  10.8 4.7 %shard_map.340 = (bf16[256,3072]{1,0:T(8,128)(2,1)}, f32[256,384]{1,0:T(8,128)}, bf16[256,384]{1,0:T(8,128)(2,1)S(1)}, bf16[256,1024]{1,0:T(8,128)(2,1)S(1)}, bf...) custom-call(bf16[256,1024]{1,0:T(8,128)(2,1)} %bitcast.7, ...), custom_call_target="tpu_custom_call" | custom-call | flops 1275068416 | bytes 8388608 | tf_op jit(solution)/shard_map/pallas_call | solution.py:647
  15.5 2.9 %all-to-all-done.refs_0_ = bf16[16,8,384]{2,1,0:T(8,128)(2,1)S(1)} async-done(((bf16[16,8,384]{2,1,0:T(8,128)(2,1)}), bf16[16,8,384]{2,1,0:T(8,128)(2,1)S(1)}, u32[]{:S(2)}, u32[]{:S(2)}) %all-to-all-start) | async-done | bytes 98336 | tf_op jit(solution)/shard_map/all_to_all | solution.py:679
  18.4 0.0 copy-start.1
  18.4 7.5 %shard_map.342 = (bf16[256,1024]{1,0:T(8,128)(2,1)S(1)}, f32[256,1024]{1,0:T(8,128)S(1)}, bf16[256,4608]{1,0:T(8,128)(2,1)S(1)}, f32[256,1024]{1,0:T(8,128)S(1)}...) custom-call(bf16[16,8,384]{2,1,0:T(8,128)(2,1)S(1)} %all-to-all-done, ...), custom_call_target="tpu_custom_call" | custom-call | flops 3825205248 | bytes 8388608 | tf_op jit(solution)/shard_map/pallas_call | solution.py:647
  26.0 0.1 collective-permute-start.2
  26.1 0.0 copy-done.1
  26.1 0.5 %collective-permute-start = (bf16[256,3072]{1,0:T(8,128)(2,1)S(1)}, bf16[256,3072]{1,0:T(8,128)(2,1)S(1)}, u32[]{:S(2)}, u32[]{:S(2)}) collective-permute-start(bf16[256,3072]{1,0:T(8,128)(2,1)S(1)} %copy-done.1), channel_id=1, source_target_pairs={{0,16},{16,0},{1,17},{17,1},{2,18},{18,2},{3,19},{19,3},{4,20},{20... | collective-permute-start | bytes 4718600 | tf_op jit(solution)/shard_map/ppermute | solution.py:673
  26.6 5.9 %shard_map.343 = (bf16[256,1536]{1,0:T(8,128)(2,1)S(1)}, f32[3,1,384]{2,1,0:T(1,128)}, f32[256,1024]{1,0:T(8,128)}) custom-call(bf16[16,8,384]{2,1,0:T(8,128)(2,1)S(1)} %all-to-all-done.refs_0_, s32[1,384]{1,0:T(1,128)} %refs_1_.3, f32[256,384]{1,0:T(8,128)} %get-tuple-element.58.refs_2_, f32[256,384]{1,0:T(8,128)S(1)} %get-tuple-element.65.refs_3_, ...), custom_call_target="tpu_custom_call" | custom-call | flops 1744830464 | bytes 8388608 | tf_op jit(solution)/shard_map/pallas_call | solution.py:647
  32.5 0.0 copy-start
  32.5 0.2 collective-permute-start.1
  32.6 0.2 collective-permute-done.refs_3_.refs_1_
  32.8 0.0 collective-permute-done.2.refs_1_
  32.8 5.0 %shard_map.344 = (f32[1024,1024]{1,0:T(8,128)}, f32[1024]{0:T(1024)}, f32[1024,1024]{1,0:T(8,128)}, f32[1024]{0:T(1024)}, f32[261,1024]{1,0:T(8,128)}, /*index=5*/f32[1024]{0:T(1024)}) custom-call(bf16[256,4608]{1,0:T(8,128)(2,1)S(1)} %get-tuple-element.77.refs_0_, bf16[256,4608]{1,0:T(8,128)(2,1)S(1)} %collective-permute-done.2.refs_1_, ...), custom_call_target="tpu_custom_call" | custom-call | flops 2550136832 | bytes 10485760 | tf_op jit(solution)/shard_map/pallas_call | solution.py:647
  37.8 0.0 collective-permute-done.1.refs_3_
  37.8 0.0 copy-done
  37.8 3.7 %shard_map.345 = (bf16[256,1024]{1,0:T(8,128)(2,1)}, f32[1024,1024]{1,0:T(8,128)}, f32[1024]{0:T(1024)}, f32[261,1024]{1,0:T(8,128)}, f32[1024]{0:T(1024)}, /*in...) custom-call(bf16[256,3072]{1,0:T(8,128)(2,1)S(1)} %copy-done.1, ...), custom_call_target="tpu_custom_call" | custom-call | flops 1476395008 | bytes 6291456 | tf_op jit(solution)/shard_map/pallas_call | solution.py:647
Async XLA Ops:
  2.4 16.0 %all-to-all-start = ((bf16[16,8,384]{2,1,0:T(8,128)(2,1)}), bf16[16,8,384]{2,1,0:T(8,128)(2,1)S(1)}, u32[]{:S(2)}, u32[]{:S(2)}) async-start(bf16[16,8,384]{2,1,0:T(8,128)(2,1)} %shard_map.341), calls=%async_computation | async-start | bytes 196608 | tf_op jit(solution)/shard_map/all_to_all | solution.py:679
  18.4 7.6 %copy-start.1 = (bf16[256,3072]{1,0:T(8,128)(2,1)S(1)}, bf16[256,3072]{1,0:T(8,128)(2,1)}, u32[]{:S(2)}) copy-start(bf16[256,3072]{1,0:T(8,128)(2,1)} %get-tuple-element.57.refs_2_.refs_0_) | copy-start | bytes 4718596
  26.0 6.9 %collective-permute-start.2 = (bf16[256,4608]{1,0:T(8,128)(2,1)S(1)}, bf16[256,4608]{1,0:T(8,128)(2,1)S(1)}, u32[]{:S(2)}, u32[]{:S(2)}) collective-permute-start(bf16[256,4608]{1,0:T(8,128)(2,1)S(1)} %get-tuple-element.77.refs_0_), channel_id=1, source_target_pairs={{0,16},{16,0},{1,17},{17,1},{2,18},{18,2},{3,19},{19,3},{4,20},{20... | collective-permute-start | bytes 7077896 | tf_op jit(solution)/shard_map/ppermute | solution.py:673
  26.1 6.8 %collective-permute-start = (bf16[256,3072]{1,0:T(8,128)(2,1)S(1)}, bf16[256,3072]{1,0:T(8,128)(2,1)S(1)}, u32[]{:S(2)}, u32[]{:S(2)}) collective-permute-start(bf16[256,3072]{1,0:T(8,128)(2,1)S(1)} %copy-done.1), channel_id=1, source_target_pairs={{0,16},{16,0},{1,17},{17,1},{2,18},{18,2},{3,19},{19,3},{4,20},{20... | collective-permute-start | bytes 4718600 | tf_op jit(solution)/shard_map/ppermute | solution.py:673
  32.5 5.3 %copy-start = (bf16[1024,1024]{1,0:T(8,128)(2,1)S(1)}, bf16[1024,1024]{1,0:T(8,128)(2,1)}, u32[]{:S(2)}) copy-start(bf16[1024,1024]{1,0:T(8,128)(2,1)} %refs_6_.3) | copy-start | bytes 6291460
  32.5 5.3 %collective-permute-start.1 = (bf16[256,1536]{1,0:T(8,128)(2,1)S(1)}, bf16[256,1536]{1,0:T(8,128)(2,1)S(1)}, u32[]{:S(2)}, u32[]{:S(2)}) collective-permute-start(bf16[256,1536]{1,0:T(8,128)(2,1)S(1)} %get-tuple-element.74.refs_2_), channel_id=1, source_target_pairs={{0,16},{16,0},{1,17},{17,1},{2,18},{18,2},{3,19},{19,3},{4,20},{20... | collective-permute-start | bytes 2359304 | tf_op jit(solution)/shard_map/ppermute | solution.py:673

commit v6 on v5

--- a/solution.py
+++ b/solution.py
@@ -211,7 +211,7 @@
     latent = latent.get()
     count, dim = latent.shape
     tall = absorbed.shape[1]
-    turned, query, kept_grad = (early.at[:, at * dim : (at + 1) * dim] for at in range(3))
+    turned, query = early.at[:, :dim], early.at[:, dim:]
     step = 32
     lat_gain, lat_shift = row_of(gain), row_of(shift)
     for start in range(0, count, step):
@@ -235,7 +235,6 @@
     ends[0:1, :] = gains
     ends[1:2, :] = gain_row(in_shift, tall, features)
     grad = grad.get()
-    kept_grad[...] = grad[...]
     leave = [
         pltpu.make_async_copy(early, early_out, sems.at[2]),
         pltpu.make_async_copy(absorbed, absorbed_out, sems.at[3]),
@@ -337,10 +336,12 @@
     gains, shifts = ends[0:1, :], ends[1:2, :]
     count, dim = mixed.shape
     value_bias, gain, shift, up_bias = (rows[at : at + 1, :] for at in range(4))
-    hidden_turned, two_turned, pre_grad, attn_grad = (packs.at[:, at * dim : (at + 1) * dim] for at in range(4))
+    hidden_turned, two_turned, pre_grad, attn_grad, kept_grad = (
+        packs.at[:, at * dim : (at + 1) * dim] for at in range(5)
+    )
     pool = waves_last(pool_unit[...] * gains + shifts, features)
     pool_low[...] = pool.astype(BF)
-    turn_pool(packs.at[:, 4 * dim :], pool)
+    turn_pool(packs.at[:, 5 * dim :], pool)
 
     latent = latent.get()
     pad_rows(value, value_raw.get())
@@ -370,6 +371,7 @@
         span = slice(start, start + wide)
         back[:, span] = contract(pre_grad[...], up[span, :], 1, 1)
     grad = grad.get()
+    kept_grad[...] = grad[...]
     gain_sum = jnp.zeros((8, dim), F32)
     shift_sum = jnp.zeros((8, dim), F32)
     for start in range(0, count, low):
@@ -425,8 +427,8 @@
     features,
     segments, kept_row, absorbed, lifted, puller, unit_in, spread_in, score, pool_unit, stats,
     key_raw, sums, ends, query_weight, latent, rows, mixed_grad,
-    late, color_out, latent_out,
-    pulls, pooled, key, color_grad, back, latent_grad, lines, out_sems,
+    late, color_grad, latent_grad,
+    pulls, pooled, key, back, lines,
 ):
     count, dim = pooled.shape[0], key.shape[1]
     own = segments.shape[2]
@@ -506,14 +508,6 @@
         shift_sum = shift_sum + fold_rows(upstream)
     vectors += [jnp.sum(gain_sum, axis=0, keepdims=True), jnp.sum(shift_sum, axis=0, keepdims=True)]
     write_vectors(late, lines, vectors)
-    leave = [
-        pltpu.make_async_copy(color_grad, color_out, out_sems.at[0]),
-        pltpu.make_async_copy(latent_grad, latent_out, out_sems.at[1]),
-    ]
-    for copy in leave:
-        copy.start()
-    for copy in leave:
-        copy.wait()
 
 
 class Leaving:
@@ -578,20 +572,27 @@
 
 def late_kernel(
     features,
-    packs, packs_far, early, early_far,
-    down_out, down_bias, up_out, up_bias, value_out, value_bias,
-    buffers, held, sems, held_sem,
+    packs, packs_far, color_grad, latent_grad,
+    color_out, latent_out, down_out, down_bias, up_out, up_bias, value_out, value_bias,
+    buffers, held, sems, held_sem, out_sems,
 ):
     dim = down_out.shape[1]
-    hidden, two, pre, attn, pool = parts_of(packs, dim)
-    hidden_far, two_far, pre_far, attn_far, pool_far = parts_of(packs_far, dim)
-    grad, grad_far = parts_of(early, dim)[2], parts_of(early_far, dim)[2]
+    hidden, two, pre, attn, grad, pool = parts_of(packs, dim)
+    hidden_far, two_far, pre_far, attn_far, grad_far, pool_far = parts_of(packs_far, dim)
+    first = [
+        pltpu.make_async_copy(latent_grad, latent_out, out_sems.at[0]),
+        pltpu.make_async_copy(color_grad, color_out, out_sems.at[1]),
+    ]
+    for copy in first:
+        copy.start()
     leaving = Leaving(buffers, sems)
     products(leaving, hidden, hidden_far, grad, grad_far, down_out, down_bias)
     short_product(held, pool, pool_far, attn, attn_far, value_bias, None)
     leave = pltpu.make_async_copy(held, value_out, held_sem)
     leave.start()
     products(leaving, two, two_far, pre, pre_far, up_out, up_bias)
+    for copy in first:
+        copy.wait()
     leave.wait()
     leaving.end()
 
@@ -603,8 +604,8 @@
     buffers, held, encoded, sems, held_sem, encoded_sem,
 ):
     dim = query_out.shape[1]
-    one, query, _ = parts_of(early, dim)
-    one_far, query_far, _ = parts_of(early_far, dim)
+    one, query = parts_of(early, dim)
+    one_far, query_far = parts_of(early_far, dim)
     grad, pool = parts_of(late, dim)
     grad_far, pool_far = parts_of(late_far, dim)
     leaving = Leaving(buffers, sems)
@@ -683,7 +684,7 @@
     early, absorbed, scorer, hidden_grad, table_kept, rows, ends, up_kept = call(
         lambda *refs: query_kernel(features, *refs),
         [
-            ((count, 3 * dim), BF, HBM), ((count, tall), F32, HBM), ((count, tall), BF, VM), ((count, dim), BF, VM),
+            ((count, 2 * dim), BF, HBM), ((count, tall), F32, HBM), ((count, tall), BF, VM), ((count, dim), BF, VM),
             (table.shape, BF, VM), ((8, dim), F32, VM), ((8, tall), F32, VM), ((dim, dim), BF, VM),
         ],
         (
@@ -692,7 +693,7 @@
         ),
         tuple(range(16)),
         [
-            pltpu.VMEM((count, dim), BF), wide, pltpu.VMEM((count, 3 * dim), BF), pltpu.VMEM((count, tall), F32),
+            pltpu.VMEM((count, dim), BF), wide, pltpu.VMEM((count, 2 * dim), BF), pltpu.VMEM((count, tall), F32),
             pltpu.SemaphoreType.DMA((4,)),
         ],
         16, 4 * count * dim * dim + 2 * count * dim * tall, 8 * MIB, (16,),
@@ -707,7 +708,7 @@
     ) = call(
         lambda *refs: forward_kernel(features, *refs),
         [
-            ((count, dim), BF, VM), ((count, dim), F32, VM), ((count, 4 * dim + spare), BF, VM),
+            ((count, dim), BF, VM), ((count, dim), F32, VM), ((count, 5 * dim + spare), BF, VM),
             ((count, dim), F32, VM),
             ((count, tall), F32, VM), ((count, tall), BF, VM), ((tall, kept), BF, VM), ((8, kept), F32, VM),
             ((count, kept), F32, VM), ((count, tall), F32, VM), ((count, LANES), F32, VM), ((8, dim), F32, VM),
@@ -727,7 +728,7 @@
     late, color_grad, latent_grad = call(
         lambda *refs: pull_kernel(features, *refs),
         [
-            ((count, dim + spare), BF, VM), ((3, 1, own), F32, HBM), ((count, dim), F32, HBM),
+            ((count, dim + spare), BF, VM), ((3, 1, own), F32, VM), ((count, dim), F32, VM),
         ],
         (
             segments, kept_mask, absorbed, lifted, puller, unit_in, spread_in, score, pool_unit, stats, key_weight,
@@ -735,14 +736,14 @@
         ),
         (1, 2, 10, 13, 14),
         [
-            pltpu.VMEM((count, kept), BF), pltpu.VMEM((count, tall), F32), wide, pltpu.VMEM((3, 1, own), F32), area,
-            area, pltpu.VMEM((80, count), F32), pltpu.SemaphoreType.DMA((2,)),
+            pltpu.VMEM((count, kept), BF), pltpu.VMEM((count, tall), F32), wide, area, pltpu.VMEM((80, count), F32),
         ],
         16, 2 * count * dim * dim + 4 * kept * count * tall, 8 * MIB,
     )
 
+    packs_far = other(packs)
+    early, late = lax.optimization_barrier((early, late))
     early_far = other(early)
-    packs_far = other(packs)
     late_far = other(late)
     square = ((dim, dim), F32, HBM)
     slab = ((features, dim), F32, HBM)
@@ -752,10 +753,14 @@
         pltpu.VMEM((4, STRIP, dim), F32), pltpu.VMEM((features, dim), F32),
     ]
     sems = [pltpu.SemaphoreType.DMA((4,)), pltpu.SemaphoreType.DMA(())]
-    down_weight_grad, down_bias_grad, up_weight_grad, up_bias_grad, value_weight_grad, value_bias_grad = call(
+    (
+        color_grad, latent_grad, down_weight_grad, down_bias_grad, up_weight_grad, up_bias_grad, value_weight_grad,
+        value_bias_grad,
+    ) = call(
         lambda *refs: late_kernel(features, *refs),
-        [square, line, square, line, slab, line], (packs, packs_far, early, early_far), (),
-        slots + sems, 12, 8 * count * dim * dim + 4 * count * dim * tall, 10 * MIB,
+        [((3, 1, own), F32, HBM), ((count, dim), F32, HBM), square, line, square, line, slab, line],
+        (packs, packs_far, color_grad, latent_grad), (),
+        slots + sems + [pltpu.SemaphoreType.DMA((2,))], 12, 8 * count * dim * dim + 4 * count * dim * tall, 10 * MIB,
     )
     (
         encoded, query_weight_grad, query_bias_grad, key_weight_grad, lat_gain_grad, lat_shift_grad, mlp_gain_grad,

time: 42 us -> 41.1 us (0.979)
  Pallas kernels: 28.7 us -> 27.7 us
    pallas_call x6, Pallas kernels: 28.7 us -> 27.7 us  [call(): pl.pallas_call(whole, out_shape=shapes if len(shapes) > 1 else shapes[0],...]
  transfers between devices with their start and end apart: 4 -> 4, of which waited for: 2 -> 1; matrix products, arithmetic and copies ran while one was open for 0% -> 0% of each run, Pallas kernels for 37% -> 36%
where the time goes in v6:
time: 41.1 us; the launch traced here: 40.8 us
  Pallas kernels  27.7 us (67%)
  starting transfers between devices  9.02 us (22%)
  waiting for transfers between devices  3.13 us (8%)
  between operations  0.91 us (2%)
    pallas_call x6, Pallas kernels, call(): pl.pallas_call(whole, out_shape=shapes if len(shapes) > 1 else shapes[0],...  27.7 us
    all_to_all x1, starting transfers between devices, on_chip(): segments = lax.all_to_all(packed, 'pix', 0, 0)  8.32 us
    all_to_all x1, waiting for transfers between devices, on_chip(): segments = lax.all_to_all(packed, 'pix', 0, 0)  3.12 us
  transfers between devices with their start and end apart: 4, of which 1 were waited for; matrix products, arithmetic and copies ran while one was open for 0% of the time, Pallas kernels for 36%

profile of v6, /device:TPU:0, one launch (start us, length us, event | category | flops | bytes accessed | tf_op | source)
XLA Modules:
  0.0 40.8 jit_solution(15190165653401697027)
XLA Ops:
  0.7 1.8 %shard_map.341 = bf16[16,8,384]{2,1,0:T(8,128)(2,1)} custom-call(f32[3,1,384]{2,1,0:T(1,128)} %bitcast.12, s32[2,384]{1,0:T(2,128)} %bitcast.13, s32[1,384]{1,0:T(1,128)} %refs_1_.3), custom_call_target="tpu_custom_call" | custom-call | flops 4718592 | bytes 49152 | tf_op jit(solution)/shard_map/pallas_call | solution.py:648
  2.4 8.3 %all-to-all-start = ((bf16[16,8,384]{2,1,0:T(8,128)(2,1)}), bf16[16,8,384]{2,1,0:T(8,128)(2,1)S(1)}, u32[]{:S(2)}, u32[]{:S(2)}) async-start(bf16[16,8,384]{2,1,0:T(8,128)(2,1)} %shard_map.341), calls=%async_computation | async-start | bytes 196608 | tf_op jit(solution)/shard_map/all_to_all | solution.py:680
  10.8 4.5 %shard_map.340 = (bf16[256,2048]{1,0:T(8,128)(2,1)}, f32[256,384]{1,0:T(8,128)}, bf16[256,384]{1,0:T(8,128)(2,1)S(1)}, bf16[256,1024]{1,0:T(8,128)(2,1)S(1)}, bf...) custom-call(bf16[256,1024]{1,0:T(8,128)(2,1)} %bitcast.7, ...), custom_call_target="tpu_custom_call" | custom-call | flops 1275068416 | bytes 8388608 | tf_op jit(solution)/shard_map/pallas_call | solution.py:648
  15.3 3.1 %all-to-all-done.refs_0_ = bf16[16,8,384]{2,1,0:T(8,128)(2,1)S(1)} async-done(((bf16[16,8,384]{2,1,0:T(8,128)(2,1)}), bf16[16,8,384]{2,1,0:T(8,128)(2,1)S(1)}, u32[]{:S(2)}, u32[]{:S(2)}) %all-to-all-start) | async-done | bytes 98336 | tf_op jit(solution)/shard_map/all_to_all | solution.py:680
  18.4 7.6 %shard_map.342 = (bf16[256,1024]{1,0:T(8,128)(2,1)S(1)}, f32[256,1024]{1,0:T(8,128)S(1)}, bf16[256,5632]{1,0:T(8,128)(2,1)S(1)}, f32[256,1024]{1,0:T(8,128)S(1)}...) custom-call(bf16[16,8,384]{2,1,0:T(8,128)(2,1)S(1)} %all-to-all-done, ...), custom_call_target="tpu_custom_call" | custom-call | flops 3825205248 | bytes 8388608 | tf_op jit(solution)/shard_map/pallas_call | solution.py:648
  26.0 0.1 collective-permute-start.2
  26.1 0.0 copy-start.1
  26.1 5.0 %shard_map.343 = (bf16[256,1536]{1,0:T(8,128)(2,1)S(1)}, f32[3,1,384]{2,1,0:T(1,128)S(1)}, f32[256,1024]{1,0:T(8,128)S(1)}) custom-call(bf16[16,8,384]{2,1,0:T(8,128)(2,1)S(1)} %all-to-all-done.refs_0_, s32[1,384]{1,0:T(1,128)} %refs_1_.3, f32[256,384]{1,0:T(8,128)} %get-tuple-element.62.refs_2_, f32[256,384]{1,0:T(8,128)S(1)} %get-tuple-element.69.refs_3_, ...), custom_call_target="tpu_custom_call" | custom-call | flops 1744830464 | bytes 8388608 | tf_op jit(solution)/shard_map/pallas_call | solution.py:648
  31.1 0.0 copy-done.1
  31.1 0.5 %collective-permute-start = (bf16[256,2048]{1,0:T(8,128)(2,1)S(1)}, bf16[256,2048]{1,0:T(8,128)(2,1)S(1)}, u32[]{:S(2)}, u32[]{:S(2)}) collective-permute-start(bf16[256,2048]{1,0:T(8,128)(2,1)S(1)} %copy-done.1), channel_id=1, source_target_pairs={{0,16},{16,0},{1,17},{17,1},{2,18},{18,2},{3,19},{19,3},{4,20},{20... | collective-permute-start | bytes 3145736 | tf_op jit(solution)/shard_map/ppermute | solution.py:674
  31.6 0.1 collective-permute-start.1
  31.7 0.0 collective-permute-done.2.refs_1_
  31.7 0.0 copy-start
  31.7 5.1 %shard_map.344 = (f32[3,1,384]{2,1,0:T(1,128)}, f32[256,1024]{1,0:T(8,128)}, f32[1024,1024]{1,0:T(8,128)}, f32[1024]{0:T(1024)}, f32[1024,1024]{1,0:T(8,128)}, /...) custom-call(bf16[256,5632]{1,0:T(8,128)(2,1)S(1)} %get-tuple-element.83.refs_0_, ...), custom_call_target="tpu_custom_call" | custom-call | flops 2550136832 | bytes 10485760 | tf_op jit(solution)/shard_map/pallas_call | solution.py:648
  36.9 0.0 collective-permute-done.1.refs_3_
  36.9 0.0 collective-permute-done.refs_1_
  36.9 0.0 copy-done
  36.9 3.7 %shard_map.345 = (bf16[256,1024]{1,0:T(8,128)(2,1)}, f32[1024,1024]{1,0:T(8,128)}, f32[1024]{0:T(1024)}, f32[261,1024]{1,0:T(8,128)}, f32[1024]{0:T(1024)}, /*in...) custom-call(bf16[256,2048]{1,0:T(8,128)(2,1)S(1)} %copy-done.1, ...), custom_call_target="tpu_custom_call" | custom-call | flops 1476395008 | bytes 6291456 | tf_op jit(solution)/shard_map/pallas_call | solution.py:648
Async XLA Ops:
  2.4 16.0 %all-to-all-start = ((bf16[16,8,384]{2,1,0:T(8,128)(2,1)}), bf16[16,8,384]{2,1,0:T(8,128)(2,1)S(1)}, u32[]{:S(2)}, u32[]{:S(2)}) async-start(bf16[16,8,384]{2,1,0:T(8,128)(2,1)} %shard_map.341), calls=%async_computation | async-start | bytes 196608 | tf_op jit(solution)/shard_map/all_to_all | solution.py:680
  26.0 5.7 %collective-permute-start.2 = (bf16[256,5632]{1,0:T(8,128)(2,1)S(1)}, bf16[256,5632]{1,0:T(8,128)(2,1)S(1)}, u32[]{:S(2)}, u32[]{:S(2)}) collective-permute-start(bf16[256,5632]{1,0:T(8,128)(2,1)S(1)} %get-tuple-element.83.refs_0_), channel_id=1, source_target_pairs={{0,16},{16,0},{1,17},{17,1},{2,18},{18,2},{3,19},{19,3},{4,20},{20... | collective-permute-start | bytes 8650760 | tf_op jit(solution)/shard_map/ppermute | solution.py:674
  26.1 5.0 %copy-start.1 = (bf16[256,2048]{1,0:T(8,128)(2,1)S(1)}, bf16[256,2048]{1,0:T(8,128)(2,1)}, u32[]{:S(2)}) copy-start(bf16[256,2048]{1,0:T(8,128)(2,1)} %get-tuple-element.79.refs_0_) | copy-start | bytes 3145732
  31.1 5.8 %collective-permute-start = (bf16[256,2048]{1,0:T(8,128)(2,1)S(1)}, bf16[256,2048]{1,0:T(8,128)(2,1)S(1)}, u32[]{:S(2)}, u32[]{:S(2)}) collective-permute-start(bf16[256,2048]{1,0:T(8,128)(2,1)S(1)} %copy-done.1), channel_id=1, source_target_pairs={{0,16},{16,0},{1,17},{17,1},{2,18},{18,2},{3,19},{19,3},{4,20},{20... | collective-permute-start | bytes 3145736 | tf_op jit(solution)/shard_map/ppermute | solution.py:674
  31.6 5.2 %collective-permute-start.1 = (bf16[256,1536]{1,0:T(8,128)(2,1)S(1)}, bf16[256,1536]{1,0:T(8,128)(2,1)S(1)}, u32[]{:S(2)}, u32[]{:S(2)}) collective-permute-start(bf16[256,1536]{1,0:T(8,128)(2,1)S(1)} %get-tuple-element.80.refs_2_), channel_id=1, source_target_pairs={{0,16},{16,0},{1,17},{17,1},{2,18},{18,2},{3,19},{19,3},{4,20},{20... | collective-permute-start | bytes 2359304 | tf_op jit(solution)/shard_map/ppermute | solution.py:674
  31.7 5.2 %copy-start = (bf16[1024,1024]{1,0:T(8,128)(2,1)S(1)}, bf16[1024,1024]{1,0:T(8,128)(2,1)}, u32[]{:S(2)}) copy-start(bf16[1024,1024]{1,0:T(8,128)(2,1)} %refs_6_.3) | copy-start | bytes 6291460

commit v7 on v6

--- a/solution.py
+++ b/solution.py
@@ -426,13 +426,15 @@
 def pull_kernel(
     features,
     segments, kept_row, absorbed, lifted, puller, unit_in, spread_in, score, pool_unit, stats,
-    key_raw, sums, ends, query_weight, latent, rows, mixed_grad,
+    key_raw, sums, ends, query_weight, latent, rows, mixed_grad, early,
     late, color_grad, latent_grad,
-    pulls, pooled, key, back, lines,
+    pulls, pooled, key, back, lines, early_sem,
 ):
     count, dim = pooled.shape[0], key.shape[1]
     own = segments.shape[2]
     tall, kept = unit_in.shape
+    bring = pltpu.make_async_copy(early, late.at[:, dim : 3 * dim], early_sem)
+    bring.start()
     waves = 4 * BANDS
     def shares(lanes):
         inner = jnp.dot(puller[...], unit_in[:, lanes], preferred_element_type=F32)
@@ -476,7 +478,7 @@
     held = pooled[...]
     total = held[:, features : features + 1]
     pool = waves_last(held * gains + shifts * total, features)
-    turn_pool(late.at[:, dim:], pool)
+    turn_pool(late.at[:, 3 * dim :], pool)
     pool = pool.astype(BF)
     pad_rows(key, key_raw)
     gain_sum = absorbed[...] * held + lifted[...] * pool_unit[...]
@@ -508,6 +510,7 @@
         shift_sum = shift_sum + fold_rows(upstream)
     vectors += [jnp.sum(gain_sum, axis=0, keepdims=True), jnp.sum(shift_sum, axis=0, keepdims=True)]
     write_vectors(late, lines, vectors)
+    bring.wait()
 
 
 class Leaving:
@@ -599,15 +602,13 @@
 
 def last_kernel(
     features,
-    early, early_far, late, late_far, hidden, mixed, down, rows, _,
+    late, late_far, hidden, mixed, down, rows, _,
     encoded_out, query_out, query_bias, key_out, lat_gain, lat_shift, mlp_gain, mlp_shift, in_gain, in_shift,
     buffers, held, encoded, sems, held_sem, encoded_sem,
 ):
     dim = query_out.shape[1]
-    one, query = parts_of(early, dim)
-    one_far, query_far = parts_of(early_far, dim)
-    grad, pool = parts_of(late, dim)
-    grad_far, pool_far = parts_of(late_far, dim)
+    grad, one, query, pool = parts_of(late, dim)
+    grad_far, one_far, query_far, pool_far = parts_of(late_far, dim)
     leaving = Leaving(buffers, sems)
     products(leaving, one, one_far, grad, grad_far, query_out, query_bias)
     short_product(held, pool, pool_far, query, query_far, None, 1.0 / math.sqrt(dim))
@@ -728,22 +729,21 @@
     late, color_grad, latent_grad = call(
         lambda *refs: pull_kernel(features, *refs),
         [
-            ((count, dim + spare), BF, VM), ((3, 1, own), F32, VM), ((count, dim), F32, VM),
+            ((count, 3 * dim + spare), BF, VM), ((3, 1, own), F32, VM), ((count, dim), F32, VM),
         ],
         (
             segments, kept_mask, absorbed, lifted, puller, unit_in, spread_in, score, pool_unit, stats, key_weight,
-            sums, ends, query_weight, latent, rows, mixed_grad,
+            sums, ends, query_weight, latent, rows, mixed_grad, early,
         ),
         (1, 2, 10, 13, 14),
         [
             pltpu.VMEM((count, kept), BF), pltpu.VMEM((count, tall), F32), wide, area, pltpu.VMEM((80, count), F32),
+            pltpu.SemaphoreType.DMA(()),
         ],
-        16, 2 * count * dim * dim + 4 * kept * count * tall, 8 * MIB,
+        16, 2 * count * dim * dim + 4 * kept * count * tall, 8 * MIB, (17,),
     )
 
     packs_far = other(packs)
-    early, late = lax.optimization_barrier((early, late))
-    early_far = other(early)
     late_far = other(late)
     square = ((dim, dim), F32, HBM)
     slab = ((features, dim), F32, HBM)
@@ -769,10 +769,10 @@
         lambda *refs: last_kernel(features, *refs),
         [((count, dim), BF, HBM), square, line, slab, line, line, line, line, short, short],
         (
-            early, early_far, late, late_far, hidden, mixed, down_weight, rows,
+            late, late_far, hidden, mixed, down_weight, rows,
             down_weight_grad,
         ),
-        (), slots + [low] + sems + [pltpu.SemaphoreType.DMA(())], 12, 4 * count * dim * dim + 4 * count * dim * tall, 6 * MIB, (8,),
+        (), slots + [low] + sems + [pltpu.SemaphoreType.DMA(())], 12, 4 * count * dim * dim + 4 * count * dim * tall, 6 * MIB, (6,),
     )
 
     return (

time: 41.1 us -> 40.9 us (level)
  transfers between devices with their start and end apart: 4 -> 3, of which waited for: 1 -> 1; matrix products, arithmetic and copies ran while one was open for 0% -> 0% of each run, Pallas kernels for 36% -> 36%
where the time goes in v7:
time: 40.9 us; the launch traced here: 40.6 us
  Pallas kernels  27.6 us (67%)
  starting transfers between devices  8.95 us (22%)
  waiting for transfers between devices  3.13 us (8%)
  between operations  0.89 us (2%)
    pallas_call x6, Pallas kernels, call(): pl.pallas_call(whole, out_shape=shapes if len(shapes) > 1 else shapes[0],...  27.6 us
    all_to_all x1, starting transfers between devices, on_chip(): segments = lax.all_to_all(packed, 'pix', 0, 0)  8.32 us
    all_to_all x1, waiting for transfers between devices, on_chip(): segments = lax.all_to_all(packed, 'pix', 0, 0)  3.12 us
  transfers between devices with their start and end apart: 3, of which 1 were waited for; matrix products, arithmetic and copies ran while one was open for 0% of the time, Pallas kernels for 36%

profile of v7, /device:TPU:0, one launch (start us, length us, event | category | flops | bytes accessed | tf_op | source)
XLA Modules:
  0.0 40.6 jit_solution(13158323037049606131)
XLA Ops:
  0.7 1.8 %shard_map.340 = bf16[16,8,384]{2,1,0:T(8,128)(2,1)} custom-call(f32[3,1,384]{2,1,0:T(1,128)} %bitcast.12, s32[2,384]{1,0:T(2,128)} %bitcast.13, s32[1,384]{1,0:T(1,128)} %refs_1_.3), custom_call_target="tpu_custom_call" | custom-call | flops 4718592 | bytes 49152 | tf_op jit(solution)/shard_map/pallas_call | solution.py:649
  2.4 8.3 %all-to-all-start = ((bf16[16,8,384]{2,1,0:T(8,128)(2,1)}), bf16[16,8,384]{2,1,0:T(8,128)(2,1)S(1)}, u32[]{:S(2)}, u32[]{:S(2)}) async-start(bf16[16,8,384]{2,1,0:T(8,128)(2,1)} %shard_map.340), calls=%async_computation | async-start | bytes 196608 | tf_op jit(solution)/shard_map/all_to_all | solution.py:681
  10.8 4.5 %shard_map.341 = (bf16[256,2048]{1,0:T(8,128)(2,1)}, f32[256,384]{1,0:T(8,128)}, bf16[256,384]{1,0:T(8,128)(2,1)S(1)}, bf16[256,1024]{1,0:T(8,128)(2,1)S(1)}, bf...) custom-call(bf16[256,1024]{1,0:T(8,128)(2,1)} %bitcast.7, ...), custom_call_target="tpu_custom_call" | custom-call | flops 1275068416 | bytes 8388608 | tf_op jit(solution)/shard_map/pallas_call | solution.py:649
  15.3 3.1 %all-to-all-done.refs_0_ = bf16[16,8,384]{2,1,0:T(8,128)(2,1)S(1)} async-done(((bf16[16,8,384]{2,1,0:T(8,128)(2,1)}), bf16[16,8,384]{2,1,0:T(8,128)(2,1)S(1)}, u32[]{:S(2)}, u32[]{:S(2)}) %all-to-all-start) | async-done | bytes 98336 | tf_op jit(solution)/shard_map/all_to_all | solution.py:681
  18.4 7.6 %shard_map.342 = (bf16[256,1024]{1,0:T(8,128)(2,1)S(1)}, f32[256,1024]{1,0:T(8,128)S(1)}, bf16[256,5632]{1,0:T(8,128)(2,1)S(1)}, f32[256,1024]{1,0:T(8,128)S(1)}...) custom-call(bf16[16,8,384]{2,1,0:T(8,128)(2,1)S(1)} %all-to-all-done, ...), custom_call_target="tpu_custom_call" | custom-call | flops 3825205248 | bytes 8388608 | tf_op jit(solution)/shard_map/pallas_call | solution.py:649
  26.0 0.1 collective-permute-start.1
  26.1 4.9 %shard_map.343 = (bf16[256,3584]{1,0:T(8,128)(2,1)S(1)}, f32[3,1,384]{2,1,0:T(1,128)S(1)}, f32[256,1024]{1,0:T(8,128)S(1)}) custom-call(bf16[16,8,384]{2,1,0:T(8,128)(2,1)S(1)} %all-to-all-done.refs_0_, s32[1,384]{1,0:T(1,128)} %refs_1_.3, f32[256,384]{1,0:T(8,128)} %get-tuple-element.59.refs_2_, f32[256,384]{1,0:T(8,128)S(1)} %get-tuple-element.66.refs_3_, ...), custom_call_target="tpu_custom_call" | custom-call | flops 1744830464 | bytes 8388608 | tf_op jit(solution)/shard_map/pallas_call | solution.py:649
  31.0 0.6 %collective-permute-start = (bf16[256,3584]{1,0:T(8,128)(2,1)S(1)}, bf16[256,3584]{1,0:T(8,128)(2,1)S(1)}, u32[]{:S(2)}, u32[]{:S(2)}) collective-permute-start(bf16[256,3584]{1,0:T(8,128)(2,1)S(1)} %get-tuple-element.76.refs_0_), channel_id=1, source_target_pairs={{0,16},{16,0},{1,17},{17,1},{2,18},{18,2},{3,19},{19,3},{4,20},{20... | collective-permute-start | bytes 5505032 | tf_op jit(solution)/shard_map/ppermute | solution.py:675
  31.5 0.0 collective-permute-done.1.refs_1_
  31.5 0.0 copy-start
  31.5 5.1 %shard_map.344 = (f32[3,1,384]{2,1,0:T(1,128)}, f32[256,1024]{1,0:T(8,128)}, f32[1024,1024]{1,0:T(8,128)}, f32[1024]{0:T(1024)}, f32[1024,1024]{1,0:T(8,128)}, /...) custom-call(bf16[256,5632]{1,0:T(8,128)(2,1)S(1)} %get-tuple-element.79.refs_0_, ...), custom_call_target="tpu_custom_call" | custom-call | flops 2550136832 | bytes 10485760 | tf_op jit(solution)/shard_map/pallas_call | solution.py:649
  36.7 0.0 collective-permute-done.refs_1_
  36.7 0.0 copy-done
  36.7 3.7 %shard_map.345 = (bf16[256,1024]{1,0:T(8,128)(2,1)}, f32[1024,1024]{1,0:T(8,128)}, f32[1024]{0:T(1024)}, f32[261,1024]{1,0:T(8,128)}, f32[1024]{0:T(1024)}, /*in...) custom-call(bf16[256,3584]{1,0:T(8,128)(2,1)S(1)} %get-tuple-element.76.refs_0_, ...), custom_call_target="tpu_custom_call" | custom-call | flops 1476395008 | bytes 6291456 | tf_op jit(solution)/shard_map/pallas_call | solution.py:649
Async XLA Ops:
  2.4 16.0 %all-to-all-start = ((bf16[16,8,384]{2,1,0:T(8,128)(2,1)}), bf16[16,8,384]{2,1,0:T(8,128)(2,1)S(1)}, u32[]{:S(2)}, u32[]{:S(2)}) async-start(bf16[16,8,384]{2,1,0:T(8,128)(2,1)} %shard_map.340), calls=%async_computation | async-start | bytes 196608 | tf_op jit(solution)/shard_map/all_to_all | solution.py:681
  26.0 5.5 %collective-permute-start.1 = (bf16[256,5632]{1,0:T(8,128)(2,1)S(1)}, bf16[256,5632]{1,0:T(8,128)(2,1)S(1)}, u32[]{:S(2)}, u32[]{:S(2)}) collective-permute-start(bf16[256,5632]{1,0:T(8,128)(2,1)S(1)} %get-tuple-element.79.refs_0_), channel_id=1, source_target_pairs={{0,16},{16,0},{1,17},{17,1},{2,18},{18,2},{3,19},{19,3},{4,20},{20... | collective-permute-start | bytes 8650760 | tf_op jit(solution)/shard_map/ppermute | solution.py:675
  31.0 5.7 %collective-permute-start = (bf16[256,3584]{1,0:T(8,128)(2,1)S(1)}, bf16[256,3584]{1,0:T(8,128)(2,1)S(1)}, u32[]{:S(2)}, u32[]{:S(2)}) collective-permute-start(bf16[256,3584]{1,0:T(8,128)(2,1)S(1)} %get-tuple-element.76.refs_0_), channel_id=1, source_target_pairs={{0,16},{16,0},{1,17},{17,1},{2,18},{18,2},{3,19},{19,3},{4,20},{20... | collective-permute-start | bytes 5505032 | tf_op jit(solution)/shard_map/ppermute | solution.py:675
  31.5 5.2 %copy-start = (bf16[1024,1024]{1,0:T(8,128)(2,1)S(1)}, bf16[1024,1024]{1,0:T(8,128)(2,1)}, u32[]{:S(2)}) copy-start(bf16[1024,1024]{1,0:T(8,128)(2,1)} %refs_4_.3) | copy-start | bytes 6291460

commit v8 on v7

--- a/solution.py
+++ b/solution.py
@@ -21,7 +21,7 @@
 MIB = 1 << 20
 MAKE = 256
 SCORE = 1024
-POOL = 512
+POOL = 256
 PULL = 1024
 WIDE = 256
 STRIP = 256
@@ -189,7 +189,7 @@
     size = source.shape[0]
     for start in range(0, source.shape[1], size):
         span = slice(start, start + size)
-        target[:, span] = jnp.transpose(source[:, span].astype(F32)).astype(BF)
+        target[:, span] = jnp.transpose(source[:, span])
 
 
 def turn_pool(target, pool):
@@ -363,8 +363,9 @@
         act = jnp.dot(two[...], up[:, span], preferred_element_type=F32) + up_bias[:, span]
         half = 0.5 * (1.0 + lax.erf(act * (1.0 / math.sqrt(2.0))))
         active = act * half
-        hidden[:, span] = active.astype(BF)
-        hidden_turned[:, span] = jnp.transpose(active).astype(BF)
+        active = active.astype(BF)
+        hidden[:, span] = active
+        hidden_turned[:, span] = jnp.transpose(active)
         slope = half + act * jnp.exp(-0.5 * act * act) * (1.0 / math.sqrt(2.0 * math.pi))
         pre_grad[:, span] = (hidden_grad[:, span].astype(F32) * slope).astype(BF)
     for start in range(0, dim, wide):

time: 40.9 us -> 40.7 us (level)
  no operation moved by 1% of the time
where the time goes in v8:
time: 40.7 us; the launch traced here: 40.5 us
  Pallas kernels  27.5 us (68%)
  starting transfers between devices  8.95 us (22%)
  waiting for transfers between devices  3.12 us (8%)
  between operations  0.89 us (2%)
    pallas_call x6, Pallas kernels, call(): pl.pallas_call(whole, out_shape=shapes if len(shapes) > 1 else shapes[0],...  27.5 us
    all_to_all x1, starting transfers between devices, on_chip(): segments = lax.all_to_all(packed, 'pix', 0, 0)  8.32 us
    all_to_all x1, waiting for transfers between devices, on_chip(): segments = lax.all_to_all(packed, 'pix', 0, 0)  3.11 us
  transfers between devices with their start and end apart: 3, of which 1 were waited for; matrix products, arithmetic and copies ran while one was open for 0% of the time, Pallas kernels for 36%

profile of v8, /device:TPU:0, one launch (start us, length us, event | category | flops | bytes accessed | tf_op | source)
XLA Modules:
  0.0 40.5 jit_solution(13597458811551765446)
XLA Ops:
  0.7 1.8 %shard_map.340 = bf16[16,8,384]{2,1,0:T(8,128)(2,1)} custom-call(f32[3,1,384]{2,1,0:T(1,128)} %bitcast.12, s32[2,384]{1,0:T(2,128)} %bitcast.13, s32[1,384]{1,0:T(1,128)} %refs_1_.3), custom_call_target="tpu_custom_call" | custom-call | flops 4718592 | bytes 49152 | tf_op jit(solution)/shard_map/pallas_call | solution.py:650
  2.4 8.3 %all-to-all-start = ((bf16[16,8,384]{2,1,0:T(8,128)(2,1)}), bf16[16,8,384]{2,1,0:T(8,128)(2,1)S(1)}, u32[]{:S(2)}, u32[]{:S(2)}) async-start(bf16[16,8,384]{2,1,0:T(8,128)(2,1)} %shard_map.340), calls=%async_computation | async-start | bytes 196608 | tf_op jit(solution)/shard_map/all_to_all | solution.py:682
  10.8 4.5 %shard_map.341 = (bf16[256,2048]{1,0:T(8,128)(2,1)}, f32[256,384]{1,0:T(8,128)}, bf16[256,384]{1,0:T(8,128)(2,1)S(1)}, bf16[256,1024]{1,0:T(8,128)(2,1)S(1)}, bf...) custom-call(bf16[256,1024]{1,0:T(8,128)(2,1)} %bitcast.7, ...), custom_call_target="tpu_custom_call" | custom-call | flops 1275068416 | bytes 8388608 | tf_op jit(solution)/shard_map/pallas_call | solution.py:650
  15.3 3.1 %all-to-all-done.refs_0_ = bf16[16,8,384]{2,1,0:T(8,128)(2,1)S(1)} async-done(((bf16[16,8,384]{2,1,0:T(8,128)(2,1)}), bf16[16,8,384]{2,1,0:T(8,128)(2,1)S(1)}, u32[]{:S(2)}, u32[]{:S(2)}) %all-to-all-start) | async-done | bytes 98336 | tf_op jit(solution)/shard_map/all_to_all | solution.py:682
  18.4 7.4 %shard_map.342 = (bf16[256,1024]{1,0:T(8,128)(2,1)S(1)}, f32[256,1024]{1,0:T(8,128)S(1)}, bf16[256,5632]{1,0:T(8,128)(2,1)S(1)}, f32[256,1024]{1,0:T(8,128)S(1)}...) custom-call(bf16[16,8,384]{2,1,0:T(8,128)(2,1)S(1)} %all-to-all-done, ...), custom_call_target="tpu_custom_call" | custom-call | flops 3825205248 | bytes 8388608 | tf_op jit(solution)/shard_map/pallas_call | solution.py:650
  25.9 0.1 collective-permute-start.1
  25.9 4.9 %shard_map.343 = (bf16[256,3584]{1,0:T(8,128)(2,1)S(1)}, f32[3,1,384]{2,1,0:T(1,128)S(1)}, f32[256,1024]{1,0:T(8,128)S(1)}) custom-call(bf16[16,8,384]{2,1,0:T(8,128)(2,1)S(1)} %all-to-all-done.refs_0_, s32[1,384]{1,0:T(1,128)} %refs_1_.3, f32[256,384]{1,0:T(8,128)} %get-tuple-element.59.refs_2_, f32[256,384]{1,0:T(8,128)S(1)} %get-tuple-element.66.refs_3_, ...), custom_call_target="tpu_custom_call" | custom-call | flops 1744830464 | bytes 8388608 | tf_op jit(solution)/shard_map/pallas_call | solution.py:650
  30.8 0.6 %collective-permute-start = (bf16[256,3584]{1,0:T(8,128)(2,1)S(1)}, bf16[256,3584]{1,0:T(8,128)(2,1)S(1)}, u32[]{:S(2)}, u32[]{:S(2)}) collective-permute-start(bf16[256,3584]{1,0:T(8,128)(2,1)S(1)} %get-tuple-element.76.refs_0_), channel_id=1, source_target_pairs={{0,16},{16,0},{1,17},{17,1},{2,18},{18,2},{3,19},{19,3},{4,20},{20... | collective-permute-start | bytes 5505032 | tf_op jit(solution)/shard_map/ppermute | solution.py:676
  31.4 0.0 collective-permute-done.1.refs_1_
  31.4 0.0 copy-start
  31.4 5.1 %shard_map.344 = (f32[3,1,384]{2,1,0:T(1,128)}, f32[256,1024]{1,0:T(8,128)}, f32[1024,1024]{1,0:T(8,128)}, f32[1024]{0:T(1024)}, f32[1024,1024]{1,0:T(8,128)}, /...) custom-call(bf16[256,5632]{1,0:T(8,128)(2,1)S(1)} %get-tuple-element.79.refs_0_, ...), custom_call_target="tpu_custom_call" | custom-call | flops 2550136832 | bytes 10485760 | tf_op jit(solution)/shard_map/pallas_call | solution.py:650
  36.6 0.0 collective-permute-done.refs_1_
  36.6 0.0 copy-done
  36.6 3.7 %shard_map.345 = (bf16[256,1024]{1,0:T(8,128)(2,1)}, f32[1024,1024]{1,0:T(8,128)}, f32[1024]{0:T(1024)}, f32[261,1024]{1,0:T(8,128)}, f32[1024]{0:T(1024)}, /*in...) custom-call(bf16[256,3584]{1,0:T(8,128)(2,1)S(1)} %get-tuple-element.76.refs_0_, ...), custom_call_target="tpu_custom_call" | custom-call | flops 1476395008 | bytes 6291456 | tf_op jit(solution)/shard_map/pallas_call | solution.py:650
Async XLA Ops:
  2.4 16.0 %all-to-all-start = ((bf16[16,8,384]{2,1,0:T(8,128)(2,1)}), bf16[16,8,384]{2,1,0:T(8,128)(2,1)S(1)}, u32[]{:S(2)}, u32[]{:S(2)}) async-start(bf16[16,8,384]{2,1,0:T(8,128)(2,1)} %shard_map.340), calls=%async_computation | async-start | bytes 196608 | tf_op jit(solution)/shard_map/all_to_all | solution.py:682
  25.9 5.5 %collective-permute-start.1 = (bf16[256,5632]{1,0:T(8,128)(2,1)S(1)}, bf16[256,5632]{1,0:T(8,128)(2,1)S(1)}, u32[]{:S(2)}, u32[]{:S(2)}) collective-permute-start(bf16[256,5632]{1,0:T(8,128)(2,1)S(1)} %get-tuple-element.79.refs_0_), channel_id=1, source_target_pairs={{0,16},{16,0},{1,17},{17,1},{2,18},{18,2},{3,19},{19,3},{4,20},{20... | collective-permute-start | bytes 8650760 | tf_op jit(solution)/shard_map/ppermute | solution.py:676
  30.8 5.7 %collective-permute-start = (bf16[256,3584]{1,0:T(8,128)(2,1)S(1)}, bf16[256,3584]{1,0:T(8,128)(2,1)S(1)}, u32[]{:S(2)}, u32[]{:S(2)}) collective-permute-start(bf16[256,3584]{1,0:T(8,128)(2,1)S(1)} %get-tuple-element.76.refs_0_), channel_id=1, source_target_pairs={{0,16},{16,0},{1,17},{17,1},{2,18},{18,2},{3,19},{19,3},{4,20},{20... | collective-permute-start | bytes 5505032 | tf_op jit(solution)/shard_map/ppermute | solution.py:676
  31.4 5.2 %copy-start = (bf16[1024,1024]{1,0:T(8,128)(2,1)S(1)}, bf16[1024,1024]{1,0:T(8,128)(2,1)}, u32[]{:S(2)}) copy-start(bf16[1024,1024]{1,0:T(8,128)(2,1)} %refs_4_.3) | copy-start | bytes 6291460
